TPU v7x, 32 devices: a whole 2x2x4 slice. The times are simulated.
32 devices in a mesh: ctx: 8 (over z, x), fsdp: 4 (over y, core).
Axes of the slice: x: 2, y: 2, z: 4, core: 2. Of those that a mesh axis runs over, the one named last changes fastest.
Arguments:
- tokens: bfloat16 [4, 1024, 768], P('fsdp', 'ctx'), may hold values from -6 to 6
- segment_ids: int32 [4, 1024], P('fsdp', 'ctx'), may hold values from 0 to 1023, as said below
- ln1_gain: bfloat16 [768], P('fsdp'), may hold values from 0.5 to 1.5
- ln1_bias: bfloat16 [768], P('fsdp'), may hold values from -1.5 to 1.5
- attn_weight: bfloat16 [768, 2304], P('fsdp'), may hold values from -0.21875 to 0.21875
- attn_bias: bfloat16 [1536], P('fsdp'), may hold values from -1.5 to 1.5
- proj_weight: bfloat16 [768, 768], P('fsdp'), may hold values from -1.25 to 1.25
- proj_bias: bfloat16 [768], P('fsdp'), may hold values from -1.5 to 1.5
- ln2_gain: bfloat16 [768], P('fsdp'), may hold values from 0.5 to 1.5
- ln2_bias: bfloat16 [768], P('fsdp'), may hold values from -1.5 to 1.5
- fc_weight: bfloat16 [768, 3072], P('fsdp'), may hold values from -0.21875 to 0.21875
- fc_bias: bfloat16 [3072], P('fsdp'), may hold values from -1.5 to 1.5
- out_weight: bfloat16 [3072, 768], P('fsdp'), may hold values from -0.109375 to 0.109375
- out_bias: bfloat16 [768], P('fsdp'), may hold values from -1.5 to 1.5
- out_cotangent: bfloat16 [4, 1024, 768], P('fsdp', 'ctx'), may hold values from -6 to 6
Outputs:
- output: bfloat16 [4, 1024, 768], P('fsdp', 'ctx')
- tokens_grad: bfloat16 [4, 1024, 768], P('fsdp', 'ctx')
- ln1_gain_grad: float32 [768], P('fsdp')
- ln1_bias_grad: float32 [768], P('fsdp')
- attn_weight_grad: float32 [768, 2304], P('fsdp')
- attn_bias_grad: float32 [1536], P('fsdp')
- proj_weight_grad: float32 [768, 768], P('fsdp')
- proj_bias_grad: float32 [768], P('fsdp')
- ln2_gain_grad: float32 [768], P('fsdp')
- ln2_bias_grad: float32 [768], P('fsdp')
- fc_weight_grad: float32 [768, 3072], P('fsdp')
- fc_bias_grad: float32 [3072], P('fsdp')
- out_weight_grad: float32 [3072, 768], P('fsdp')
- out_bias_grad: float32 [768], P('fsdp')
Inputs may be any that keep to these rules, and one draw needn't show every extreme that they name: `segment_ids`: along each sequence the id is 0 at the first token and never falls; equal ids mark one document. Every sequence's last document has the id 1024 - 1. In every aligned group of 4 sequences one, placed by the seed, keeps a single id from token 63 to token 959.
All inputs are finite; a program needn't handle non-finite values.
Results may differ from a plain program's by a relative error of at most 0.023.
Values may be sent and summed in bfloat16 or wider, within the bound.
A program may use at most 256 MiB of HBM per device.

v0:
```python
from functools import partial

import jax
import jax.numpy as jnp
from jax import lax
from jax.sharding import PartitionSpec as P

D = 768
HEADS = 12
HDIM = 64


EPSILON = 1e-05
NEGATIVE = -1e30


def keep_same(value_in):
    return value_in


def split_heads(block_rows):
    return block_rows.reshape(block_rows.shape[0], HEADS, HDIM)


def norm_forward(resid, gain_row, bias_row):
    average = jnp.mean(resid, axis=-1, keepdims=True)
    centred = resid - average
    variance = jnp.mean(centred * centred, axis=-1, keepdims=True)
    inverse = lax.rsqrt(variance + EPSILON)
    normal = centred * inverse
    return ((normal * gain_row + bias_row).astype(jnp.bfloat16), normal, inverse)


def norm_backward(grad_normed, normal, inverse, gain_row):
    scaled = grad_normed * gain_row
    mean_term = jnp.mean(scaled, axis=-1, keepdims=True)
    second = jnp.mean(scaled * normal, axis=-1, keepdims=True)
    grad_input = inverse * (scaled - mean_term - normal * second)
    return (grad_input, jnp.sum(grad_normed * normal, axis=0), jnp.sum(grad_normed, axis=0))


def block_active(query_segs, key_segs, query_start, key_start):
    diagonal = key_start == query_start
    earlier = (key_start < query_start) & (key_segs[-1] == query_segs[0])
    return diagonal | earlier


def allowed_pairs(query_segs, key_segs, query_start, key_start):
    places = jnp.arange(query_segs.shape[0], dtype=jnp.int32)
    causal = (key_start + places)[None, :] <= (query_start + places)[:, None]
    return (causal & (query_segs[:, None] == key_segs[None, :]))[None]


def block_grads(queries, grad_rows, key_heads, value_heads, lse_rows, delta_rows, allowed):
    scores = jnp.einsum(
        "qhd,khd->hqk", queries, key_heads, preferred_element_type=jnp.float32
    ) * HDIM ** (-0.5)
    attention = jnp.where(allowed, jnp.exp(scores - lse_rows[:, :, None]), 0.0)
    grad_attention = jnp.einsum(
        "qhd,khd->hqk", grad_rows, value_heads, preferred_element_type=jnp.float32
    )
    grad_scores = (attention * (grad_attention - delta_rows[:, :, None])).astype(jnp.bfloat16)
    return (attention, grad_scores)


def forward_fold(query_heads, own_segs, all_segs, own_start):
    members, seq_dev = own_segs.shape

    def fold(running, arrived, first_row):
        key_piece, value_piece = arrived
        blocks = key_piece.shape[1] // seq_dev

        def visit(block_index, carried):
            offset = block_index * seq_dev
            key_block = lax.dynamic_slice_in_dim(key_piece, offset, seq_dev, 1)
            value_block = lax.dynamic_slice_in_dim(value_piece, offset, seq_dev, 1)
            key_segs = lax.dynamic_slice_in_dim(all_segs[0], offset, seq_dev, 0)
            key_heads = split_heads(key_block[0])
            value_heads = split_heads(value_block[0])

            def update(current):
                running_max, denominator, numerator = current
                allowed = allowed_pairs(own_segs[0], key_segs, own_start, offset)
                scores = jnp.einsum(
                    "qhd,khd->hqk", query_heads[0], key_heads, preferred_element_type=jnp.float32
                ) * HDIM ** (-0.5)
                scores = jnp.where(allowed, scores, NEGATIVE)
                new_max = jnp.maximum(running_max, jnp.max(scores, axis=-1))
                weights = jnp.where(allowed, jnp.exp(scores - new_max[:, :, None]), 0.0)
                factor = jnp.exp(running_max - new_max)
                denominator = denominator * factor + jnp.sum(weights, axis=-1)
                increment = jnp.einsum(
                    "hqk,khd->qhd",
                    weights.astype(jnp.bfloat16),
                    value_heads,
                    preferred_element_type=jnp.float32,
                )
                numerator = numerator * factor.T[:, :, None] + increment
                return (new_max, denominator, numerator)

            current = (carried[0][0], carried[1][0], carried[2][0])
            active = block_active(own_segs[0], key_segs, own_start, offset)
            updated = [lax.cond(active, update, keep_same, current)]
            return tuple(
                (jnp.stack([result[item_index] for result in updated]) for item_index in range(3))
            )

        return lax.fori_loop(0, blocks, visit, running)

    return fold


def query_grad_fold(query_heads, grad_heads, own_segs, all_segs, own_start, lse, row_delta):
    members, seq_dev = own_segs.shape

    def fold(running, arrived, first_row):
        key_piece, value_piece = arrived
        blocks = key_piece.shape[1] // seq_dev

        def visit(block_index, carried):
            offset = block_index * seq_dev
            key_block = lax.dynamic_slice_in_dim(key_piece, offset, seq_dev, 1)
            value_block = lax.dynamic_slice_in_dim(value_piece, offset, seq_dev, 1)
            key_segs = lax.dynamic_slice_in_dim(all_segs[0], offset, seq_dev, 0)
            key_heads = split_heads(key_block[0])
            value_heads = split_heads(value_block[0])

            def update(current):
                allowed = allowed_pairs(own_segs[0], key_segs, own_start, offset)
                attention, grad_scores = block_grads(
                    query_heads[0],
                    grad_heads[0],
                    key_heads,
                    value_heads,
                    lse[0],
                    row_delta[0],
                    allowed,
                )
                increment = jnp.einsum(
                    "hqk,khd->qhd", grad_scores, key_heads, preferred_element_type=jnp.float32
                ) * HDIM ** (-0.5)
                return current + increment.reshape(seq_dev, HEADS * HDIM)

            active = block_active(own_segs[0], key_segs, own_start, offset)
            updated = [lax.cond(active, update, keep_same, carried[0])]
            return jnp.stack(updated)

        return lax.fori_loop(0, blocks, visit, running)

    return fold


def key_grad_fold(
    key_heads_own, value_heads_own, own_segs, all_segs, own_start, all_lse, all_delta
):
    members, seq_dev = own_segs.shape

    def fold(running, arrived, first_row):
        query_piece, grad_piece = arrived
        blocks = query_piece.shape[1] // seq_dev

        def visit(block_index, carried):
            offset = block_index * seq_dev
            query_block = lax.dynamic_slice_in_dim(query_piece, offset, seq_dev, 1)
            grad_block = lax.dynamic_slice_in_dim(grad_piece, offset, seq_dev, 1)
            query_segs = lax.dynamic_slice_in_dim(all_segs[0], offset, seq_dev, 0)
            lse_rows = lax.dynamic_slice_in_dim(all_lse[0], offset, seq_dev, 1)
            delta_rows = lax.dynamic_slice_in_dim(all_delta[0], offset, seq_dev, 1)
            query_heads = split_heads(query_block[0])
            grad_heads = split_heads(grad_block[0])

            def update(current):
                grad_keys, grad_values = current
                allowed = allowed_pairs(query_segs, own_segs[0], offset, own_start)
                attention, grad_scores = block_grads(
                    query_heads,
                    grad_heads,
                    key_heads_own[0],
                    value_heads_own[0],
                    lse_rows,
                    delta_rows,
                    allowed,
                )
                key_step = jnp.einsum(
                    "hqk,qhd->khd", grad_scores, query_heads, preferred_element_type=jnp.float32
                ) * HDIM ** (-0.5)
                value_step = jnp.einsum(
                    "hqk,qhd->khd",
                    attention.astype(jnp.bfloat16),
                    grad_heads,
                    preferred_element_type=jnp.float32,
                )
                return (
                    grad_keys + key_step.reshape(seq_dev, HEADS * HDIM),
                    grad_values + value_step.reshape(seq_dev, HEADS * HDIM),
                )

            active = block_active(query_segs, own_segs[0], offset, own_start)
            updated = [lax.cond(active, update, keep_same, (carried[0][0], carried[1][0]))]
            return tuple(
                (jnp.stack([result[item_index] for result in updated]) for item_index in range(2))
            )

        return lax.fori_loop(0, blocks, visit, running)

    return fold


def layer_forward(resid, weights, own_segs, all_segs, own_start):
    (
        gain_one,
        bias_one,
        weight_qkv,
        bias_qv,
        weight_proj,
        bias_proj,
        gain_two,
        bias_two,
        weight_fc,
        bias_fc,
        weight_out,
        bias_out,
    ) = weights
    members, seq_dev = own_segs.shape
    normed_one, normal_one, inverse_one = norm_forward(
        resid, gain_one.astype(jnp.float32), bias_one.astype(jnp.float32)
    )
    projected = jnp.dot(normed_one, weight_qkv, preferred_element_type=jnp.float32)
    biases = bias_qv.astype(jnp.float32)
    queries = (projected[:, :D] + biases[:D]).astype(jnp.bfloat16)
    key_rows = projected[:, D : 2 * D].astype(jnp.bfloat16)
    value_rows = (projected[:, 2 * D :] + biases[D:]).astype(jnp.bfloat16)
    query_heads = queries.reshape(members, seq_dev, HEADS, HDIM)
    start_state = (
        jnp.full((members, HEADS, seq_dev), NEGATIVE, jnp.float32),
        jnp.zeros((members, HEADS, seq_dev), jnp.float32),
        jnp.zeros((members, seq_dev, HEADS, HDIM), jnp.float32),
    )
    fold = forward_fold(query_heads, own_segs, all_segs, own_start)
    key_flat = key_rows.reshape(members, seq_dev, D)
    value_flat = value_rows.reshape(members, seq_dev, D)
    running_max, denominator, numerator = fold(
        start_state,
        (
            lax.all_gather(key_flat, "ctx", axis=1, tiled=True),
            lax.all_gather(value_flat, "ctx", axis=1, tiled=True),
        ),
        jnp.int32(0),
    )
    lse = running_max + jnp.log(denominator)
    attended = (numerator / jnp.transpose(denominator, (0, 2, 1))[..., None]).reshape(
        members * seq_dev, D
    )
    attended = attended.astype(jnp.bfloat16)
    middle = (
        resid
        + jnp.dot(attended, weight_proj, preferred_element_type=jnp.float32)
        + bias_proj.astype(jnp.float32)
    )
    normed_two, normal_two, inverse_two = norm_forward(
        middle, gain_two.astype(jnp.float32), bias_two.astype(jnp.float32)
    )
    hidden = jnp.dot(normed_two, weight_fc, preferred_element_type=jnp.float32) + bias_fc.astype(
        jnp.float32
    )
    activated = jax.nn.gelu(hidden, approximate=True).astype(jnp.bfloat16)
    result_rows = (
        middle
        + jnp.dot(activated, weight_out, preferred_element_type=jnp.float32)
        + bias_out.astype(jnp.float32)
    )
    saved = (
        normed_one,
        normal_one,
        inverse_one,
        query_heads,
        key_flat,
        value_flat,
        attended,
        lse,
        normed_two,
        normal_two,
        inverse_two,
        hidden,
        activated,
    )
    return (result_rows, saved)


def layer_backward(gradient, weights, saved, own_segs, all_segs, own_start):
    (
        gain_one,
        bias_one,
        weight_qkv,
        bias_qv,
        weight_proj,
        bias_proj,
        gain_two,
        bias_two,
        weight_fc,
        bias_fc,
        weight_out,
        bias_out,
    ) = weights
    (
        normed_one,
        normal_one,
        inverse_one,
        query_heads,
        key_flat,
        value_flat,
        attended,
        lse,
        normed_two,
        normal_two,
        inverse_two,
        hidden,
        activated,
    ) = saved
    members, seq_dev = own_segs.shape
    row_count = members * seq_dev
    grad_branch = gradient.astype(jnp.bfloat16)
    grad_bias_out = jnp.sum(grad_branch.astype(jnp.float32), axis=0)
    grad_weight_out = jnp.einsum(
        "rf,rd->fd", activated, grad_branch, preferred_element_type=jnp.float32
    )
    grad_activated = jnp.einsum(
        "rd,fd->rf", grad_branch, weight_out, preferred_element_type=jnp.float32
    )
    gelu_pull = jax.vjp(partial(jax.nn.gelu, approximate=True), hidden)[1]
    grad_hidden = gelu_pull(grad_activated)[0].astype(jnp.bfloat16)
    grad_bias_fc = jnp.sum(grad_hidden.astype(jnp.float32), axis=0)
    grad_weight_fc = jnp.einsum(
        "rd,rf->df", normed_two, grad_hidden, preferred_element_type=jnp.float32
    )
    grad_normed_two = jnp.einsum(
        "rf,df->rd", grad_hidden, weight_fc, preferred_element_type=jnp.float32
    )
    grad_in_two, grad_gain_two, grad_bias_two = norm_backward(
        grad_normed_two, normal_two, inverse_two, gain_two.astype(jnp.float32)
    )
    grad_middle = gradient + grad_in_two
    grad_proj = grad_middle.astype(jnp.bfloat16)
    grad_bias_proj = jnp.sum(grad_proj.astype(jnp.float32), axis=0)
    grad_weight_proj = jnp.einsum(
        "re,rd->ed", attended, grad_proj, preferred_element_type=jnp.float32
    )
    grad_attended = jnp.einsum(
        "rd,ed->re", grad_proj, weight_proj, preferred_element_type=jnp.float32
    )
    grad_attended = grad_attended.astype(jnp.bfloat16)
    grad_heads = grad_attended.reshape(members, seq_dev, HEADS, HDIM)
    attended_heads = attended.reshape(members, seq_dev, HEADS, HDIM)
    row_delta = jnp.einsum(
        "sqhd,sqhd->shq", grad_heads, attended_heads, preferred_element_type=jnp.float32
    )
    zero_rows = jnp.zeros((members, seq_dev, D), jnp.float32)
    all_lse, all_delta = (
        lax.all_gather(lse, "ctx", axis=2, tiled=True),
        lax.all_gather(row_delta, "ctx", axis=2, tiled=True),
    )
    fold_one = query_grad_fold(
        query_heads, grad_heads, own_segs, all_segs, own_start, lse, row_delta
    )
    grad_query = fold_one(
        zero_rows,
        (
            lax.all_gather(key_flat, "ctx", axis=1, tiled=True),
            lax.all_gather(value_flat, "ctx", axis=1, tiled=True),
        ),
        jnp.int32(0),
    )
    fold_two = key_grad_fold(
        key_flat.reshape(members, seq_dev, HEADS, HDIM),
        value_flat.reshape(members, seq_dev, HEADS, HDIM),
        own_segs,
        all_segs,
        own_start,
        all_lse,
        all_delta,
    )
    query_flat = query_heads.reshape(members, seq_dev, D)
    grad_flat = grad_attended.reshape(members, seq_dev, D)
    grad_keys, grad_values = fold_two(
        (zero_rows, zero_rows),
        (
            lax.all_gather(query_flat, "ctx", axis=1, tiled=True),
            lax.all_gather(grad_flat, "ctx", axis=1, tiled=True),
        ),
        jnp.int32(0),
    )
    grad_query_low = grad_query.reshape(row_count, D).astype(jnp.bfloat16)
    grad_keys_low = grad_keys.reshape(row_count, D).astype(jnp.bfloat16)
    grad_values_low = grad_values.reshape(row_count, D).astype(jnp.bfloat16)
    grad_projected = jnp.concatenate([grad_query_low, grad_keys_low, grad_values_low], axis=1)
    grad_bias_qv = jnp.concatenate(
        [
            jnp.sum(grad_query_low.astype(jnp.float32), axis=0),
            jnp.sum(grad_values_low.astype(jnp.float32), axis=0),
        ]
    )
    grad_weight_qkv = jnp.einsum(
        "rd,re->de", normed_one, grad_projected, preferred_element_type=jnp.float32
    )
    grad_normed_one = jnp.einsum(
        "re,de->rd", grad_projected, weight_qkv, preferred_element_type=jnp.float32
    )
    grad_in_one, grad_gain_one, grad_bias_one = norm_backward(
        grad_normed_one, normal_one, inverse_one, gain_one.astype(jnp.float32)
    )
    grad_input = grad_middle + grad_in_one
    grad_terms = (
        grad_gain_one,
        grad_bias_one,
        grad_weight_qkv,
        grad_bias_qv,
        grad_weight_proj,
        grad_bias_proj,
        grad_gain_two,
        grad_bias_two,
        grad_weight_fc,
        grad_bias_fc,
        grad_weight_out,
        grad_bias_out,
    )
    return (grad_input, grad_terms)


def reduce_grads(grad_terms):
    (
        grad_gain_one,
        grad_bias_one,
        grad_weight_qkv,
        grad_bias_qv,
        grad_weight_proj,
        grad_bias_proj,
        grad_gain_two,
        grad_bias_two,
        grad_weight_fc,
        grad_bias_fc,
        grad_weight_out,
        grad_bias_out,
    ) = grad_terms
    shares = (
        lax.psum_scatter(
            grad_gain_one.astype(jnp.bfloat16), "fsdp", scatter_dimension=0, tiled=True
        ).astype(jnp.float32),
        lax.psum_scatter(
            grad_bias_one.astype(jnp.bfloat16), "fsdp", scatter_dimension=0, tiled=True
        ).astype(jnp.float32),
        lax.psum_scatter(
            grad_weight_qkv.astype(jnp.bfloat16), "fsdp", scatter_dimension=0, tiled=True
        ).astype(jnp.float32),
        lax.psum_scatter(
            grad_bias_qv.astype(jnp.bfloat16), "fsdp", scatter_dimension=0, tiled=True
        ).astype(jnp.float32),
        lax.psum_scatter(
            grad_weight_proj.astype(jnp.bfloat16), "fsdp", scatter_dimension=0, tiled=True
        ).astype(jnp.float32),
        lax.psum_scatter(
            grad_bias_proj.astype(jnp.bfloat16), "fsdp", scatter_dimension=0, tiled=True
        ).astype(jnp.float32),
        lax.psum_scatter(
            grad_gain_two.astype(jnp.bfloat16), "fsdp", scatter_dimension=0, tiled=True
        ).astype(jnp.float32),
        lax.psum_scatter(
            grad_bias_two.astype(jnp.bfloat16), "fsdp", scatter_dimension=0, tiled=True
        ).astype(jnp.float32),
        lax.psum_scatter(
            grad_weight_fc.astype(jnp.bfloat16), "fsdp", scatter_dimension=0, tiled=True
        ).astype(jnp.float32),
        lax.psum_scatter(
            grad_bias_fc.astype(jnp.bfloat16), "fsdp", scatter_dimension=0, tiled=True
        ).astype(jnp.float32),
        lax.psum_scatter(
            grad_weight_out.astype(jnp.bfloat16), "fsdp", scatter_dimension=0, tiled=True
        ).astype(jnp.float32),
        lax.psum_scatter(
            grad_bias_out.astype(jnp.bfloat16), "fsdp", scatter_dimension=0, tiled=True
        ).astype(jnp.float32),
    )
    (
        share_gain_one,
        share_bias_one,
        share_weight_qkv,
        share_bias_qv,
        share_weight_proj,
        share_bias_proj,
        share_gain_two,
        share_bias_two,
        share_weight_fc,
        share_bias_fc,
        share_weight_out,
        share_bias_out,
    ) = shares
    return lax.psum(
        (
            share_gain_one,
            share_bias_one,
            share_weight_qkv,
            share_bias_qv,
            share_weight_proj,
            share_bias_proj,
            share_gain_two,
            share_bias_two,
            share_weight_fc,
            share_bias_fc,
            share_weight_out,
            share_bias_out,
        ),
        "ctx",
    )


def body(
    tokens,
    segment_ids,
    ln1_gain,
    ln1_bias,
    attn_weight,
    attn_bias,
    proj_weight,
    proj_bias,
    ln2_gain,
    ln2_bias,
    fc_weight,
    fc_bias,
    out_weight,
    out_bias,
    out_cotangent,
):
    members, seq_dev, features = tokens.shape
    row_count = members * seq_dev
    position = lax.axis_index("ctx")
    own_start = position * seq_dev
    all_segs = lax.all_gather(segment_ids, "ctx", axis=1, tiled=True)

    def gather_weights():
        return (
            lax.all_gather(ln1_gain, "fsdp", axis=0, tiled=True),
            lax.all_gather(ln1_bias, "fsdp", axis=0, tiled=True),
            lax.all_gather(attn_weight, "fsdp", axis=0, tiled=True),
            lax.all_gather(attn_bias, "fsdp", axis=0, tiled=True),
            lax.all_gather(proj_weight, "fsdp", axis=0, tiled=True),
            lax.all_gather(proj_bias, "fsdp", axis=0, tiled=True),
            lax.all_gather(ln2_gain, "fsdp", axis=0, tiled=True),
            lax.all_gather(ln2_bias, "fsdp", axis=0, tiled=True),
            lax.all_gather(fc_weight, "fsdp", axis=0, tiled=True),
            lax.all_gather(fc_bias, "fsdp", axis=0, tiled=True),
            lax.all_gather(out_weight, "fsdp", axis=0, tiled=True),
            lax.all_gather(out_bias, "fsdp", axis=0, tiled=True),
        )

    resid = tokens.reshape(row_count, features).astype(jnp.float32)
    saved_layers = []
    for layer_index in range(2):
        weights = gather_weights()
        resid, saved = layer_forward(resid, weights, segment_ids, all_segs, own_start)
        saved_layers.append(saved)
    output = resid.astype(jnp.bfloat16).reshape(members, seq_dev, features)
    gradient = out_cotangent.reshape(row_count, features).astype(jnp.float32)
    collected = []
    for layer_index in (1, 0):
        weights = gather_weights()
        gradient, grad_terms = layer_backward(
            gradient, weights, saved_layers[layer_index], segment_ids, all_segs, own_start
        )
        collected.append(reduce_grads(grad_terms))
    summed = tuple(
        (first_term + second_term for first_term, second_term in zip(collected[0], collected[1]))
    )
    tokens_grad = gradient.astype(jnp.bfloat16).reshape(members, seq_dev, features)
    return (
        output,
        tokens_grad,
        summed[0],
        summed[1],
        summed[2],
        summed[3],
        summed[4],
        summed[5],
        summed[6],
        summed[7],
        summed[8],
        summed[9],
        summed[10],
        summed[11],
    )


def solution(mesh):
    in_specs = (
        P("fsdp", "ctx", None),
        P("fsdp", "ctx"),
        P("fsdp"),
        P("fsdp"),
        P("fsdp", None),
        P("fsdp"),
        P("fsdp", None),
        P("fsdp"),
        P("fsdp"),
        P("fsdp"),
        P("fsdp", None),
        P("fsdp"),
        P("fsdp", None),
        P("fsdp"),
        P("fsdp", "ctx", None),
    )
    out_specs = (
        P("fsdp", "ctx", None),
        P("fsdp", "ctx", None),
        P("fsdp"),
        P("fsdp"),
        P("fsdp", None),
        P("fsdp"),
        P("fsdp", None),
        P("fsdp"),
        P("fsdp"),
        P("fsdp"),
        P("fsdp", None),
        P("fsdp"),
        P("fsdp", None),
        P("fsdp"),
    )
    return jax.shard_map(body, mesh=mesh, in_specs=in_specs, out_specs=out_specs, check_vma=False)
```

profile of v0, /device:TPU:0, one launch (start us, length us, event | category | flops | bytes accessed | tf_op | source)
XLA Modules:
  0.0 1233.1 jit_solution(17954904659151395319)
XLA Ops:
  15.0 13.1 %all-reduce.25 = (bf16[768]{0:T(1024)(128)(2,1)S(1)}, bf16[768]{0:T(1024)(128)(2,1)S(1)}, bf16[768]{0:T(1024)(128)(2,1)S(1)}, bf16[768]{0:T(1024)(128)(2,1)S(1)}...) all-reduce(bf16[768]{0:T(1024)(128)(2,1)S(1)} %dynamic-update-slice, ...), channel_id=1, replica_groups=mesh['ctx'=8,'fsdp'=4] {'fsdp'}, use_global_device_ids=true, to_apply=%add.1 | all-reduce | flops 4608 | bytes 18432
  28.8 5.1 all-gather.10
  36.2 7.0 all-gather.25.cloned.1.call-done
  49.4 5.2 all-gather.11
  54.6 21.4 %all_gather.50 = s32[1,1024]{1,0:T(1,128)} all-gather(s32[1,128]{1,0:T(1,128)} %param.40), channel_id=1, replica_groups=mesh['ctx'=8,'fsdp'=4] {'ctx'}, dimensions={1}, use_global_device_ids=true | all-gather | bytes 4608 | tf_op jit(solution)/shard_map/all_gather | solution.py:536
  76.2 15.0 %all-gather.35.cloned.1.call-done = bf16[1024,768]{1,0:T(8,128)(2,1)} async-done(((bf16[128,768]{1,0:T(8,128)(2,1)}), bf16[1024,768]{1,0:T(8,128)(2,1)}) %all-gather.35.cloned.1.call-update) | async-done | bytes 1572880 | tf_op jit(solution)/shard_map/all_gather | solution.py:246
  92.8 44.1 %all-gather.33.cloned.1.call-done = bf16[1024,768]{1,0:T(8,128)(2,1)} async-done(((bf16[128,768]{1,0:T(8,128)(2,1)}), bf16[1024,768]{1,0:T(8,128)(2,1)}) %all-gather.33.cloned.1.call-update) | async-done | bytes 1572880 | tf_op jit(solution)/shard_map/all_gather | solution.py:245
  140.1 31.6 %while.90 = (s32[]{:T(128)}, f32[1,12,128]{2,1,0:T(8,128)}, f32[1,12,128]{2,1,0:T(8,128)S(1)}, f32[1,128,12,64]{1,3,2,0:T(8,128)S(1)}, s32[]{:T(128)}, /*index=5...) while((s32[]{:T(128)}, f32[1,12,128]{2,1,0:T(8,128)}, ...), condition=%wide.region_7.8_spmd, body=%wide.region_2.7_spmd.sunk | while | flops 52351756 | bytes 4690297 | solution.py:108
  143.4 5.3 conditional.12
  174.8 18.7 %all-gather.29.cloned.1.call-done = bf16[768,3072]{1,0:T(8,128)(2,1)} async-done(((bf16[192,3072]{1,0:T(8,128)(2,1)}), bf16[768,3072]{1,0:T(8,128)(2,1)}) %all-gather.29.cloned.1.call-update) | async-done | bytes 4718608 | tf_op jit(solution)/shard_map/all_gather | solution.py:548
  196.8 35.7 %all-gather.31.cloned.1.call-done = bf16[3072,768]{1,0:T(8,128)(2,1)} async-done(((bf16[768,768]{1,0:T(8,128)(2,1)}), bf16[3072,768]{1,0:T(8,128)(2,1)}) %all-gather.31.cloned.1.call-update) | async-done | bytes 4718608 | tf_op jit(solution)/shard_map/all_gather | solution.py:550
  232.5 3.6 fusion.135
  239.6 42.6 %all-gather.39.cloned.1.call-done = bf16[1024,768]{1,0:T(8,128)(2,1)} async-done(((bf16[128,768]{1,0:T(8,128)(2,1)}), bf16[1024,768]{1,0:T(8,128)(2,1)}) %all-gather.39.cloned.1.call-update) | async-done | bytes 1572880 | tf_op jit(solution)/shard_map/all_gather | solution.py:246
  284.8 42.6 %all-gather.37.cloned.1.call-done = bf16[1024,768]{1,0:T(8,128)(2,1)} async-done(((bf16[128,768]{1,0:T(8,128)(2,1)}), bf16[1024,768]{1,0:T(8,128)(2,1)}) %all-gather.37.cloned.1.call-update) | async-done | bytes 1572880 | tf_op jit(solution)/shard_map/all_gather | solution.py:245
  330.6 31.7 %while.91 = (s32[]{:T(128)}, f32[1,12,128]{2,1,0:T(8,128)}, f32[1,12,128]{2,1,0:T(8,128)S(1)}, f32[1,128,12,64]{1,3,2,0:T(8,128)S(1)}, s32[]{:T(128)}, /*index=5...) while((s32[]{:T(128)}, f32[1,12,128]{2,1,0:T(8,128)}, ...), condition=%wide.region_17.18_spmd, body=%wide.region_12.17_spmd.sunk | while | flops 52351756 | bytes 4690297 | solution.py:108
  334.0 5.3 conditional.13
  363.1 3.4 convolution_add_fusion
  366.5 5.5 fusion.138
  380.7 36.6 %all-gather.6 = f32[12,1024]{1,0:T(8,128)} all-gather(f32[12,128]{1,0:T(8,128)S(1)} %fusion.105), channel_id=8, replica_groups=mesh['ctx'=8,'fsdp'=4] {'ctx'}, dimensions={1}, use_global_device_ids=true | all-gather | bytes 55296 | tf_op jit(solution)/shard_map/all_gather | solution.py:360
  417.3 33.1 %all_gather.121 = f32[1,12,1024]{2,1,0:T(8,128)} all-gather(f32[1,12,128]{2,1,0:T(8,128)S(1)} %log_add_fusion.1), channel_id=1, replica_groups=mesh['ctx'=8,'fsdp'=4] {'ctx'}, dimensions={2}, use_global_device_ids=true | all-gather | bytes 55296 | tf_op jit(solution)/shard_map/all_gather | solution.py:359
  450.4 23.3 %while.92 = (s32[]{:T(128)}, f32[1,128,768]{1,2,0:T(8,128)S(1)}, s32[]{:T(128)}, s32[1,1024]{1,0:T(1,128)}, s32[1,128]{1,0:T(1,128)}, /*index=5*/bf16[1,1024,768...) while((s32[]{:T(128)}, f32[1,128,768]{1,2,0:T(8,128)S(1)}, ...), condition=%wide.region_25.26_spmd, body=%wide.region_22.25_spmd.sunk | while | flops 76923144 | bytes 4964705 | solution.py:148
  479.6 35.2 %while.93 = (s32[]{:T(128)}, f32[1,128,768]{1,2,0:T(8,128)S(1)}, f32[1,128,768]{1,2,0:T(8,128)S(1)}, s32[]{:T(128)}, s32[1,128]{1,0:T(1,128)}, /*index=5*/s32[1,...) while((s32[]{:T(128)}, f32[1,128,768]{1,2,0:T(8,128)S(1)}, ...), condition=%wide.region_29.0_spmd, body=%wide.region_26.29_spmd.sunk | while | flops 102383880 | bytes 7545237 | solution.py:204
  482.2 7.3 conditional.15
  492.1 7.3 conditional.15
  514.9 4.3 multiply_reduce_fusion.2
  520.7 5.0 fusion.137
  535.6 5.2 convolution_convert_fusion.1
  540.9 5.3 convolution_convert_fusion
  547.3 3.6 convolution_convert_fusion.3
  552.1 3.6 convolution_convert_fusion.2
  565.9 31.6 %all_gather.125 = f32[1,12,1024]{2,1,0:T(8,128)} all-gather(f32[1,12,128]{2,1,0:T(8,128)S(1)} %log_add_fusion), channel_id=1, replica_groups=mesh['ctx'=8,'fsdp'=4] {'ctx'}, dimensions={2}, use_global_device_ids=true | all-gather | bytes 55296 | tf_op jit(solution)/shard_map/all_gather | solution.py:359
  597.7 32.0 %all-gather.9 = f32[12,1024]{1,0:T(8,128)} all-gather(f32[12,128]{1,0:T(8,128)S(1)} %fusion.104), channel_id=11, replica_groups=mesh['ctx'=8,'fsdp'=4] {'ctx'}, dimensions={1}, use_global_device_ids=true | all-gather | bytes 55296 | tf_op jit(solution)/shard_map/all_gather | solution.py:360
  629.8 22.9 %while.94 = (s32[]{:T(128)}, f32[1,128,768]{1,2,0:T(8,128)S(1)}, s32[]{:T(128)}, s32[1,1024]{1,0:T(1,128)}, s32[1,128]{1,0:T(1,128)}, /*index=5*/bf16[1,1024,768...) while((s32[]{:T(128)}, f32[1,128,768]{1,2,0:T(8,128)S(1)}, ...), condition=%wide.region_37.38_spmd, body=%wide.region_34.37_spmd.sunk | while | flops 76923144 | bytes 4964705 | solution.py:148
  656.1 35.3 %while.95 = (s32[]{:T(128)}, f32[1,128,768]{1,2,0:T(8,128)S(1)}, f32[1,128,768]{1,2,0:T(8,128)S(1)}, s32[]{:T(128)}, s32[1,128]{1,0:T(1,128)}, /*index=5*/s32[1,...) while((s32[]{:T(128)}, f32[1,128,768]{1,2,0:T(8,128)S(1)}, ...), condition=%wide.region_41.42_spmd, body=%wide.region_38.41_spmd.sunk | while | flops 102383880 | bytes 7545237 | solution.py:204
  658.7 7.3 conditional.17
  668.6 7.3 conditional.17
  692.8 4.2 convolution_convert_fusion.4
  699.4 39.6 %reduce-scatter.21.cloned.1.call-done = bf16[768,768]{1,0:T(8,128)(2,1)} async-done(((bf16[3072,768]{1,0:T(8,128)(2,1)}), bf16[768,768]{1,0:T(8,128)(2,1)}) %reduce-scatter.21.cloned.1.call-update) | async-done | bytes 1179664 | tf_op jit(solution)/shard_map/reduce_scatter | solution.py:475
  738.9 50.4 %reduce-scatter.23.cloned.1.call-done = bf16[768,768]{1,0:T(8,128)(2,1)} async-done(((bf16[3072,768]{1,0:T(8,128)(2,1)}), bf16[768,768]{1,0:T(8,128)(2,1)}) %reduce-scatter.23.cloned.1.call-update) | async-done | bytes 1179664 | tf_op jit(solution)/shard_map/reduce_scatter | solution.py:475
  792.6 47.0 %reduce-scatter.17.cloned.1.call-done = bf16[192,3072]{1,0:T(8,128)(2,1)} async-done(((bf16[768,3072]{1,0:T(8,128)(2,1)}), bf16[192,3072]{1,0:T(8,128)(2,1)}) %reduce-scatter.17.cloned.1.call-update) | async-done | bytes 1179664 | tf_op jit(solution)/shard_map/reduce_scatter | solution.py:469
  839.6 50.4 %reduce-scatter.19.cloned.1.call-done = bf16[192,3072]{1,0:T(8,128)(2,1)} async-done(((bf16[768,3072]{1,0:T(8,128)(2,1)}), bf16[192,3072]{1,0:T(8,128)(2,1)}) %reduce-scatter.19.cloned.1.call-update) | async-done | bytes 1179664 | tf_op jit(solution)/shard_map/reduce_scatter | solution.py:469
  890.0 3.4 convert_add_fusion.1
  893.4 39.7 %reduce-scatter.9.cloned.1.call-done = bf16[192,2304]{1,0:T(8,128)(2,1)} async-done(((bf16[768,2304]{1,0:T(8,128)(2,1)}), bf16[192,2304]{1,0:T(8,128)(2,1)}) %reduce-scatter.9.cloned.1.call-update) | async-done | bytes 884752 | tf_op jit(solution)/shard_map/reduce_scatter | solution.py:451
  933.0 43.0 %reduce-scatter.11.cloned.1.call-done = bf16[192,2304]{1,0:T(8,128)(2,1)} async-done(((bf16[768,2304]{1,0:T(8,128)(2,1)}), bf16[192,2304]{1,0:T(8,128)(2,1)}) %reduce-scatter.11.cloned.1.call-update) | async-done | bytes 884752 | tf_op jit(solution)/shard_map/reduce_scatter | solution.py:451
  982.9 4.2 fusion.83
  989.4 11.4 all-reduce.24
  1001.4 39.4 %all-reduce.22 = (f32[192]{0:T(256)}, f32[192]{0:T(256)}, f32[384]{0:T(512)}, f32[192]{0:T(256)}, f32[192]{0:T(256)}, /*index=5*/f32[192]{0:T(256)}, f32[768]{0:T(1024)}, f32[192]{0:T(256)}) all-reduce(f32[192]{0:T(256)S(1)} %convert_add_fusion.11, f32[192]{0:T(256)S(1)} %convert_add_fusion.10, ...), channel_id=1, replica_groups=mesh['ctx'=8,'fsdp'=4] {'ctx'}, use_global_device_ids=true, to_apply=%region_46.47 | all-reduce | flops 2304 | bytes 18432 | tf_op jit(solution)/shard_map/psum | solution.py:496
  1041.7 176.3 %all-reduce.28.cloned.1.call-done = (f32[192,2304]{1,0:T(8,128)}, f32[192,768]{1,0:T(8,128)}, f32[192,3072]{1,0:T(8,128)}, f32[768,768]{1,0:T(8,128)}) async-done(((f32[192,2304]{1,0:T(8,128)}, f32[192,768]{1,0:T(8,128)}, f32[192,3072]{1,0:T(8,128)}, f32[768,768]{1,0:T(8,128)}), (f32[192,2304]{1,0:T(8,128)}, f32[192,768]{1,0:T(8,128)}, f32[192,3072]{1,0:T(8,128)}, ...) | async-done | bytes 7077904 | tf_op jit(solution)/shard_map/psum | solution.py:496
  (598 shorter events, 234.0 us)
Async XLA Ops:
  7.2 36.1 %copy-start.14 = (bf16[1,128,768]{2,1,0:T(8,128)(2,1)S(1)}, bf16[1,128,768]{2,1,0:T(8,128)(2,1)}, u32[]{:S(2)}) copy-start(bf16[1,128,768]{2,1,0:T(8,128)(2,1)} %param.39) | copy-start | bytes 589828
  7.2 36.1 %all-gather.25.cloned.1.call-start = ((), (), s32[]{:S(2)}) async-start(), calls=%async_computation.8 | async-start | bytes 4423680 | tf_op jit(solution)/shard_map/all_gather | solution.py:542
  7.9 83.2 %all-gather.35.cloned.1.call-start = ((), (), s32[]{:S(2)}) async-start(), calls=%async_computation.21 | async-start | bytes 1769472 | tf_op jit(solution)/shard_map/all_gather | solution.py:246
  28.1 208.2 %copy-start.55 = (f32[768]{0:T(1024)}, f32[768]{0:T(1024)S(1)}, u32[]{:S(2)}) copy-start(f32[768]{0:T(1024)S(1)} %convert_element_type.392) | copy-start | bytes 9220
  35.1 10.9 copy-start.69
  36.2 9.8 copy-start.82
  46.7 29.2 %copy-start.29 = (bf16[128,768]{1,0:T(8,128)(2,1)}, bf16[128,768]{1,0:T(8,128)(2,1)S(1)}, u32[]{:S(2)}) copy-start(bf16[128,768]{1,0:T(8,128)(2,1)S(1)} %get-tuple-element.2265) | copy-start | bytes 589828
  46.8 90.1 %all-gather.33.cloned.1.call-start = ((), (), s32[]{:S(2)}) async-start(), calls=%async_computation.20 | async-start | bytes 1769472 | tf_op jit(solution)/shard_map/all_gather | solution.py:245
  47.6 124.3 %all-gather.27.cloned.1.call-start = ((), (), s32[]{:S(2)}) async-start(), calls=%async_computation.9 | async-start | bytes 1474560 | tf_op jit(solution)/shard_map/all_gather | solution.py:544
  48.1 145.4 %all-gather.29.cloned.1.call-start = ((), (), s32[]{:S(2)}) async-start(), calls=%async_computation.10 | async-start | bytes 5898240 | tf_op jit(solution)/shard_map/all_gather | solution.py:548
  48.7 183.8 %all-gather.31.cloned.1.call-start = ((), (), s32[]{:S(2)}) async-start(), calls=%async_computation.11 | async-start | bytes 5898240 | tf_op jit(solution)/shard_map/all_gather | solution.py:550
  49.3 232.9 %all-gather.39.cloned.1.call-start = ((), (), s32[]{:S(2)}) async-start(), calls=%async_computation.23 | async-start | bytes 1769472 | tf_op jit(solution)/shard_map/all_gather | solution.py:246
  49.4 313.7 %copy-start.53 = (f32[768]{0:T(1024)}, f32[768]{0:T(1024)S(1)}, u32[]{:S(2)}) copy-start(f32[768]{0:T(1024)S(1)} %convert_element_type.401) | copy-start | bytes 9220
  54.6 177.9 %copy-start.87 = (f32[768]{0:T(1024)}, f32[768]{0:T(1024)S(1)}, u32[]{:S(2)}) copy-start(f32[768]{0:T(1024)S(1)} %convert_element_type.405) | copy-start | bytes 9220
  171.7 21.9 %copy-start.17 = (bf16[128,768]{0,1:T(8,128)(2,1)}, bf16[128,768]{0,1:T(8,128)(2,1)S(1)}, u32[]{:S(2)}) copy-start(bf16[128,768]{0,1:T(8,128)(2,1)S(1)} %get-tuple-element.3145) | copy-start | bytes 589828
  171.7 25.1 %copy-start.50 = (f32[1,12,128]{2,1,0:T(8,128)}, f32[1,12,128]{2,1,0:T(8,128)S(1)}, u32[]{:S(2)}) copy-start(f32[1,12,128]{2,1,0:T(8,128)S(1)} %get-tuple-element.1823) | copy-start | bytes 18436
  171.8 21.8 %copy-start.32 = (bf16[1,128,12,64]{1,3,2,0:T(8,128)(2,1)}, bf16[1,128,12,64]{1,3,2,0:T(8,128)(2,1)S(1)}, u32[]{:S(2)}) copy-start(bf16[1,128,12,64]{1,3,2,0:T(8,128)(2,1)S(1)} %divide_convert_fusion.1) | copy-start | bytes 589828
  174.6 57.9 %copy-start.4 = (f32[128,768]{1,0:T(8,128)}, f32[128,768]{1,0:T(8,128)S(1)}, u32[]{:S(2)}) copy-start(f32[128,768]{1,0:T(8,128)S(1)} %get-tuple-element.2269) | copy-start | bytes 1179652
  174.6 22.2 %copy-start.57 = (f32[128]{0:T(128)}, f32[128]{0:T(128)S(1)}, u32[]{:S(2)}) copy-start(f32[128]{0:T(128)S(1)} %broadcast_multiply_fusion.10) | copy-start | bytes 1540
  174.8 22.0 %copy-start.64 = (f32[128]{0:T(128)}, f32[128]{0:T(128)S(1)}, u32[]{:S(2)}) copy-start(f32[128]{0:T(128)S(1)} %add_rsqrt_fusion.2) | copy-start | bytes 1540
  196.8 39.3 %copy-start.12 = (f32[128,3072]{1,0:T(8,128)}, f32[128,3072]{1,0:T(8,128)S(1)}, u32[]{:S(2)}) copy-start(f32[128,3072]{1,0:T(8,128)S(1)} %convolution_add_fusion.1) | copy-start | bytes 4718596
  236.1 126.2 %copy-start.8 = (f32[128,768]{1,0:T(8,128)}, f32[128,768]{1,0:T(8,128)S(1)}, u32[]{:S(2)}) copy-start(f32[128,768]{1,0:T(8,128)S(1)} %get-tuple-element.2271) | copy-start | bytes 1179652
  237.9 89.5 %all-gather.37.cloned.1.call-start = ((), (), s32[]{:S(2)}) async-start(), calls=%async_computation.22 | async-start | bytes 1769472 | tf_op jit(solution)/shard_map/all_gather | solution.py:245
  238.6 235.7 %all-gather.41.cloned.1.call-start = ((), (), s32[]{:S(2)}) async-start(), calls=%async_computation.24 | async-start | bytes 1769472 | tf_op jit(solution)/shard_map/all_gather | solution.py:387
  239.4 237.6 %all-gather.43.cloned.1.call-start = ((), (), s32[]{:S(2)}) async-start(), calls=%async_computation.25 | async-start | bytes 1769472 | tf_op jit(solution)/shard_map/all_gather | solution.py:388
  330.6 31.7 %copy-start = (bf16[768,768]{1,0:T(8,128)(2,1)S(1)}, bf16[768,768]{1,0:T(8,128)(2,1)}, u32[]{:S(2)}) copy-start(bf16[768,768]{1,0:T(8,128)(2,1)} %all-gather.27.cloned.1.call-done) | copy-start | bytes 3538948
  362.8 183.7 %copy-start.2 = (f32[128,768]{1,0:T(8,128)}, f32[128,768]{1,0:T(8,128)S(1)}, u32[]{:S(2)}) copy-start(f32[128,768]{1,0:T(8,128)S(1)} %get-tuple-element.2273) | copy-start | bytes 1179652
  362.8 11.5 copy-start.59
  363.1 11.3 copy-start.67
  363.1 8.9 slice-start
  366.5 5.5 copy-start.10
  366.5 5.5 slice-start.1
  376.4 186.1 %all-gather.45.cloned.1.call-start = ((), (), s32[]{:S(2)}) async-start(), calls=%async_computation.26 | async-start | bytes 1769472 | tf_op jit(solution)/shard_map/all_gather | solution.py:387
  377.1 276.3 %all-gather.47.cloned.1.call-start = ((), (), s32[]{:S(2)}) async-start(), calls=%async_computation.27 | async-start | bytes 1769472 | tf_op jit(solution)/shard_map/all_gather | solution.py:388
  514.9 10.7 slice-start.2
  530.5 166.9 %reduce-scatter.13.cloned.1.call-start = ((), (), s32[]{:S(2)}) async-start(), calls=%async_computation.14 | async-start | bytes 1474560 | tf_op jit(solution)/shard_map/reduce_scatter | solution.py:457
  533.0 164.4 %reduce-scatter.15.cloned.1.call-start = ((), (), s32[]{:S(2)}) async-start(), calls=%async_computation.15 | async-start | bytes 1474560 | tf_op jit(solution)/shard_map/reduce_scatter | solution.py:457
  535.5 203.4 %reduce-scatter.21.cloned.1.call-start = ((), (), s32[]{:S(2)}) async-start(), calls=%async_computation.18 | async-start | bytes 5898240 | tf_op jit(solution)/shard_map/reduce_scatter | solution.py:475
  540.9 248.5 %reduce-scatter.23.cloned.1.call-start = ((), (), s32[]{:S(2)}) async-start(), calls=%async_computation.19 | async-start | bytes 5898240 | tf_op jit(solution)/shard_map/reduce_scatter | solution.py:475
  546.2 293.4 %reduce-scatter.17.cloned.1.call-start = ((), (), s32[]{:S(2)}) async-start(), calls=%async_computation.16 | async-start | bytes 5898240 | tf_op jit(solution)/shard_map/reduce_scatter | solution.py:469
  551.0 339.0 %reduce-scatter.19.cloned.1.call-start = ((), (), s32[]{:S(2)}) async-start(), calls=%async_computation.17 | async-start | bytes 5898240 | tf_op jit(solution)/shard_map/reduce_scatter | solution.py:469
  555.8 377.2 %reduce-scatter.9.cloned.1.call-start = ((), (), s32[]{:S(2)}) async-start(), calls=%async_computation.12 | async-start | bytes 4423680 | tf_op jit(solution)/shard_map/reduce_scatter | solution.py:451
  560.0 416.1 %reduce-scatter.11.cloned.1.call-start = ((), (), s32[]{:S(2)}) async-start(), calls=%async_computation.13 | async-start | bytes 4423680 | tf_op jit(solution)/shard_map/reduce_scatter | solution.py:451
  562.5 35.0 %copy-start.36 = (bf16[128,768]{1,0:T(8,128)(2,1)S(1)}, bf16[128,768]{1,0:T(8,128)(2,1)}, u32[]{:S(2)}) copy-start(bf16[128,768]{1,0:T(8,128)(2,1)} %convolution_convert_fusion.8) | copy-start | bytes 589828
  562.5 67.3 %copy-start.18 = (bf16[128,768]{0,1:T(8,128)(2,1)S(1)}, bf16[128,768]{0,1:T(8,128)(2,1)}, u32[]{:S(2)}) copy-start(bf16[128,768]{0,1:T(8,128)(2,1)} %copy-done.17) | copy-start | bytes 589828
  697.0 521.0 %all-reduce.28.cloned.1.call-start = ((), (), s32[]{:S(2)}) async-start(), calls=%async_computation.28 | async-start | bytes 14155776 | tf_op jit(solution)/shard_map/psum | solution.py:496
  987.8 53.0 %copy-start.20 = (f32[128,768]{1,0:T(8,128)S(1)}, f32[128,768]{1,0:T(8,128)}, u32[]{:S(2)}) copy-start(f32[128,768]{1,0:T(8,128)} %copy-done.19) | copy-start | bytes 1179652
  987.9 53.0 %copy-start.84 = (f32[128]{0:T(128)S(1)}, f32[128]{0:T(128)}, u32[]{:S(2)}) copy-start(f32[128]{0:T(128)} %copy-done.82) | copy-start | bytes 1540
  (69 other events, 182.6 us)
Sparse Core Ops, SparseCore 0:
  9.6 33.6 all-gather.24
  46.9 44.1 all-gather.34
  93.9 42.9 all-gather.32
  138.3 16.2 all-gather.26
  156.0 37.4 all-gather.28
  195.0 37.4 all-gather.30
  238.0 44.1 all-gather.38
  284.4 42.9 all-gather.36
  329.6 42.9 all-gather.40
  376.5 78.7 all-gather.42
  457.5 42.9 all-gather.44
  530.6 101.9 all-gather.46
  635.2 24.4 reduce-scatter.12
  662.9 25.7 reduce-scatter.14
  691.1 47.8 reduce-scatter.20
  741.5 47.7 reduce-scatter.22
  791.7 47.8 reduce-scatter.16
  842.1 47.8 reduce-scatter.18
  892.6 40.4 reduce-scatter.8
  935.6 40.4 reduce-scatter.10
  981.7 236.3 all-reduce.27
where the time goes:
time: 1250 us; the launch traced here: 1230 us
  waiting for transfers between devices  656 us (52%)
  blocking collectives  229 us (18%)
  local copies, waits for them, and re-layouts  148 us (12%)
  matrix products  89.6 us (7%)
  loops' own time  53.9 us (4%)
  other arithmetic  36 us (3%)
  between operations  18.9 us (2%)
    psum x1, waiting for transfers between devices, reduce_grads(): lax.psum((share_gain_one, share_bias_one, share_weight_qkv, share_bias_qv...  176 us
    reduce_scatter x2, waiting for transfers between devices, reduce_grads(): lax.psum_scatter(grad_weight_fc.astype(jnp.bfloat16), 'fsdp', scatter_dim...  97.4 us
    reduce_scatter x2, waiting for transfers between devices, reduce_grads(): lax.psum_scatter(grad_weight_out.astype(jnp.bfloat16), 'fsdp', scatter_di...  90 us
    all_gather x2, waiting for transfers between devices, layer_forward(): lax.all_gather(key_flat, 'ctx', axis=1, tiled=True)  86.7 us
    reduce_scatter x2, waiting for transfers between devices, reduce_grads(): lax.psum_scatter(grad_weight_qkv.astype(jnp.bfloat16), 'fsdp', scatter_di...  82.7 us
    all_gather x2, blocking collectives, layer_backward(): lax.all_gather(row_delta, 'ctx', axis=2, tiled=True)  68.6 us
    all_gather x2, blocking collectives, layer_backward(): lax.all_gather(lse, 'ctx', axis=2, tiled=True)  64.7 us
    all_gather x2, waiting for transfers between devices, layer_forward(): lax.all_gather(value_flat, 'ctx', axis=1, tiled=True)  57.6 us
  transfers between devices with their start and end apart: 21, of which 14 were waited for; matrix products, arithmetic and copies ran while one was open for 20% of the time, Pallas kernels for 0%

commit v1 on v0

v1 whole, which is shorter than its diff:
```python
from functools import partial

import jax
import jax.numpy as jnp
from jax import lax
from jax.experimental import pallas as pl
from jax.experimental.pallas import tpu as pltpu
from jax.sharding import PartitionSpec as P

D = 768
HEADS = 12
HDIM = 64
PAIRS = HEADS // 2
LANES = 128
EPSILON = 1e-05
NEGATIVE = -1e30
SCALE = HDIM ** (-0.5)
MESH = pl.DeviceIdType.MESH
F32 = jnp.float32
BF16 = jnp.bfloat16


def norm_forward(resid, gain_row, bias_row):
    average = jnp.mean(resid, axis=-1, keepdims=True)
    centred = resid - average
    variance = jnp.mean(centred * centred, axis=-1, keepdims=True)
    inverse = lax.rsqrt(variance + EPSILON)
    normal = centred * inverse
    return ((normal * gain_row + bias_row).astype(BF16), normal, inverse)


def norm_backward(grad_normed, normal, inverse, gain_row):
    scaled = grad_normed * gain_row
    mean_term = jnp.mean(scaled, axis=-1, keepdims=True)
    second = jnp.mean(scaled * normal, axis=-1, keepdims=True)
    grad_input = inverse * (scaled - mean_term - normal * second)
    return (grad_input, jnp.sum(grad_normed * normal, axis=0), jnp.sum(grad_normed, axis=0))


def two_heads(rows):
    lane = lax.broadcasted_iota(jnp.int32, rows.shape, 1)
    zero = jnp.zeros_like(rows)
    first = jnp.where(lane < HDIM, rows, zero)
    second = jnp.where(lane < HDIM, zero, rows)
    return jnp.concatenate([first, second], axis=0)


def one_pair(stacked):
    half = stacked.shape[0] // 2
    lane = lax.broadcasted_iota(jnp.int32, (half, LANES), 1)
    return jnp.where(lane < HDIM, stacked[:half], stacked[half:])


def dot_rows(left, right):
    return lax.dot_general(left, right, (((1,), (1,)), ((), ())), preferred_element_type=F32)


def pick_lanes(columns, pair):
    lane = lax.broadcasted_iota(jnp.int32, columns.shape, 1)
    first = jnp.sum(jnp.where(lane == 2 * pair, columns, 0.0), axis=1, keepdims=True)
    second = jnp.sum(jnp.where(lane == 2 * pair + 1, columns, 0.0), axis=1, keepdims=True)
    return jnp.concatenate([first, second], axis=0)


def mask_columns(bias_ref, own_segs, all_segs_ref, start, own_is_query):
    rows, columns = bias_ref.shape
    step = min(1024, columns)
    own_place = start + lax.broadcasted_iota(jnp.int32, (rows, step), 0)
    for offset in range(0, columns, step):
        place = offset + lax.broadcasted_iota(jnp.int32, (rows, step), 1)
        causal = (place <= own_place) if own_is_query else (own_place <= place)
        same = own_segs == all_segs_ref[:, offset : offset + step]
        bias_ref[:, offset : offset + step] = jnp.where(causal & same, 0.0, NEGATIVE)


def attention_forward_kernel(
    start_ref, q_ref, k_ref, v_ref, own_segs_ref, all_segs_ref, out_ref, lse_ref, lse_rows_ref, bias_ref
):
    pair = pl.program_id(0)
    rows, keys = bias_ref.shape

    @pl.when(pair == 0)
    def _():
        mask_columns(bias_ref, own_segs_ref[...], all_segs_ref, start_ref[0], True)
        lse_ref[...] = jnp.zeros_like(lse_ref)

    queries = two_heads(q_ref[...] * jnp.asarray(SCALE, BF16))
    step = min(1024, keys)

    def scores_of(offset):
        scores = dot_rows(queries, k_ref[pl.ds(offset, step), :])
        bias = bias_ref[:, pl.ds(offset, step)]
        return scores + jnp.concatenate([bias, bias], axis=0)

    if step == keys:
        scores = scores_of(0)
        top = jnp.max(scores, axis=1, keepdims=True)
        weights = jnp.exp(scores - top)
        total = jnp.sum(weights, axis=1, keepdims=True)
        mixed = jnp.dot(weights.astype(BF16), v_ref[...], preferred_element_type=F32)
    else:

        def visit(index, carried):
            top, total, mixed = carried
            offset = pl.multiple_of(index * step, step)
            scores = scores_of(offset)
            new_top = jnp.maximum(top, jnp.max(scores, axis=1, keepdims=True))
            weights = jnp.exp(scores - new_top)
            factor = jnp.exp(top - new_top)
            total = total * factor + jnp.sum(weights, axis=1, keepdims=True)
            more = jnp.dot(
                weights.astype(BF16), v_ref[pl.ds(offset, step), :], preferred_element_type=F32
            )
            return new_top, total, mixed * factor + more

        top, total, mixed = lax.fori_loop(
            0,
            (start_ref[0] + rows + step - 1) // step,
            visit,
            (
                jnp.full((2 * rows, 1), NEGATIVE, F32),
                jnp.zeros((2 * rows, 1), F32),
                jnp.zeros((2 * rows, LANES), F32),
            ),
        )
    out_ref[...] = one_pair(mixed / total).astype(BF16)
    lse = top + jnp.log(total)
    lane = lax.broadcasted_iota(jnp.int32, (rows, LANES), 1)
    kept = lse_ref[...]
    kept = jnp.where(lane == 2 * pair, lse[:rows], kept)
    kept = jnp.where(lane == 2 * pair + 1, lse[rows:], kept)
    lse_ref[...] = kept

    @pl.when(pair == PAIRS - 1)
    def _():
        lse_rows_ref[...] = kept.T[:16]


def attention_forward(start, queries, kv, own_segs, all_segs):
    rows = queries.shape[0]
    keys = kv.shape[0]
    whole = lambda shape: pl.BlockSpec(shape, lambda p: (0, 0))
    return pl.pallas_call(
        attention_forward_kernel,
        grid=(PAIRS,),
        in_specs=[
            pl.BlockSpec(memory_space=pltpu.SMEM),
            pl.BlockSpec((rows, LANES), lambda p: (0, p)),
            pl.BlockSpec((keys, LANES), lambda p: (0, p)),
            pl.BlockSpec((keys, LANES), lambda p: (0, PAIRS + p)),
            whole((rows, 1)),
            whole((1, keys)),
        ],
        out_specs=[
            pl.BlockSpec((rows, LANES), lambda p: (0, p)),
            whole((rows, LANES)),
            whole((16, rows)),
        ],
        out_shape=[
            jax.ShapeDtypeStruct((rows, D), BF16),
            jax.ShapeDtypeStruct((rows, LANES), F32),
            jax.ShapeDtypeStruct((16, rows), F32),
        ],
        scratch_shapes=[pltpu.VMEM((rows, keys), F32)],
        compiler_params=pltpu.CompilerParams(vmem_limit_bytes=40 << 20),
        cost_estimate=pl.CostEstimate(
            flops=8 * rows * keys * D, bytes_accessed=4 * keys * D, transcendentals=rows * keys * HEADS
        ),
        name="attention_forward",
    )(start, queries, kv, kv, own_segs, all_segs)


def attention_backward_kernel(
    start_ref,
    q_ref,
    grad_ref,
    k_own_ref,
    v_own_ref,
    lse_ref,
    delta_ref,
    k_ref,
    v_ref,
    q_all_ref,
    grad_all_ref,
    stats_ref,
    own_segs_ref,
    all_segs_ref,
    out_ref,
    query_bias_ref,
    key_bias_ref,
):
    pair = pl.program_id(0)
    rows, tokens = query_bias_ref.shape
    start = start_ref[0]

    @pl.when(pair == 0)
    def _():
        mask_columns(query_bias_ref, own_segs_ref[...], all_segs_ref, start, True)
        mask_columns(key_bias_ref, own_segs_ref[...], all_segs_ref, start, False)

    step = min(256, tokens)
    blocks = step // rows
    scale = jnp.asarray(SCALE, BF16)

    def doubled(bias):
        return jnp.concatenate([bias, bias], axis=0)

    queries = two_heads(q_ref[...] * scale)
    grads = two_heads(grad_ref[...])
    lse = pick_lanes(lse_ref[...], pair)
    delta = pick_lanes(delta_ref[...], pair)

    def visit_keys(index, grad_query):
        offset = pl.multiple_of(index * step, step)
        keys = k_ref[pl.ds(offset, step), :]
        values = v_ref[pl.ds(offset, step), :]
        bias = doubled(query_bias_ref[:, pl.ds(offset, step)])
        attention = jnp.exp(dot_rows(queries, keys) + bias - lse)
        grad_attention = dot_rows(grads, values)
        grad_scores = (attention * (grad_attention - delta)).astype(BF16)
        return grad_query + jnp.dot(grad_scores, keys, preferred_element_type=F32)

    zeros = jnp.zeros((2 * rows, LANES), F32)
    grad_query = lax.fori_loop(0, (start + rows + step - 1) // step, visit_keys, zeros)

    own_keys = two_heads(k_own_ref[...] * scale)
    own_values = two_heads(v_own_ref[...])

    def row_of(block, row):
        return jnp.broadcast_to(stats_ref[block, pl.ds(row, 1), :], (rows, rows))

    def stat_rows(index, row):
        first = [row_of(index * blocks + b, row + 2 * pair) for b in range(blocks)]
        second = [row_of(index * blocks + b, row + 2 * pair + 1) for b in range(blocks)]
        return jnp.concatenate(
            [jnp.concatenate(first, axis=1), jnp.concatenate(second, axis=1)], axis=0
        )

    def visit_queries(index, carried):
        grad_keys, grad_values = carried
        offset = pl.multiple_of(index * step, step)
        later = q_all_ref[pl.ds(offset, step), :]
        later_grads = grad_all_ref[pl.ds(offset, step), :]
        bias = doubled(key_bias_ref[:, pl.ds(offset, step)])
        attention = jnp.exp(dot_rows(own_keys, later) + bias - stat_rows(index, 0))
        grad_attention = dot_rows(own_values, later_grads)
        grad_scores = (attention * (grad_attention - stat_rows(index, 16))).astype(BF16)
        grad_keys = grad_keys + jnp.dot(grad_scores, later, preferred_element_type=F32)
        grad_values = grad_values + jnp.dot(
            attention.astype(BF16), later_grads, preferred_element_type=F32
        )
        return grad_keys, grad_values

    grad_keys, grad_values = lax.fori_loop(
        start // step, tokens // step, visit_queries, (zeros, zeros)
    )
    base = pl.multiple_of(pair * LANES, LANES)
    out_ref[:, pl.ds(base, LANES)] = (one_pair(grad_query) * SCALE).astype(BF16)
    out_ref[:, pl.ds(D + base, LANES)] = (one_pair(grad_keys) * SCALE).astype(BF16)
    out_ref[:, pl.ds(2 * D + base, LANES)] = one_pair(grad_values).astype(BF16)


def attention_backward(
    start, queries, grads, kv_own, lse, delta, kv, q_all, grad_all, stats, own_segs, all_segs
):
    rows = queries.shape[0]
    tokens = kv.shape[0]
    whole = lambda shape: pl.BlockSpec(shape, lambda p: (0,) * len(shape))
    own = pl.BlockSpec((rows, LANES), lambda p: (0, p))
    every = pl.BlockSpec((tokens, LANES), lambda p: (0, p))
    return pl.pallas_call(
        attention_backward_kernel,
        grid=(PAIRS,),
        in_specs=[
            pl.BlockSpec(memory_space=pltpu.SMEM),
            own,
            own,
            own,
            pl.BlockSpec((rows, LANES), lambda p: (0, PAIRS + p)),
            whole((rows, LANES)),
            whole((rows, LANES)),
            every,
            pl.BlockSpec((tokens, LANES), lambda p: (0, PAIRS + p)),
            every,
            every,
            whole(stats.shape),
            whole((rows, 1)),
            whole((1, tokens)),
        ],
        out_specs=whole((rows, 3 * D)),
        out_shape=jax.ShapeDtypeStruct((rows, 3 * D), BF16),
        scratch_shapes=[pltpu.VMEM((rows, tokens), F32), pltpu.VMEM((rows, tokens), F32)],
        compiler_params=pltpu.CompilerParams(vmem_limit_bytes=44 << 20),
        cost_estimate=pl.CostEstimate(
            flops=16 * rows * tokens * D,
            bytes_accessed=8 * tokens * D,
            transcendentals=rows * tokens * HEADS,
        ),
        name="attention_backward",
    )(
        start,
        queries,
        grads,
        kv_own,
        kv_own,
        lse,
        delta,
        kv,
        kv,
        q_all,
        grad_all,
        stats,
        own_segs,
        all_segs,
    )


def place_bits():
    ctx, fsdp = lax.axis_index("ctx"), lax.axis_index("fsdp")
    return lax.rem(ctx, 2), ctx // 2, fsdp // 2, lax.rem(fsdp, 2)


def greet(devices):
    barrier = pltpu.get_barrier_semaphore()
    for device in devices:
        pl.semaphore_signal(barrier, inc=1, device_id=device, device_id_type=MESH)
    pl.semaphore_wait(barrier, len(devices))


WEIGHT_COPIES = 11


def gather_weights_kernel(count, *refs):
    shares, fulls = refs[:count], refs[count : 2 * count]
    send_sems, recv_sems, local_sems = refs[2 * count :]
    x, z, y, core = place_bits()
    low = lax.rem(z, 2)
    z_next = z + 1 - 2 * low
    sibling = (2 * z + x, 2 * y + 1 - core)
    over_y = (2 * z + x, 2 * (1 - y) + core)
    over_x = (2 * z + 1 - x, 2 * y + core)
    over_z = (2 * z_next + x, 2 * y + core)
    own = 2 * y + core
    other = 2 * (1 - y) + core
    greet((sibling, over_y, over_x, over_z))

    def copy(index, which, src, dst, device):
        slot = which * WEIGHT_COPIES + index
        return pltpu.make_async_remote_copy(
            src_ref=src,
            dst_ref=dst,
            send_sem=send_sems.at[slot],
            recv_sem=recv_sems.at[slot],
            device_id=device,
            device_id_type=MESH,
        )

    started = []
    locals_started = []
    plans = []
    for which in range(count):
        share, full = shares[which], fulls[which]
        rows, columns = share.shape
        part = rows // 4
        half = columns // 2

        def piece(ref, x_bit, low_bit, part=part):
            return ref.at[pl.ds((2 * low_bit + x_bit) * part, part), :]

        def piece_half(ref, x_bit, low_bit, side, part=part, half=half):
            return ref.at[pl.ds((2 * low_bit + x_bit) * part, part), pl.ds(side * half, half)]

        theirs = full.at[other]
        same = lambda index, view, device, which=which: copy(index, which, view, view, device)
        mine = piece(theirs, x, low)
        from_x = piece(theirs, 1 - x, low)
        from_z = piece(theirs, x, 1 - low)
        plan = {
            0: copy(0, which, piece(share, x, low), piece(full.at[own], x, low), over_y),
            1: same(1, mine, over_x),
            2: same(2, mine, over_z),
            3: same(3, mine, sibling),
            4: same(4, piece_half(theirs, 1 - x, low, 0), over_z),
            5: same(5, from_x, sibling),
            6: same(6, piece_half(theirs, x, 1 - low, 1), over_x),
            7: same(7, from_z, sibling),
            8: same(8, piece_half(theirs, 1 - x, 1 - low, 0), sibling),
            9: same(9, piece_half(theirs, 1 - x, 1 - low, 1), sibling),
            10: copy(10, which, share, full.at[own], sibling),
        }
        plans.append(plan)
        plan[0].start()
        plan[10].start()
        local = pltpu.make_async_copy(share, full.at[own], local_sems.at[which])
        local.start()
        locals_started.append(local)

    for step in range(count + 2):
        if step < count:
            plan = plans[step]
            plan[0].wait_recv()
            plan[1].start()
            plan[2].start()
            plan[3].start()
        if 0 <= step - 1 < count:
            plan = plans[step - 1]
            plan[1].wait_recv()
            plan[4].start()
            plan[5].start()
            plan[2].wait_recv()
            plan[6].start()
            plan[7].start()
        if 0 <= step - 2 < count:
            plan = plans[step - 2]
            plan[4].wait_recv()
            plan[8].start()
            plan[6].wait_recv()
            plan[9].start()
    for plan in plans:
        for index in (3, 5, 7, 8, 9, 10):
            plan[index].wait_recv()
        for index in range(WEIGHT_COPIES):
            plan[index].wait_send()
    for local in locals_started:
        local.wait()


def gather_weights(shares, collective_id):
    count = len(shares)
    copies = count * WEIGHT_COPIES
    anywhere = pl.BlockSpec(memory_space=pl.ANY)
    fulls = pl.pallas_call(
        partial(gather_weights_kernel, count),
        in_specs=[anywhere] * count,
        out_specs=[anywhere] * count,
        out_shape=[jax.ShapeDtypeStruct((4, *share.shape), share.dtype) for share in shares],
        scratch_shapes=[
            pltpu.SemaphoreType.DMA((copies,)),
            pltpu.SemaphoreType.DMA((copies,)),
            pltpu.SemaphoreType.DMA((count,)),
        ],
        compiler_params=pltpu.CompilerParams(collective_id=collective_id, has_side_effects=True),
        name="gather_weights",
    )(*shares)
    return fulls


BLOCK_COPIES = 13


def gather_blocks_kernel(count, *refs):
    blocks, fulls = refs[:count], refs[count : 2 * count]
    send_sems, recv_sems, local_sems = refs[2 * count :]
    x, z, y, core = place_bits()
    sibling = (2 * z + x, 2 * y + 1 - core)
    over_x = (2 * z + 1 - x, 2 * y + core)
    over_y = (2 * z + x, 2 * (1 - y) + core)
    greet((sibling, over_x, over_y))

    plans = []
    locals_started = []
    for which in range(count):
        block, full = blocks[which], fulls[which]
        half = block.shape[0] // 2

        def copy(index, src, dst, device, which=which):
            slot = which * BLOCK_COPIES + index
            return pltpu.make_async_remote_copy(
                src_ref=src,
                dst_ref=dst,
                send_sem=send_sems.at[slot],
                recv_sem=recv_sems.at[slot],
                device_id=device,
                device_id_type=MESH,
            )

        def part(ref, side, half=half):
            return ref.at[pl.ds(side * half, half), :]

        def slot_of(x_bit, y_bit, full=full):
            return full.at[4 * y_bit + 2 * core + x_bit]

        same = lambda index, view, device, copy=copy: copy(index, view, view, device)
        mine = slot_of(x, y)
        from_x, from_y, from_both = slot_of(1 - x, y), slot_of(x, 1 - y), slot_of(1 - x, 1 - y)
        plan = {
            0: copy(0, block, mine, sibling),
            1: copy(1, part(block, 0), part(mine, 0), over_x),
            2: copy(2, part(block, 1), part(mine, 1), over_y),
            3: copy(3, part(block, 1), part(mine, 1), over_x),
            4: copy(4, part(block, 0), part(mine, 0), over_y),
            5: same(5, part(from_x, 0), over_y),
            6: same(6, part(from_x, 0), sibling),
            7: same(7, part(from_y, 1), over_x),
            8: same(8, part(from_y, 1), sibling),
            9: same(9, part(from_x, 1), sibling),
            10: same(10, part(from_y, 0), sibling),
            11: same(11, part(from_both, 0), sibling),
            12: same(12, part(from_both, 1), sibling),
        }
        plans.append(plan)
        for index in (1, 2, 3, 4, 0):
            plan[index].start()
        local = pltpu.make_async_copy(block, mine, local_sems.at[which])
        local.start()
        locals_started.append(local)

    for plan in plans:
        plan[1].wait_recv()
        plan[5].start()
        plan[6].start()
        plan[2].wait_recv()
        plan[7].start()
        plan[8].start()
    for plan in plans:
        plan[3].wait_recv()
        plan[9].start()
        plan[4].wait_recv()
        plan[10].start()
    for plan in plans:
        plan[5].wait_recv()
        plan[11].start()
        plan[7].wait_recv()
        plan[12].start()
    for plan in plans:
        for index in (0, 6, 8, 9, 10, 11, 12):
            plan[index].wait_recv()
        for index in range(BLOCK_COPIES):
            plan[index].wait_send()
    for local in locals_started:
        local.wait()


def gather_blocks(blocks, collective_id):
    count = len(blocks)
    copies = count * BLOCK_COPIES
    anywhere = pl.BlockSpec(memory_space=pl.ANY)
    return pl.pallas_call(
        partial(gather_blocks_kernel, count),
        in_specs=[anywhere] * count,
        out_specs=[anywhere] * count,
        out_shape=[jax.ShapeDtypeStruct((8, *block.shape), block.dtype) for block in blocks],
        scratch_shapes=[
            pltpu.SemaphoreType.DMA((copies,)),
            pltpu.SemaphoreType.DMA((copies,)),
            pltpu.SemaphoreType.DMA((count,)),
        ],
        compiler_params=pltpu.CompilerParams(collective_id=collective_id, has_side_effects=True),
        name="gather_blocks",
    )(*blocks)


class PlaneLinks:
    def __init__(self):
        self.x, self.z, self.y, self.core = place_bits()
        self.block = 2 * lax.axis_index("fsdp") + self.x
        self.count = 8

    def permute(self, value, target):
        pairs = [(c * 4 + f, target(c, f)) for c in range(8) for f in range(4)]
        return lax.ppermute(value, ("ctx", "fsdp"), pairs)

    def swap(self, value):
        return self.permute(value, lambda c, f: (2 * f + c % 2) * 4 + c // 2)

    enter = swap
    leave = swap

    def across(self, value, axis):
        target = {
            "core": lambda c, f: c * 4 + (f ^ 1),
            "y": lambda c, f: c * 4 + (f ^ 2),
            "x": lambda c, f: (c ^ 1) * 4 + f,
            "z": lambda c, f: (c ^ 2) * 4 + f,
            "zz": lambda c, f: (c ^ 4) * 4 + f,
        }[axis]
        return self.permute(value, target)

    def weights(self, shares):
        return gather_weights(shares, 0)

    def blocks(self, blocks, collective_id):
        return gather_blocks(blocks, collective_id)

    def halve(self, total, bit, axis):
        rows = total.shape[0] // 2
        sent = lax.dynamic_slice_in_dim(total, (1 - bit) * rows, rows, 0).astype(BF16)
        kept = lax.dynamic_slice_in_dim(total, bit * rows, rows, 0)
        return kept + self.across(sent, axis).astype(F32)

    def double(self, rows, bit, axis):
        got = self.across(rows, axis)
        low = jnp.where(bit == 0, rows, got)
        high = jnp.where(bit == 0, got, rows)
        return jnp.concatenate([low, high], axis=0)

    def weight_sum(self, left, right):
        tokens, rows = left.shape
        quarter = rows // 4
        columns = left.reshape(tokens, 2, 2, quarter)

        def term(part):
            return lax.dot_general(
                part, right, (((0,), (0,)), ((), ())), preferred_element_type=F32
            )

        pick = lambda array, index, axis: lax.dynamic_index_in_dim(array, index, axis, keepdims=False)
        sent = term(pick(columns, 1 - self.core, 2).reshape(tokens, 2 * quarter)).astype(BF16)
        got = self.across(sent, "core").reshape(2, quarter, right.shape[1])
        mine = pick(columns, self.core, 2)
        sent = (term(pick(mine, 1 - self.y, 1)) + pick(got, 1 - self.y, 0).astype(F32)).astype(BF16)
        got_y = self.across(sent, "y")
        kept = term(pick(mine, self.y, 1)) + pick(got, self.y, 0).astype(F32)
        total = kept + got_y.astype(F32)
        low, high = lax.rem(self.z, 2), self.z // 2
        total = self.halve(total, self.x, "x")
        total = self.halve(total, low, "z")
        total = self.halve(total, high, "zz").astype(BF16)
        total = self.double(total, high, "zz")
        total = self.double(total, low, "z")
        return self.double(total, self.x, "x").astype(F32)

    def vector_sum(self, packed):
        for axis in ("core", "y", "x", "z", "zz"):
            packed = packed + self.across(packed, axis)
        return lax.dynamic_index_in_dim(packed, 2 * self.y + self.core, 0, keepdims=False)


class PlainLinks:
    def __init__(self, ctx_size, fsdp_size):
        self.block = lax.axis_index("ctx")
        self.count = ctx_size
        self.fsdp_size = fsdp_size

    def enter(self, value):
        return value

    leave = enter

    def weights(self, shares):
        return [lax.all_gather(share, "fsdp", axis=0) for share in shares]

    def blocks(self, blocks, collective_id):
        return [lax.all_gather(block, "ctx", axis=0) for block in blocks]

    def weight_sum(self, left, right):
        term = lax.dot_general(left, right, (((0,), (0,)), ((), ())), preferred_element_type=F32)
        share = lax.psum_scatter(term.astype(BF16), "fsdp", scatter_dimension=0, tiled=True)
        return lax.psum(share.astype(F32), "ctx")

    def vector_sum(self, packed):
        share = lax.psum_scatter(packed, "fsdp", scatter_dimension=0, tiled=False)
        return lax.psum(share, "ctx")


def layer_forward(resid, weights, links, start, own_segs, segs, layer_index):
    (
        gain_one,
        bias_one,
        weight_qkv,
        bias_qv,
        weight_proj,
        bias_proj,
        gain_two,
        bias_two,
        weight_fc,
        bias_fc,
        weight_out,
        bias_out,
    ) = weights
    normed_one, normal_one, inverse_one = norm_forward(resid, gain_one, bias_one)
    projected = jnp.dot(normed_one, weight_qkv, preferred_element_type=F32)
    biases = jnp.concatenate([bias_qv[:D], jnp.zeros((D,), F32), bias_qv[D:]])
    projected = (projected + biases).astype(BF16)
    queries, kv_own = projected[:, :D], projected[:, D:]
    if layer_index == 0:
        kv, segs = links.blocks([kv_own, segs], 1)
        segs = segs[:, 0, :].reshape(1, -1)
    else:
        (kv,) = links.blocks([kv_own], 2)
    kv = kv.reshape(-1, 2 * D)
    attended, lse, lse_rows = attention_forward(start, queries, kv, own_segs, segs)
    middle = resid + jnp.dot(attended, weight_proj, preferred_element_type=F32) + bias_proj
    normed_two, normal_two, inverse_two = norm_forward(middle, gain_two, bias_two)
    hidden = jnp.dot(normed_two, weight_fc, preferred_element_type=F32) + bias_fc
    activated = jax.nn.gelu(hidden, approximate=True).astype(BF16)
    result_rows = middle + jnp.dot(activated, weight_out, preferred_element_type=F32) + bias_out
    saved = (
        normed_one,
        normal_one,
        inverse_one,
        queries,
        kv_own,
        kv,
        attended,
        lse,
        lse_rows,
        normed_two,
        normal_two,
        inverse_two,
        hidden,
        activated,
    )
    return result_rows, saved, segs


def layer_backward(gradient, weights, saved, links, start, own_segs, segs):
    (
        gain_one,
        _,
        weight_qkv,
        _,
        weight_proj,
        _,
        gain_two,
        _,
        weight_fc,
        _,
        weight_out,
        _,
    ) = weights
    (
        normed_one,
        normal_one,
        inverse_one,
        queries,
        kv_own,
        kv,
        attended,
        lse,
        lse_rows,
        normed_two,
        normal_two,
        inverse_two,
        hidden,
        activated,
    ) = saved
    rows = gradient.shape[0]
    total = lambda value: jnp.sum(value.astype(F32), axis=0)
    grad_branch = gradient.astype(BF16)
    grad_activated = dot_rows(grad_branch, weight_out)
    gelu_pull = jax.vjp(partial(jax.nn.gelu, approximate=True), hidden)[1]
    grad_hidden = gelu_pull(grad_activated)[0].astype(BF16)
    grad_normed_two = dot_rows(grad_hidden, weight_fc)
    grad_in_two, grad_gain_two, grad_bias_two = norm_backward(
        grad_normed_two, normal_two, inverse_two, gain_two
    )
    grad_middle = gradient + grad_in_two
    grad_proj = grad_middle.astype(BF16)
    grad_attended = dot_rows(grad_proj, weight_proj).astype(BF16)
    products = grad_attended.astype(F32) * attended.astype(F32)
    head_of = jnp.arange(D, dtype=jnp.int32) // HDIM
    by_lane = (head_of[:, None] == jnp.arange(LANES, dtype=jnp.int32)[None, :]).astype(F32)
    by_row = (jnp.arange(16, dtype=jnp.int32)[:, None] == head_of[None, :]).astype(F32)
    delta = jnp.dot(products, by_lane, precision=lax.Precision.HIGHEST, preferred_element_type=F32)
    delta_rows = lax.dot_general(
        by_row,
        products,
        (((1,), (1,)), ((), ())),
        precision=lax.Precision.HIGHEST,
        preferred_element_type=F32,
    )
    stats = jnp.concatenate([lse_rows, delta_rows], axis=0)
    q_all, grad_all, stats = links.blocks([queries, grad_attended, stats], 3)
    grad_projected = attention_backward(
        start,
        queries,
        grad_attended,
        kv_own,
        lse,
        delta,
        kv,
        q_all.reshape(-1, D),
        grad_all.reshape(-1, D),
        stats,
        own_segs,
        segs,
    )
    grad_normed_one = dot_rows(grad_projected, weight_qkv)
    grad_in_one, grad_gain_one, grad_bias_one = norm_backward(
        grad_normed_one, normal_one, inverse_one, gain_one
    )
    grad_input = grad_middle + grad_in_one
    matrices = (
        (activated, grad_branch),
        (normed_two, grad_hidden),
        (attended, grad_proj),
        (normed_one, grad_projected),
    )
    vectors = (
        grad_gain_one,
        grad_bias_one,
        jnp.concatenate([total(grad_projected[:, :D]), total(grad_projected[:, 2 * D :])]),
        total(grad_proj),
        grad_gain_two,
        grad_bias_two,
        total(grad_hidden),
        total(grad_branch),
    )
    return grad_input, matrices, vectors


def body(
    links_of,
    tokens,
    segment_ids,
    ln1_gain,
    ln1_bias,
    attn_weight,
    attn_bias,
    proj_weight,
    proj_bias,
    ln2_gain,
    ln2_bias,
    fc_weight,
    fc_bias,
    out_weight,
    out_bias,
    out_cotangent,
):
    members, seq_dev, features = tokens.shape
    links = links_of()
    start = (links.block * seq_dev).reshape(1).astype(jnp.int32)
    resid = links.enter(tokens[0])
    segs_row = links.enter(segment_ids)
    gradient = links.enter(out_cotangent[0])
    own_segs = segs_row.reshape(seq_dev, 1)
    segs = jnp.broadcast_to(segs_row, (16, seq_dev))

    vectors = (ln1_gain, ln1_bias, attn_bias, proj_bias, ln2_gain, ln2_bias, fc_bias, out_bias)
    sizes = [vector.shape[0] for vector in vectors]
    packed = jnp.concatenate(vectors)
    padding = -packed.shape[0] % (64 * 2 * LANES)
    packed = jnp.pad(packed, (0, padding)).reshape(-1, 2 * LANES)
    qkv_full, packed, proj_full, fc_full, out_full = links.weights(
        [attn_weight, packed, proj_weight, fc_weight, out_weight]
    )
    matrix = lambda full: full.reshape(-1, full.shape[-1])
    packed = packed.reshape(packed.shape[0], -1).astype(F32)
    pieces = []
    offset = 0
    for size in sizes:
        pieces.append(packed[:, offset : offset + size].reshape(-1))
        offset += size
    gain_one, bias_one, bias_qv, bias_proj, gain_two, bias_two, bias_fc, bias_out = pieces
    weights = (
        gain_one,
        bias_one,
        matrix(qkv_full),
        bias_qv,
        matrix(proj_full),
        bias_proj,
        gain_two,
        bias_two,
        matrix(fc_full),
        bias_fc,
        matrix(out_full),
        bias_out,
    )

    resid = resid.astype(F32)
    saved_layers = []
    for layer_index in range(2):
        resid, saved, segs = layer_forward(
            resid, weights, links, start, own_segs, segs, layer_index
        )
        saved_layers.append(saved)
    output = links.leave(resid.astype(BF16))
    gradient = gradient.astype(F32)
    collected = []
    for layer_index in (1, 0):
        gradient, matrices, terms = layer_backward(
            gradient, weights, saved_layers[layer_index], links, start, own_segs, segs
        )
        collected.append((matrices, terms))
    tokens_grad = links.leave(gradient.astype(BF16))

    sums = []
    for second, first in zip(collected[0][0], collected[1][0]):
        left = jnp.concatenate([second[0], first[0]], axis=0)
        right = jnp.concatenate([second[1], first[1]], axis=0)
        sums.append(links.weight_sum(left, right))
    out_grad, fc_grad, proj_grad, qkv_grad = sums
    shares = packed.shape[0]
    added = [a + b for a, b in zip(collected[0][1], collected[1][1])]
    rows = jnp.concatenate([vector.reshape(shares, -1) for vector in added], axis=1)
    summed = links.vector_sum(rows.reshape(shares, -1, LANES)).reshape(-1)
    small = []
    offset = 0
    for size in sizes:
        small.append(summed[offset : offset + size])
        offset += size
    g_gain_one, g_bias_one, g_bias_qv, g_bias_proj, g_gain_two, g_bias_two, g_bias_fc, g_bias_out = small
    return (
        output[None],
        tokens_grad[None],
        g_gain_one,
        g_bias_one,
        qkv_grad,
        g_bias_qv,
        proj_grad,
        g_bias_proj,
        g_gain_two,
        g_bias_two,
        fc_grad,
        g_bias_fc,
        out_grad,
        g_bias_out,
    )


def solution(mesh):
    ctx_size, fsdp_size = mesh.shape["ctx"], mesh.shape["fsdp"]
    if (ctx_size, fsdp_size) == (8, 4):
        links_of = PlaneLinks
    else:
        links_of = partial(PlainLinks, ctx_size, fsdp_size)
    rows = P("fsdp", "ctx", None)
    vector, matrix = P("fsdp"), P("fsdp", None)
    in_specs = (
        rows,
        P("fsdp", "ctx"),
        vector,
        vector,
        matrix,
        vector,
        matrix,
        vector,
        vector,
        vector,
        matrix,
        vector,
        matrix,
        vector,
        rows,
    )
    out_specs = (
        rows,
        rows,
        vector,
        vector,
        matrix,
        vector,
        matrix,
        vector,
        vector,
        vector,
        matrix,
        vector,
        matrix,
        vector,
    )
    return jax.shard_map(
        partial(body, links_of), mesh=mesh, in_specs=in_specs, out_specs=out_specs, check_vma=False
    )
```

time: 1250 us -> 547 us (0.44)
  waiting for transfers between devices: 656 us -> 128 us
  Pallas kernels: 0 us -> 236 us
  blocking collectives: 229 us -> 0 us
  local copies, waits for them, and re-layouts: 148 us -> 53.2 us
  loops' own time: 53.9 us -> 0 us
  starting transfers between devices: 1.57 us -> 43.6 us
  matrix products: 89.6 us -> 49.7 us
  between operations: 18.9 us -> 2.97 us
  other arithmetic: 36 us -> 22 us
    reduce_scatter x8 -> x0, waiting for transfers between devices: 270 us -> none  [the longest x2 97.4 us: reduce_grads(): lax.psum_scatter(grad_weight_fc.astype(jnp.bfloat16), 'fsdp', scatter_dim...]
    pallas_call x0 -> x9, Pallas kernels: none -> 236 us  [the longest x1 121 us: gather_weights(): pl.pallas_call(partial(gather_weights_kernel, count), in_specs=[anywhere]...]
    all_gather x12 -> x0, waiting for transfers between devices: 206 us -> none  [the longest x2 86.7 us: layer_forward(): lax.all_gather(key_flat, 'ctx', axis=1, tiled=True)]
    psum x1 -> x0, waiting for transfers between devices: 176 us -> none  [reduce_grads(): lax.psum((share_gain_one, share_bias_one, share_weight_qkv, share_bias_qv...]
    all_gather x7 -> x0, blocking collectives: 165 us -> none  [the longest x2 68.6 us: layer_backward(): lax.all_gather(row_delta, 'ctx', axis=2, tiled=True)]
    ppermute x0 -> x42, waiting for transfers between devices: none -> 128 us  [permute(): return lax.ppermute(value, ('ctx', 'fsdp'), pairs)]
    another operation x54 -> x0, loops' own time: 53.9 us -> none  [the longest x6 53 us: fold(): return lax.fori_loop(0, blocks, visit, running)]
    ppermute x0 -> x42, starting transfers between devices: none -> 43.6 us  [permute(): return lax.ppermute(value, ('ctx', 'fsdp'), pairs)]
  transfers between devices with their start and end apart: 21 -> 42, of which waited for: 14 -> 25; matrix products, arithmetic and copies ran while one was open for 20% -> 13% of each run, Pallas kernels for 0% -> 38%
where the time goes in v1:
time: 547 us; the launch traced here: 536 us
  Pallas kernels  236 us (43%)
  waiting for transfers between devices  128 us (23%)
  local copies, waits for them, and re-layouts  53.2 us (10%)
  matrix products  49.7 us (9%)
  starting transfers between devices  43.6 us (8%)
  other arithmetic  22 us (4%)
    ppermute x42, waiting for transfers between devices, permute(): return lax.ppermute(value, ('ctx', 'fsdp'), pairs)  128 us
    pallas_call x1, Pallas kernels, gather_weights(): pl.pallas_call(partial(gather_weights_kernel, count), in_specs=[anywhere]...  121 us
    pallas_call x4, Pallas kernels, gather_blocks(): pl.pallas_call(partial(gather_blocks_kernel, count), in_specs=[anywhere]...  75.5 us
    ppermute x42, starting transfers between devices, permute(): return lax.ppermute(value, ('ctx', 'fsdp'), pairs)  43.6 us
    unnamed x266, local copies, waits for them, and re-layouts  30.1 us
    pallas_call x2, Pallas kernels, attention_backward(): pl.pallas_call(attention_backward_kernel, grid=(PAIRS,), in_specs=[pl.Blo...  29.9 us
    dot_general x8, matrix products, dot_rows(): lax.dot_general(left, right, (((1,), (1,)), ((), ())), preferred_element_...  17 us
    dot_general x12, matrix products, term(): lax.dot_general(part, right, (((0,), (0,)), ((), ())), preferred_element_...  13.6 us
  transfers between devices with their start and end apart: 42, of which 25 were waited for; matrix products, arithmetic and copies ran while one was open for 13% of the time, Pallas kernels for 38%

profile of v1, /device:TPU:0, one launch (start us, length us, event | category | flops | bytes accessed | tf_op | source)
XLA Modules:
  0.0 536.2 jit_solution(818800474511484610)
XLA Ops:
  5.1 5.5 %concatenate.92 = bf16[2304]{0:T(1024)(128)(2,1)S(1)} concatenate(bf16[192]{0:T(256)(128)(2,1)} %param.17, bf16[192]{0:T(256)(128)(2,1)} %param.18, bf16[384]{0:T(512)(128)(2,1)} %param.20, bf16[192]{0:T(256)(128)(2,1)} %param.22, bf16[192]{0:T(256)(128)(2,1)} %param.23, bf16[192]{0:T(256)(128)(2,1)} %param.24, bf16[768]{0:T(1024)(128)(2,1)} %param.26, bf16[192]{0:T(256)(128)(2,1)} %param.28), dimensions={0} | concatenate | bytes 9216 | tf_op jit(solution)/shard_map/concatenate | solution.py:832
  11.2 120.9 %gather_weights.1 = (bf16[4,192,2304]{2,1,0:T(8,128)(2,1)}, bf16[4,64,256]{2,1,0:T(8,128)(2,1)}, bf16[4,192,768]{2,1,0:T(8,128)(2,1)}, bf16[4,192,3072]{2,1,0:T(8,128)(2,1)}, bf16[4,768,768]{2,1,0:T(8,128)(2,1)}) custom-call(bf16[192,2304]{1,0:T(8,128)(2,1)} %refs_0_.1, bf16[64,256]{1,0:T(8,128)(2,1)} %reshape.301.refs_1_, bf16[192,768]{1,0:T(8,128)(2,1)} %refs_2_.1, ...), custom_call_target="tpu_custom_call" | custom-call | tf_op jit(solution)/shard_map/gather_weights/pallas_call | solution.py:432
  136.0 2.7 fusion
  140.1 19.4 %gather_blocks.4 = (bf16[8,128,1536]{2,1,0:T(8,128)(2,1)}, s32[8,16,128]{2,1,0:T(8,128)}) custom-call(bf16[128,1536]{1,0:T(8,128)(2,1)} %slice.126.refs_0_.k_own_ref.v_own_ref, s32[16,128]{1,0:T(8,128)} %broadcast_in_dim.9.refs_1_), custom_call_target="tpu_custom_call" | custom-call | tf_op jit(solution)/shard_map/gather_blocks/pallas_call | solution.py:538
  160.3 1.9 copy-done.2
  162.2 5.0 attention_forward.2
  168.1 4.9 multiply_convert_fusion.1
  177.1 17.9 %gather_blocks.5 = bf16[8,128,1536]{2,1,0:T(8,128)(2,1)} custom-call(bf16[128,1536]{1,0:T(8,128)(2,1)} %slice.133.refs_0_.k_own_ref.v_own_ref), custom_call_target="tpu_custom_call" | custom-call | tf_op jit(solution)/shard_map/gather_blocks/pallas_call | solution.py:538
  196.9 4.9 attention_forward.3
  202.7 4.9 multiply_convert_fusion
  207.7 2.6 convert_reduce_fusion.1
  210.3 2.3 multiply_reduce_fusion.1
  216.9 18.6 %gather_blocks.6 = (bf16[8,128,768]{2,1,0:T(8,128)(2,1)}, bf16[8,128,768]{2,1,0:T(8,128)(2,1)}, f32[8,32,128]{2,1,0:T(8,128)}) custom-call(bf16[128,768]{1,0:T(8,128)(2,1)} %copy-done.12, bf16[128,768]{1,0:T(8,128)(2,1)} %copy-done.16, f32[32,128]{1,0:T(8,128)} %pad_maximum_fusion.38.refs_2_), custom_call_target="tpu_custom_call" | custom-call | tf_op jit(solution)/shard_map/gather_blocks/pallas_call | solution.py:538
  243.6 15.1 %attention_backward.2 = bf16[128,2304]{1,0:T(8,128)(2,1)S(1)} custom-call(s32[1]{0:T(128)} %bitcast.1.start_ref, bf16[128,768]{1,0:T(8,128)(2,1)S(1)} %copy-done.13, bf16[128,768]{1,0:T(8,128)(2,1)S(1)} %copy-done.17, bf16[128,1536]{1,0:T(8,128)(2,1)S(1)} %copy-done.8, bf16[128,1536]{1,0:T(8,128)(2,1)S(1)} %copy-done.8, f32[128,128]{1,0:T(8,128)S(1)} %copy-done.34, ...), custom_call_target="tpu_custom_call" | custom-call | flops 1610612736 | bytes 6291456 | tf_op jit(solution)/shard_map/attention_backward/pallas_call | solution.py:271
  258.8 1.9 multiply_reduce_fusion.2
  262.2 5.3 convert_reduce_fusion
  267.5 2.3 multiply_reduce_fusion
  278.0 3.0 collective-permute-start.2
  281.6 19.6 %gather_blocks.7 = (bf16[8,128,768]{2,1,0:T(8,128)(2,1)}, bf16[8,128,768]{2,1,0:T(8,128)(2,1)}, f32[8,32,128]{2,1,0:T(8,128)}) custom-call(bf16[128,768]{1,0:T(8,128)(2,1)} %copy-done.10, bf16[128,768]{1,0:T(8,128)(2,1)} %copy-done.14, f32[32,128]{1,0:T(8,128)} %pad_maximum_fusion.39.refs_2_), custom_call_target="tpu_custom_call" | custom-call | tf_op jit(solution)/shard_map/gather_blocks/pallas_call | solution.py:538
  309.3 14.7 %attention_backward.3 = bf16[128,2304]{1,0:T(8,128)(2,1)S(1)} custom-call(s32[1]{0:T(128)} %bitcast.1.start_ref, bf16[128,768]{1,0:T(8,128)(2,1)S(1)} %copy-done.11, bf16[128,768]{1,0:T(8,128)(2,1)S(1)} %copy-done.15, bf16[128,1536]{1,0:T(8,128)(2,1)S(1)} %copy-done.9, bf16[128,1536]{1,0:T(8,128)(2,1)S(1)} %copy-done.9, f32[128,128]{1,0:T(8,128)S(1)} %copy-done.32, ...), custom_call_target="tpu_custom_call" | custom-call | flops 1610612736 | bytes 6291456 | tf_op jit(solution)/shard_map/attention_backward/pallas_call | solution.py:271
  326.7 3.0 collective-permute-start.4
  337.5 4.0 reshape.324
  341.6 2.8 constant_dynamic-slice_fusion.1
  344.3 3.6 copy.44
  349.4 4.8 collective-permute-start.19
  354.2 1.9 convolution_convert_fusion.2
  357.9 4.9 collective-permute-done.6
  367.6 2.8 collective-permute-done.20
  372.9 2.0 collective-permute-done.21
  375.0 2.3 collective-permute-start.9
  383.6 3.7 collective-permute-done.23
  389.1 10.9 %collective-permute-done.11 = bf16[192,2304]{1,0:T(8,128)(2,1)S(1)} collective-permute-done((bf16[192,2304]{1,0:T(8,128)(2,1)S(1)}, bf16[192,2304]{1,0:T(8,128)(2,1)S(1)}, u32[]{:S(2)}, u32[]{:S(2)}) %collective-permute-start.11) | collective-permute-done | bytes 884768 | tf_op jit(solution)/shard_map/ppermute | solution.py:561
  405.1 6.7 %collective-permute-done.12 = bf16[96,2304]{1,0:T(8,128)(2,1)S(1)} collective-permute-done((bf16[96,2304]{1,0:T(8,128)(2,1)S(1)}, bf16[96,2304]{1,0:T(8,128)(2,1)S(1)}, u32[]{:S(2)}, u32[]{:S(2)}) %collective-permute-start.12) | collective-permute-done | bytes 442400 | tf_op jit(solution)/shard_map/ppermute | solution.py:561
  414.3 4.8 collective-permute-done.13
  419.2 2.4 collective-permute-start.14
  423.6 2.5 collective-permute-done.14
  429.5 3.6 collective-permute-done.15
  433.2 18.0 %collective-permute-done.27 = bf16[192,3072]{1,0:T(8,128)(2,1)S(1)} collective-permute-done((bf16[192,3072]{1,0:T(8,128)(2,1)S(1)}, bf16[192,3072]{1,0:T(8,128)(2,1)S(1)}, u32[]{:S(2)}, u32[]{:S(2)}) %collective-permute-start.27) | collective-permute-done | bytes 1179680 | tf_op jit(solution)/shard_map/ppermute | solution.py:561
  452.8 16.6 %collective-permute-done.35 = bf16[768,768]{1,0:T(8,128)(2,1)S(1)} collective-permute-done((bf16[768,768]{1,0:T(8,128)(2,1)S(1)}, bf16[768,768]{1,0:T(8,128)(2,1)S(1)}, u32[]{:S(2)}, u32[]{:S(2)}) %collective-permute-start.35) | collective-permute-done | bytes 1179680 | tf_op jit(solution)/shard_map/ppermute | solution.py:561
  472.8 10.2 %collective-permute-done.36 = bf16[384,768]{1,0:T(8,128)(2,1)S(1)} collective-permute-done((bf16[384,768]{1,0:T(8,128)(2,1)S(1)}, bf16[384,768]{1,0:T(8,128)(2,1)S(1)}, u32[]{:S(2)}, u32[]{:S(2)}) %collective-permute-start.36) | collective-permute-done | bytes 589856 | tf_op jit(solution)/shard_map/ppermute | solution.py:561
  483.3 4.5 collective-permute-done.17
  488.1 4.4 collective-permute-done.37
  493.0 5.9 %collective-permute-done.30 = bf16[24,3072]{1,0:T(8,128)(2,1)S(1)} collective-permute-done((bf16[24,3072]{1,0:T(8,128)(2,1)S(1)}, bf16[24,3072]{1,0:T(8,128)(2,1)S(1)}, u32[]{:S(2)}, u32[]{:S(2)}) %collective-permute-start.30) | collective-permute-done | bytes 147488 | tf_op jit(solution)/shard_map/ppermute | solution.py:561
  502.1 4.6 collective-permute-done.31
  506.8 2.6 collective-permute-done.39
  509.6 3.9 collective-permute-done.32
  517.9 6.8 %collective-permute-done.33 = bf16[96,3072]{1,0:T(8,128)(2,1)S(1)} collective-permute-done((bf16[96,3072]{1,0:T(8,128)(2,1)S(1)}, bf16[96,3072]{1,0:T(8,128)(2,1)S(1)}, u32[]{:S(2)}, u32[]{:S(2)}) %collective-permute-start.33) | collective-permute-done | bytes 589856 | tf_op jit(solution)/shard_map/ppermute | solution.py:561
  526.6 4.4 collective-permute-done.41
  (496 shorter events, 110.8 us)
Async XLA Ops:
  0.6 134.1 %collective-permute-start = (bf16[128,768]{1,0:T(8,128)(2,1)}, bf16[128,768]{1,0:T(8,128)(2,1)S(1)}, u32[]{:S(2)}, u32[]{:S(2)}) collective-permute-start(bf16[128,768]{1,0:T(8,128)(2,1)} %bitcast.186), channel_id=1, source_target_pairs={{0,0},{1,8},{2,16},{3,24},{4,4},{5,12},{6,20},{7,28},{8,1},{9,9},{... | collective-permute-start | bytes 589832 | tf_op jit(solution)/shard_map/ppermute | solution.py:561
  2.2 132.4 %collective-permute-start.1 = (s32[1,128]{1,0:T(1,128)}, s32[1,128]{1,0:T(1,128)S(1)}, u32[]{:S(2)}, u32[]{:S(2)}) collective-permute-start(s32[1,128]{1,0:T(1,128)} %param.16), channel_id=1, source_target_pairs={{0,0},{1,8},{2,16},{3,24},{4,4},{5,12},{6,20},{7,28},{8,1},{9,9},{... | collective-permute-start | bytes 1544 | tf_op jit(solution)/shard_map/ppermute | solution.py:561
  3.5 204.1 %collective-permute-start.3 = (bf16[128,768]{1,0:T(8,128)(2,1)}, bf16[128,768]{1,0:T(8,128)(2,1)S(1)}, u32[]{:S(2)}, u32[]{:S(2)}) collective-permute-start(bf16[128,768]{1,0:T(8,128)(2,1)} %bitcast.187), channel_id=1, source_target_pairs={{0,0},{1,8},{2,16},{3,24},{4,4},{5,12},{6,20},{7,28},{8,1},{9,9},{... | collective-permute-start | bytes 589832 | tf_op jit(solution)/shard_map/ppermute | solution.py:561
  133.6 39.5 %copy-start.93 = (f32[768]{0:T(1024)}, f32[768]{0:T(1024)S(1)}, u32[]{:S(2)}) copy-start(f32[768]{0:T(1024)S(1)} %add.475) | copy-start | bytes 9220
  133.8 40.5 %copy-start.88 = (f32[768]{0:T(1024)}, f32[768]{0:T(1024)S(1)}, u32[]{:S(2)}) copy-start(f32[768]{0:T(1024)S(1)} %mul.334) | copy-start | bytes 9220
  134.7 60.3 %copy-start.22 = (s32[128,1]{1,0:T(8,128)}, s32[128,1]{1,0:T(8,128)S(1)}, u32[]{:S(2)}) copy-start(s32[128,1]{1,0:T(8,128)S(1)} %copy.33.own_segs_ref) | copy-start | bytes 1540
  134.8 32.5 %copy-start.49 = (bf16[128,768]{1,0:T(8,128)(2,1)}, bf16[128,768]{1,0:T(8,128)(2,1)S(1)}, u32[]{:S(2)}) copy-start(bf16[128,768]{1,0:T(8,128)(2,1)S(1)} %collective-permute-done) | copy-start | bytes 589828
  138.7 28.6 %copy-start.10 = (bf16[128,768]{1,0:T(8,128)(2,1)}, bf16[128,768]{1,0:T(8,128)(2,1)S(1)}, u32[]{:S(2)}) copy-start(bf16[128,768]{1,0:T(8,128)(2,1)S(1)} %slice.125.q_ref.refs_0_) | copy-start | bytes 589828
  174.1 27.8 %copy-start.47 = (f32[128,768]{1,0:T(8,128)}, f32[128,768]{1,0:T(8,128)S(1)}, u32[]{:S(2)}) copy-start(f32[128,768]{1,0:T(8,128)S(1)} %get-tuple-element.129) | copy-start | bytes 1179652
  278.0 125.9 %collective-permute-start.2 = (bf16[128,768]{1,0:T(8,128)(2,1)}, bf16[128,768]{1,0:T(8,128)(2,1)}, u32[]{:S(2)}, u32[]{:S(2)}) collective-permute-start(bf16[128,768]{1,0:T(8,128)(2,1)} %fusion.26), channel_id=1, source_target_pairs={{0,0},{1,8},{2,16},{3,24},{4,4},{5,12},{6,20},{7,28},{8,1},{9,9},{... | collective-permute-start | bytes 589832 | tf_op jit(solution)/shard_map/ppermute | solution.py:561
  326.7 77.3 %collective-permute-start.4 = (bf16[128,768]{1,0:T(8,128)(2,1)}, bf16[128,768]{1,0:T(8,128)(2,1)}, u32[]{:S(2)}, u32[]{:S(2)}) collective-permute-start(bf16[128,768]{1,0:T(8,128)(2,1)} %fusion.43), channel_id=1, source_target_pairs={{0,0},{1,8},{2,16},{3,24},{4,4},{5,12},{6,20},{7,28},{8,1},{9,9},{... | collective-permute-start | bytes 589832 | tf_op jit(solution)/shard_map/ppermute | solution.py:561
  331.1 25.1 %collective-permute-start.5 = (f32[4,18,128]{2,1,0:T(8,128)}, f32[4,18,128]{2,1,0:T(8,128)}, u32[]{:S(2)}, u32[]{:S(2)}) collective-permute-start(f32[4,18,128]{2,1,0:T(8,128)} %reshape.313), channel_id=1, source_target_pairs={{0,1},{1,0},{2,3},{3,2},{4,5},{5,4},{6,7},{7,6},{8,9},{9,8},{10,11... | collective-permute-start | bytes 110600 | tf_op jit(solution)/shard_map/ppermute | solution.py:561
  333.9 14.1 %collective-permute-start.18 = (bf16[384,768]{1,0:T(8,128)(2,1)}, bf16[384,768]{1,0:T(8,128)(2,1)}, u32[]{:S(2)}, u32[]{:S(2)}) collective-permute-start(bf16[384,768]{1,0:T(8,128)(2,1)} %convolution_convert_fusion.3), channel_id=1, source_target_pairs={{0,1},{1,0},{2,3},{3,2},{4,5},{5,4},{6,7},{7,6},{8,9},{9,8},{10,11... | collective-permute-start | bytes 1769480 | tf_op jit(solution)/shard_map/ppermute | solution.py:561
  336.2 41.1 %collective-permute-start.10 = (bf16[384,2304]{1,0:T(8,128)(2,1)}, bf16[384,2304]{1,0:T(8,128)(2,1)}, u32[]{:S(2)}, u32[]{:S(2)}) collective-permute-start(bf16[384,2304]{1,0:T(8,128)(2,1)} %convolution_convert_fusion), channel_id=1, source_target_pairs={{0,1},{1,0},{2,3},{3,2},{4,5},{5,4},{6,7},{7,6},{8,9},{9,8},{10,11... | collective-permute-start | bytes 5308424 | tf_op jit(solution)/shard_map/ppermute | solution.py:561
  349.4 14.5 %collective-permute-start.19 = (bf16[192,768]{1,0:T(8,128)(2,1)S(1)}, bf16[192,768]{1,0:T(8,128)(2,1)S(1)}, u32[]{:S(2)}, u32[]{:S(2)}) collective-permute-start(bf16[192,768]{1,0:T(8,128)(2,1)S(1)} %fusion.27), channel_id=1, source_target_pairs={{0,2},{1,3},{2,0},{3,1},{4,6},{5,7},{6,4},{7,5},{8,10},{9,11},{10,... | collective-permute-start | bytes 884744 | tf_op jit(solution)/shard_map/ppermute | solution.py:561
  357.0 5.8 %collective-permute-start.6 = (f32[4,18,128]{2,1,0:T(8,128)S(1)}, f32[4,18,128]{2,1,0:T(8,128)S(1)}, u32[]{:S(2)}, u32[]{:S(2)}) collective-permute-start(f32[4,18,128]{2,1,0:T(8,128)S(1)} %add.509), channel_id=1, source_target_pairs={{0,2},{1,3},{2,0},{3,1},{4,6},{5,7},{6,4},{7,5},{8,10},{9,11},{10,... | collective-permute-start | bytes 110600 | tf_op jit(solution)/shard_map/ppermute | solution.py:561
  362.8 4.2 collective-permute-start.7
  365.3 5.2 collective-permute-start.20
  367.0 5.9 %collective-permute-start.8 = (f32[4,18,128]{2,1,0:T(8,128)S(1)}, f32[4,18,128]{2,1,0:T(8,128)S(1)}, u32[]{:S(2)}, u32[]{:S(2)}) collective-permute-start(f32[4,18,128]{2,1,0:T(8,128)S(1)} %add.511), channel_id=1, source_target_pairs={{0,8},{1,9},{2,10},{3,11},{4,12},{5,13},{6,14},{7,15},{8,0},{9,1},... | collective-permute-start | bytes 110600 | tf_op jit(solution)/shard_map/ppermute | solution.py:561
  370.5 4.4 collective-permute-start.21
  372.8 48.8 %collective-permute-start.26 = (bf16[384,3072]{1,0:T(8,128)(2,1)S(1)}, bf16[384,3072]{1,0:T(8,128)(2,1)S(1)}, u32[]{:S(2)}, u32[]{:S(2)}) collective-permute-start(bf16[384,3072]{1,0:T(8,128)(2,1)S(1)} %convolution_convert_fusion.1), channel_id=1, source_target_pairs={{0,1},{1,0},{2,3},{3,2},{4,5},{5,4},{6,7},{7,6},{8,9},{9,8},{10,11... | collective-permute-start | bytes 7077896 | tf_op jit(solution)/shard_map/ppermute | solution.py:561
  375.0 6.1 %collective-permute-start.9 = (f32[4,18,128]{2,1,0:T(8,128)S(1)}, f32[4,18,128]{2,1,0:T(8,128)S(1)}, u32[]{:S(2)}, u32[]{:S(2)}) collective-permute-start(f32[4,18,128]{2,1,0:T(8,128)S(1)} %add.512), channel_id=1, source_target_pairs={{0,16},{1,17},{2,18},{3,19},{4,20},{5,21},{6,22},{7,23},{8,24},{9,... | collective-permute-start | bytes 110600 | tf_op jit(solution)/shard_map/ppermute | solution.py:561
  377.3 5.0 collective-permute-start.22
  381.0 18.9 %collective-permute-start.11 = (bf16[192,2304]{1,0:T(8,128)(2,1)S(1)}, bf16[192,2304]{1,0:T(8,128)(2,1)S(1)}, u32[]{:S(2)}, u32[]{:S(2)}) collective-permute-start(bf16[192,2304]{1,0:T(8,128)(2,1)S(1)} %fusion.6), channel_id=1, source_target_pairs={{0,2},{1,3},{2,0},{3,1},{4,6},{5,7},{6,4},{7,5},{8,10},{9,11},{10,... | collective-permute-start | bytes 2654216 | tf_op jit(solution)/shard_map/ppermute | solution.py:561
  382.4 4.9 collective-permute-start.23
  387.3 16.7 %collective-permute-start.24 = (bf16[48,768]{1,0:T(8,128)(2,1)S(1)}, bf16[48,768]{1,0:T(8,128)(2,1)S(1)}, u32[]{:S(2)}, u32[]{:S(2)}) collective-permute-start(bf16[48,768]{1,0:T(8,128)(2,1)S(1)} %pad_maximum_fusion.37), channel_id=1, source_target_pairs={{0,8},{1,9},{2,10},{3,11},{4,12},{5,13},{6,14},{7,15},{8,0},{9,1},... | collective-permute-start | bytes 221192 | tf_op jit(solution)/shard_map/ppermute | solution.py:561
  401.6 10.2 %collective-permute-start.12 = (bf16[96,2304]{1,0:T(8,128)(2,1)S(1)}, bf16[96,2304]{1,0:T(8,128)(2,1)S(1)}, u32[]{:S(2)}, u32[]{:S(2)}) collective-permute-start(bf16[96,2304]{1,0:T(8,128)(2,1)S(1)} %dynamic-slice_convert_fusion.2), channel_id=1, source_target_pairs={{0,4},{1,5},{2,6},{3,7},{4,0},{5,1},{6,2},{7,3},{8,12},{9,13},{10,... | collective-permute-start | bytes 1327112 | tf_op jit(solution)/shard_map/ppermute | solution.py:561
  404.0 23.5 %collective-permute-start.34 = (bf16[1536,768]{1,0:T(8,128)(2,1)S(1)}, bf16[1536,768]{1,0:T(8,128)(2,1)S(1)}, u32[]{:S(2)}, u32[]{:S(2)}) collective-permute-start(bf16[1536,768]{1,0:T(8,128)(2,1)S(1)} %convolution_convert_fusion.2), channel_id=1, source_target_pairs={{0,1},{1,0},{2,3},{3,2},{4,5},{5,4},{6,7},{7,6},{8,9},{9,8},{10,11... | collective-permute-start | bytes 7077896 | tf_op jit(solution)/shard_map/ppermute | solution.py:561
  404.0 9.4 %collective-permute-start.25 = (bf16[96,768]{1,0:T(8,128)(2,1)S(1)}, bf16[96,768]{1,0:T(8,128)(2,1)S(1)}, u32[]{:S(2)}, u32[]{:S(2)}) collective-permute-start(bf16[96,768]{1,0:T(8,128)(2,1)S(1)} %pad_maximum_fusion.26), channel_id=1, source_target_pairs={{0,4},{1,5},{2,6},{3,7},{4,0},{5,1},{6,2},{7,3},{8,12},{9,13},{10,... | collective-permute-start | bytes 442376 | tf_op jit(solution)/shard_map/ppermute | solution.py:561
  412.0 7.2 %collective-permute-start.13 = (bf16[48,2304]{1,0:T(8,128)(2,1)S(1)}, bf16[48,2304]{1,0:T(8,128)(2,1)S(1)}, u32[]{:S(2)}, u32[]{:S(2)}) collective-permute-start(bf16[48,2304]{1,0:T(8,128)(2,1)S(1)} %dynamic-slice_convert_fusion.5), channel_id=1, source_target_pairs={{0,8},{1,9},{2,10},{3,11},{4,12},{5,13},{6,14},{7,15},{8,0},{9,1},... | collective-permute-start | bytes 663560 | tf_op jit(solution)/shard_map/ppermute | solution.py:561
  419.2 6.9 %collective-permute-start.14 = (bf16[24,2304]{1,0:T(8,128)(2,1)S(1)}, bf16[24,2304]{1,0:T(8,128)(2,1)S(1)}, u32[]{:S(2)}, u32[]{:S(2)}) collective-permute-start(bf16[24,2304]{1,0:T(8,128)(2,1)S(1)} %dynamic-slice_convert_fusion.9), channel_id=1, source_target_pairs={{0,16},{1,17},{2,18},{3,19},{4,20},{5,21},{6,22},{7,23},{8,24},{9,... | collective-permute-start | bytes 331784 | tf_op jit(solution)/shard_map/ppermute | solution.py:561
  422.1 29.0 %collective-permute-start.27 = (bf16[192,3072]{1,0:T(8,128)(2,1)S(1)}, bf16[192,3072]{1,0:T(8,128)(2,1)S(1)}, u32[]{:S(2)}, u32[]{:S(2)}) collective-permute-start(bf16[192,3072]{1,0:T(8,128)(2,1)S(1)} %fusion.4), channel_id=1, source_target_pairs={{0,2},{1,3},{2,0},{3,1},{4,6},{5,7},{6,4},{7,5},{8,10},{9,11},{10,... | collective-permute-start | bytes 3538952 | tf_op jit(solution)/shard_map/ppermute | solution.py:561
  426.1 6.9 %collective-permute-start.15 = (bf16[24,2304]{1,0:T(8,128)(2,1)S(1)}, bf16[24,2304]{1,0:T(8,128)(2,1)S(1)}, u32[]{:S(2)}, u32[]{:S(2)}) collective-permute-start(bf16[24,2304]{1,0:T(8,128)(2,1)S(1)} %add_convert_fusion.5), channel_id=1, source_target_pairs={{0,16},{1,17},{2,18},{3,19},{4,20},{5,21},{6,22},{7,23},{8,24},{9,... | collective-permute-start | bytes 331784 | tf_op jit(solution)/shard_map/ppermute | solution.py:561
  428.0 41.3 %collective-permute-start.35 = (bf16[768,768]{1,0:T(8,128)(2,1)S(1)}, bf16[768,768]{1,0:T(8,128)(2,1)S(1)}, u32[]{:S(2)}, u32[]{:S(2)}) collective-permute-start(bf16[768,768]{1,0:T(8,128)(2,1)S(1)} %fusion.2), channel_id=1, source_target_pairs={{0,2},{1,3},{2,0},{3,1},{4,6},{5,7},{6,4},{7,5},{8,10},{9,11},{10,... | collective-permute-start | bytes 3538952 | tf_op jit(solution)/shard_map/ppermute | solution.py:561
  433.1 37.9 %collective-permute-start.16 = (bf16[48,2304]{1,0:T(8,128)(2,1)S(1)}, bf16[48,2304]{1,0:T(8,128)(2,1)S(1)}, u32[]{:S(2)}, u32[]{:S(2)}) collective-permute-start(bf16[48,2304]{1,0:T(8,128)(2,1)S(1)} %pad_maximum_fusion.25), channel_id=1, source_target_pairs={{0,8},{1,9},{2,10},{3,11},{4,12},{5,13},{6,14},{7,15},{8,0},{9,1},... | collective-permute-start | bytes 663560 | tf_op jit(solution)/shard_map/ppermute | solution.py:561
  451.7 20.5 %collective-permute-start.28 = (bf16[96,3072]{1,0:T(8,128)(2,1)S(1)}, bf16[96,3072]{1,0:T(8,128)(2,1)S(1)}, u32[]{:S(2)}, u32[]{:S(2)}) collective-permute-start(bf16[96,3072]{1,0:T(8,128)(2,1)S(1)} %dynamic-slice_convert_fusion.1), channel_id=1, source_target_pairs={{0,4},{1,5},{2,6},{3,7},{4,0},{5,1},{6,2},{7,3},{8,12},{9,13},{10,... | collective-permute-start | bytes 1769480 | tf_op jit(solution)/shard_map/ppermute | solution.py:561
  469.9 13.1 %collective-permute-start.36 = (bf16[384,768]{1,0:T(8,128)(2,1)S(1)}, bf16[384,768]{1,0:T(8,128)(2,1)S(1)}, u32[]{:S(2)}, u32[]{:S(2)}) collective-permute-start(bf16[384,768]{1,0:T(8,128)(2,1)S(1)} %dynamic-slice_convert_fusion), channel_id=1, source_target_pairs={{0,4},{1,5},{2,6},{3,7},{4,0},{5,1},{6,2},{7,3},{8,12},{9,13},{10,... | collective-permute-start | bytes 1769480 | tf_op jit(solution)/shard_map/ppermute | solution.py:561
  471.1 16.6 %collective-permute-start.17 = (bf16[96,2304]{1,0:T(8,128)(2,1)S(1)}, bf16[96,2304]{1,0:T(8,128)(2,1)S(1)}, u32[]{:S(2)}, u32[]{:S(2)}) collective-permute-start(bf16[96,2304]{1,0:T(8,128)(2,1)S(1)} %pad_maximum_fusion.10), channel_id=1, source_target_pairs={{0,4},{1,5},{2,6},{3,7},{4,0},{5,1},{6,2},{7,3},{8,12},{9,13},{10,... | collective-permute-start | bytes 1327112 | tf_op jit(solution)/shard_map/ppermute | solution.py:561
  472.4 15.5 %collective-permute-start.29 = (bf16[48,3072]{1,0:T(8,128)(2,1)S(1)}, bf16[48,3072]{1,0:T(8,128)(2,1)S(1)}, u32[]{:S(2)}, u32[]{:S(2)}) collective-permute-start(bf16[48,3072]{1,0:T(8,128)(2,1)S(1)} %dynamic-slice_convert_fusion.4), channel_id=1, source_target_pairs={{0,8},{1,9},{2,10},{3,11},{4,12},{5,13},{6,14},{7,15},{8,0},{9,1},... | collective-permute-start | bytes 884744 | tf_op jit(solution)/shard_map/ppermute | solution.py:561
  483.2 9.4 %collective-permute-start.37 = (bf16[192,768]{1,0:T(8,128)(2,1)S(1)}, bf16[192,768]{1,0:T(8,128)(2,1)S(1)}, u32[]{:S(2)}, u32[]{:S(2)}) collective-permute-start(bf16[192,768]{1,0:T(8,128)(2,1)S(1)} %dynamic-slice_convert_fusion.3), channel_id=1, source_target_pairs={{0,8},{1,9},{2,10},{3,11},{4,12},{5,13},{6,14},{7,15},{8,0},{9,1},... | collective-permute-start | bytes 884744 | tf_op jit(solution)/shard_map/ppermute | solution.py:561
  488.0 11.0 %collective-permute-start.30 = (bf16[24,3072]{1,0:T(8,128)(2,1)S(1)}, bf16[24,3072]{1,0:T(8,128)(2,1)S(1)}, u32[]{:S(2)}, u32[]{:S(2)}) collective-permute-start(bf16[24,3072]{1,0:T(8,128)(2,1)S(1)} %dynamic-slice_convert_fusion.7), channel_id=1, source_target_pairs={{0,16},{1,17},{2,18},{3,19},{4,20},{5,21},{6,22},{7,23},{8,24},{9,... | collective-permute-start | bytes 442376 | tf_op jit(solution)/shard_map/ppermute | solution.py:561
  492.7 8.3 %collective-permute-start.38 = (bf16[96,768]{1,0:T(8,128)(2,1)S(1)}, bf16[96,768]{1,0:T(8,128)(2,1)S(1)}, u32[]{:S(2)}, u32[]{:S(2)}) collective-permute-start(bf16[96,768]{1,0:T(8,128)(2,1)S(1)} %dynamic-slice_convert_fusion.6), channel_id=1, source_target_pairs={{0,16},{1,17},{2,18},{3,19},{4,20},{5,21},{6,22},{7,23},{8,24},{9,... | collective-permute-start | bytes 442376 | tf_op jit(solution)/shard_map/ppermute | solution.py:561
  499.0 7.7 %collective-permute-start.31 = (bf16[24,3072]{1,0:T(8,128)(2,1)S(1)}, bf16[24,3072]{1,0:T(8,128)(2,1)S(1)}, u32[]{:S(2)}, u32[]{:S(2)}) collective-permute-start(bf16[24,3072]{1,0:T(8,128)(2,1)S(1)} %add_convert_fusion.4), channel_id=1, source_target_pairs={{0,16},{1,17},{2,18},{3,19},{4,20},{5,21},{6,22},{7,23},{8,24},{9,... | collective-permute-start | bytes 442376 | tf_op jit(solution)/shard_map/ppermute | solution.py:561
  501.0 8.5 %collective-permute-start.39 = (bf16[96,768]{1,0:T(8,128)(2,1)S(1)}, bf16[96,768]{1,0:T(8,128)(2,1)S(1)}, u32[]{:S(2)}, u32[]{:S(2)}) collective-permute-start(bf16[96,768]{1,0:T(8,128)(2,1)S(1)} %add_convert_fusion.3), channel_id=1, source_target_pairs={{0,16},{1,17},{2,18},{3,19},{4,20},{5,21},{6,22},{7,23},{8,24},{9,... | collective-permute-start | bytes 442376 | tf_op jit(solution)/shard_map/ppermute | solution.py:561
  506.8 6.8 %collective-permute-start.32 = (bf16[48,3072]{1,0:T(8,128)(2,1)S(1)}, bf16[48,3072]{1,0:T(8,128)(2,1)S(1)}, u32[]{:S(2)}, u32[]{:S(2)}) collective-permute-start(bf16[48,3072]{1,0:T(8,128)(2,1)S(1)} %pad_maximum_fusion.23), channel_id=1, source_target_pairs={{0,8},{1,9},{2,10},{3,11},{4,12},{5,13},{6,14},{7,15},{8,0},{9,1},... | collective-permute-start | bytes 884744 | tf_op jit(solution)/shard_map/ppermute | solution.py:561
  509.5 7.2 %collective-permute-start.40 = (bf16[192,768]{1,0:T(8,128)(2,1)S(1)}, bf16[192,768]{1,0:T(8,128)(2,1)S(1)}, u32[]{:S(2)}, u32[]{:S(2)}) collective-permute-start(bf16[192,768]{1,0:T(8,128)(2,1)S(1)} %pad_maximum_fusion.24), channel_id=1, source_target_pairs={{0,8},{1,9},{2,10},{3,11},{4,12},{5,13},{6,14},{7,15},{8,0},{9,1},... | collective-permute-start | bytes 884744 | tf_op jit(solution)/shard_map/ppermute | solution.py:561
  513.7 11.0 %collective-permute-start.33 = (bf16[96,3072]{1,0:T(8,128)(2,1)S(1)}, bf16[96,3072]{1,0:T(8,128)(2,1)S(1)}, u32[]{:S(2)}, u32[]{:S(2)}) collective-permute-start(bf16[96,3072]{1,0:T(8,128)(2,1)S(1)} %pad_maximum_fusion.3), channel_id=1, source_target_pairs={{0,4},{1,5},{2,6},{3,7},{4,0},{5,1},{6,2},{7,3},{8,12},{9,13},{10,... | collective-permute-start | bytes 1769480 | tf_op jit(solution)/shard_map/ppermute | solution.py:561
  516.9 14.1 %collective-permute-start.41 = (bf16[384,768]{1,0:T(8,128)(2,1)S(1)}, bf16[384,768]{1,0:T(8,128)(2,1)S(1)}, u32[]{:S(2)}, u32[]{:S(2)}) collective-permute-start(bf16[384,768]{1,0:T(8,128)(2,1)S(1)} %pad_maximum_fusion.4), channel_id=1, source_target_pairs={{0,4},{1,5},{2,6},{3,7},{4,0},{5,1},{6,2},{7,3},{8,12},{9,13},{10,... | collective-permute-start | bytes 1769480 | tf_op jit(solution)/shard_map/ppermute | solution.py:561
  (125 other events, 696.9 us)

commit v2 on v1

--- a/solution.py
+++ b/solution.py
@@ -53,6 +53,10 @@
 
 def dot_rows(left, right):
     return lax.dot_general(left, right, (((1,), (1,)), ((), ())), preferred_element_type=F32)
+
+
+def column_products(left, right):
+    return lax.dot_general(left, right, (((0,), (0,)), ((), ())), preferred_element_type=F32)
 
 
 def pick_lanes(columns, pair):
@@ -332,7 +336,8 @@
 
 def gather_weights_kernel(count, *refs):
     shares, fulls = refs[:count], refs[count : 2 * count]
-    send_sems, recv_sems, local_sems = refs[2 * count :]
+    send_sems, recv_sems, local_sems = refs[2 * count : 2 * count + 3]
+    stages = refs[2 * count + 3 :]
     x, z, y, core = place_bits()
     low = lax.rem(z, 2)
     z_next = z + 1 - 2 * low
@@ -391,9 +396,17 @@
         plans.append(plan)
         plan[0].start()
         plan[10].start()
-        local = pltpu.make_async_copy(share, full.at[own], local_sems.at[which])
-        local.start()
-        locals_started.append(local)
+        pltpu.make_async_copy(share, stages[which], local_sems.at[which]).start()
+        locals_started.append(
+            (
+                pltpu.make_async_copy(share, stages[which], local_sems.at[which]),
+                pltpu.make_async_copy(stages[which], full.at[own], local_sems.at[which]),
+            )
+        )
+
+    for into, out in locals_started:
+        into.wait()
+        out.start()
 
     for step in range(count + 2):
         if step < count:
@@ -421,8 +434,8 @@
             plan[index].wait_recv()
         for index in range(WEIGHT_COPIES):
             plan[index].wait_send()
-    for local in locals_started:
-        local.wait()
+    for _, out in locals_started:
+        out.wait()
 
 
 def gather_weights(shares, collective_id):
@@ -438,7 +451,8 @@
             pltpu.SemaphoreType.DMA((copies,)),
             pltpu.SemaphoreType.DMA((copies,)),
             pltpu.SemaphoreType.DMA((count,)),
-        ],
+        ]
+        + [pltpu.VMEM(share.shape, share.dtype) for share in shares],
         compiler_params=pltpu.CompilerParams(collective_id=collective_id, has_side_effects=True),
         name="gather_weights",
     )(*shares)
@@ -537,7 +551,7 @@
     anywhere = pl.BlockSpec(memory_space=pl.ANY)
     return pl.pallas_call(
         partial(gather_blocks_kernel, count),
-        in_specs=[anywhere] * count,
+        in_specs=[pl.BlockSpec(memory_space=pltpu.VMEM)] * count,
         out_specs=[anywhere] * count,
         out_shape=[jax.ShapeDtypeStruct((8, *block.shape), block.dtype) for block in blocks],
         scratch_shapes=[
@@ -550,6 +564,285 @@
     )(*blocks)
 
 
+CHUNK_ROWS, CHUNK_COLUMNS = 192, 768
+REDUCE_COPIES = 9
+VECTOR_AXES = 5
+
+
+def chunk_places(shapes):
+    return [
+        (which, row, column)
+        for which, (rows, columns) in enumerate(shapes)
+        for row in range(0, rows, CHUNK_ROWS)
+        for column in range(0, columns, CHUNK_COLUMNS)
+    ]
+
+
+def reduce_gradients_kernel(places, count, *refs):
+    partials, vector = refs[:count], refs[count]
+    sums, vector_out = refs[count + 1 : 2 * count + 1], refs[2 * count + 1]
+    (
+        own,
+        got_core,
+        got_y,
+        to_x,
+        got_x,
+        to_z,
+        got_z,
+        to_zz,
+        got_zz,
+        vector_got,
+        send_sems,
+        recv_sems,
+        local_sems,
+    ) = refs[2 * count + 2 :]
+    x, z, y, core = place_bits()
+    low, high = lax.rem(z, 2), z // 2
+    fsdp = 2 * y + core
+    sibling = (2 * z + x, 2 * y + 1 - core)
+    over_y = (2 * z + x, 2 * (1 - y) + core)
+    over_x = (2 * z + 1 - x, fsdp)
+    over_z = (2 * (z + 1 - 2 * low) + x, fsdp)
+    over_zz = (2 * (z + 2 - 4 * high) + x, fsdp)
+    greet((sibling, over_y, over_x, over_z, over_zz))
+
+    def copy(slot, src, dst, device):
+        return pltpu.make_async_remote_copy(
+            src_ref=src,
+            dst_ref=dst,
+            send_sem=send_sems.at[slot],
+            recv_sem=recv_sems.at[slot],
+            device_id=device,
+            device_id_type=MESH,
+        )
+
+    x_rows, z_rows, zz_columns = CHUNK_ROWS // 2, CHUNK_ROWS // 4, CHUNK_COLUMNS // 2
+    chunks = len(places)
+
+    def add_up(store, loads, rows):
+        step = z_rows
+
+        def visit(index, carried):
+            offset = pl.multiple_of(index * step, 16)
+            total = loads[0](offset, step).astype(F32)
+            for load in loads[1:]:
+                total = total + load(offset, step).astype(F32)
+            store(offset, step, total.astype(BF16))
+            return carried
+
+        if rows == step:
+            visit(0, 0)
+        else:
+            lax.fori_loop(0, rows // step, visit, 0)
+
+    vector_devices = (over_y, sibling, over_x, over_z, over_zz)
+    vector_copies = [
+        copy(chunks * REDUCE_COPIES + i, vector_out, vector_got.at[i], vector_devices[i])
+        for i in range(VECTOR_AXES)
+    ]
+    vector_out[...] = vector[...]
+    vector_copies[0].start()
+
+    plans = []
+    loads = []
+    for k, (which, row, column) in enumerate(places):
+        partial_sum, out = partials[which], sums[which]
+
+        def term(quarter, partial_sum=partial_sum, row=row, column=column):
+            return partial_sum.at[quarter, pl.ds(row, CHUNK_ROWS), pl.ds(column, CHUNK_COLUMNS)]
+
+        def piece(first, rows, start, width, out=out, row=row, column=column):
+            return out.at[
+                pl.ds(pl.multiple_of(row + first, 16), rows),
+                pl.ds(pl.multiple_of(column + start, LANES), width),
+            ]
+
+        final = piece(x * x_rows + low * z_rows, z_rows, high * zz_columns, zz_columns)
+        wide = piece(x * x_rows + low * z_rows, z_rows, 0, CHUNK_COLUMNS)
+        tall = piece(x * x_rows, x_rows, 0, CHUNK_COLUMNS)
+        base = k * REDUCE_COPIES
+        plans.append(
+            {
+                "core0": copy(base, term(1 - core), got_core.at[k, 0], sibling),
+                "core1": copy(base + 1, term(3 - core), got_core.at[k, 1], sibling),
+                "y": copy(base + 2, own.at[k, 1 - y], got_y.at[k], over_y),
+                "x": copy(base + 3, to_x.at[k], got_x.at[k], over_x),
+                "z": copy(base + 4, to_z.at[k], got_z.at[k], over_z),
+                "zz": copy(base + 5, to_zz.at[k], got_zz.at[k], over_zz),
+                "zz_back": copy(base + 6, final, final, over_zz),
+                "z_back": copy(base + 7, wide, wide, over_z),
+                "x_back": copy(base + 8, tall, tall, over_x),
+                "final": final,
+            }
+        )
+        loads.append(
+            [
+                pltpu.make_async_copy(term(2 * i + core), own.at[k, i], local_sems.at[2 * k + i])
+                for i in range(2)
+            ]
+        )
+        plans[k]["core0"].start()
+        plans[k]["core1"].start()
+        loads[k][0].start()
+        loads[k][1].start()
+
+    def slab(ref, *index, first=0, start=None, width=None):
+        def load(offset, rows):
+            place = pl.ds(pl.multiple_of(first + offset, 16), rows)
+            if width is None:
+                return ref[(*index, place)]
+            return ref[(*index, place, pl.ds(pl.multiple_of(start, LANES), width))]
+
+        return load
+
+    def stage_y(k):
+        plan = plans[k]
+        for load in loads[k]:
+            load.wait()
+        plan["core0"].wait_recv()
+        plan["core1"].wait_recv()
+
+        def store(offset, rows, value):
+            own[k, 1 - y, pl.ds(offset, rows)] = value
+
+        add_up(store, [slab(own, k, 1 - y), slab(got_core, k, 1 - y)], CHUNK_ROWS)
+        plan["y"].start()
+
+    def stage_x(k):
+        plan = plans[k]
+        plan["y"].wait_recv()
+        first = (1 - x) * x_rows
+
+        def store(offset, rows, value):
+            to_x[k, pl.ds(offset, rows)] = value
+
+        add_up(
+            store,
+            [slab(own, k, y, first=first), slab(got_core, k, y, first=first), slab(got_y, k, first=first)],
+            x_rows,
+        )
+        plan["x"].start()
+
+    def stage_z(k):
+        plan = plans[k]
+        plan["x"].wait_recv()
+        inner = (1 - low) * z_rows
+        first = x * x_rows + inner
+
+        def store(offset, rows, value):
+            to_z[k] = value
+
+        add_up(
+            store,
+            [
+                slab(own, k, y, first=first),
+                slab(got_core, k, y, first=first),
+                slab(got_y, k, first=first),
+                slab(got_x, k, first=inner),
+            ],
+            z_rows,
+        )
+        plan["z"].start()
+
+    def last_loads(k, start):
+        inner = low * z_rows
+        first = x * x_rows + inner
+        part = {"start": start, "width": zz_columns}
+        return [
+            slab(own, k, y, first=first, **part),
+            slab(got_core, k, y, first=first, **part),
+            slab(got_y, k, first=first, **part),
+            slab(got_x, k, first=inner, **part),
+            slab(got_z, k, **part),
+        ]
+
+    def stage_zz(k):
+        plan = plans[k]
+        plan["z"].wait_recv()
+
+        def store(offset, rows, value):
+            to_zz[k] = value
+
+        add_up(store, last_loads(k, (1 - high) * zz_columns), z_rows)
+        plan["zz"].start()
+
+    def stage_final(k):
+        plan = plans[k]
+        plan["zz"].wait_recv()
+
+        def store(offset, rows, value):
+            plan["final"][...] = value
+
+        add_up(store, last_loads(k, high * zz_columns) + [slab(got_zz, k)], z_rows)
+        plan["zz_back"].start()
+
+    def stage_z_back(k):
+        plans[k]["zz_back"].wait_recv()
+        plans[k]["z_back"].start()
+
+    def stage_x_back(k):
+        plans[k]["z_back"].wait_recv()
+        plans[k]["x_back"].start()
+
+    def vector_step(index):
+        vector_copies[index].wait()
+        vector_out[...] = vector_out[...] + vector_got[index]
+        if index + 1 < VECTOR_AXES:
+            vector_copies[index + 1].start()
+
+    for k in range(chunks):
+        stage_y(k)
+    stages = (stage_x, stage_z, stage_zz, stage_final, stage_z_back, stage_x_back)
+    for tick in range(chunks + len(stages) - 1):
+        if tick < VECTOR_AXES:
+            vector_step(tick)
+        for lag, stage in enumerate(stages):
+            if 0 <= tick - lag < chunks:
+                stage(tick - lag)
+    for plan in plans:
+        plan["x_back"].wait_recv()
+        for name in ("core0", "core1", "y", "x", "z", "zz", "zz_back", "z_back", "x_back"):
+            plan[name].wait_send()
+
+
+def reduce_gradients(partials, vector, collective_id):
+    count = len(partials)
+    places = chunk_places([partial_sum.shape[1:] for partial_sum in partials])
+    chunks = len(places)
+    slots = chunks * REDUCE_COPIES + VECTOR_AXES
+    rows, columns = CHUNK_ROWS, CHUNK_COLUMNS
+    buffers = [
+        (2, rows, columns),
+        (2, rows, columns),
+        (rows, columns),
+        (rows // 2, columns),
+        (rows // 2, columns),
+        (rows // 4, columns),
+        (rows // 4, columns),
+        (rows // 4, columns // 2),
+        (rows // 4, columns // 2),
+    ]
+    vmem = pl.BlockSpec(memory_space=pltpu.VMEM)
+    return pl.pallas_call(
+        partial(reduce_gradients_kernel, places, count),
+        in_specs=[pl.BlockSpec(memory_space=pl.ANY)] * count + [vmem],
+        out_specs=[vmem] * (count + 1),
+        out_shape=[jax.ShapeDtypeStruct(p.shape[1:], BF16) for p in partials]
+        + [jax.ShapeDtypeStruct(vector.shape, F32)],
+        scratch_shapes=[pltpu.VMEM((chunks, *shape), BF16) for shape in buffers]
+        + [
+            pltpu.VMEM((VECTOR_AXES, *vector.shape), F32),
+            pltpu.SemaphoreType.DMA((slots,)),
+            pltpu.SemaphoreType.DMA((slots,)),
+            pltpu.SemaphoreType.DMA((2 * chunks,)),
+        ],
+        compiler_params=pltpu.CompilerParams(
+            collective_id=collective_id, has_side_effects=True, vmem_limit_bytes=48 << 20
+        ),
+        name="reduce_gradients",
+    )(*partials, vector)
+
+
 class PlaneLinks:
     def __init__(self):
         self.x, self.z, self.y, self.core = place_bits()
@@ -566,64 +859,21 @@
     enter = swap
     leave = swap
 
-    def across(self, value, axis):
-        target = {
-            "core": lambda c, f: c * 4 + (f ^ 1),
-            "y": lambda c, f: c * 4 + (f ^ 2),
-            "x": lambda c, f: (c ^ 1) * 4 + f,
-            "z": lambda c, f: (c ^ 2) * 4 + f,
-            "zz": lambda c, f: (c ^ 4) * 4 + f,
-        }[axis]
-        return self.permute(value, target)
-
     def weights(self, shares):
         return gather_weights(shares, 0)
 
     def blocks(self, blocks, collective_id):
         return gather_blocks(blocks, collective_id)
 
-    def halve(self, total, bit, axis):
-        rows = total.shape[0] // 2
-        sent = lax.dynamic_slice_in_dim(total, (1 - bit) * rows, rows, 0).astype(BF16)
-        kept = lax.dynamic_slice_in_dim(total, bit * rows, rows, 0)
-        return kept + self.across(sent, axis).astype(F32)
-
-    def double(self, rows, bit, axis):
-        got = self.across(rows, axis)
-        low = jnp.where(bit == 0, rows, got)
-        high = jnp.where(bit == 0, got, rows)
-        return jnp.concatenate([low, high], axis=0)
-
-    def weight_sum(self, left, right):
-        tokens, rows = left.shape
-        quarter = rows // 4
-        columns = left.reshape(tokens, 2, 2, quarter)
-
-        def term(part):
-            return lax.dot_general(
-                part, right, (((0,), (0,)), ((), ())), preferred_element_type=F32
-            )
-
-        pick = lambda array, index, axis: lax.dynamic_index_in_dim(array, index, axis, keepdims=False)
-        sent = term(pick(columns, 1 - self.core, 2).reshape(tokens, 2 * quarter)).astype(BF16)
-        got = self.across(sent, "core").reshape(2, quarter, right.shape[1])
-        mine = pick(columns, self.core, 2)
-        sent = (term(pick(mine, 1 - self.y, 1)) + pick(got, 1 - self.y, 0).astype(F32)).astype(BF16)
-        got_y = self.across(sent, "y")
-        kept = term(pick(mine, self.y, 1)) + pick(got, self.y, 0).astype(F32)
-        total = kept + got_y.astype(F32)
-        low, high = lax.rem(self.z, 2), self.z // 2
-        total = self.halve(total, self.x, "x")
-        total = self.halve(total, low, "z")
-        total = self.halve(total, high, "zz").astype(BF16)
-        total = self.double(total, high, "zz")
-        total = self.double(total, low, "z")
-        return self.double(total, self.x, "x").astype(F32)
-
-    def vector_sum(self, packed):
-        for axis in ("core", "y", "x", "z", "zz"):
-            packed = packed + self.across(packed, axis)
-        return lax.dynamic_index_in_dim(packed, 2 * self.y + self.core, 0, keepdims=False)
+    def sum_gradients(self, factors, packed):
+        terms = []
+        for left, right in factors:
+            term = column_products(left, right).astype(BF16)
+            terms.append(term.reshape(4, term.shape[0] // 4, term.shape[1]))
+        *sums, vector = reduce_gradients(terms, packed.reshape(-1, LANES), 4)
+        vector = vector.reshape(packed.shape)
+        mine = lax.dynamic_index_in_dim(vector, 2 * self.y + self.core, 0, keepdims=False)
+        return [total.astype(F32) for total in sums], mine
 
 
 class PlainLinks:
@@ -643,14 +893,14 @@
     def blocks(self, blocks, collective_id):
         return [lax.all_gather(block, "ctx", axis=0) for block in blocks]
 
-    def weight_sum(self, left, right):
-        term = lax.dot_general(left, right, (((0,), (0,)), ((), ())), preferred_element_type=F32)
-        share = lax.psum_scatter(term.astype(BF16), "fsdp", scatter_dimension=0, tiled=True)
-        return lax.psum(share.astype(F32), "ctx")
-
-    def vector_sum(self, packed):
+    def sum_gradients(self, factors, packed):
+        sums = []
+        for left, right in factors:
+            term = column_products(left, right).astype(BF16)
+            share = lax.psum_scatter(term, "fsdp", scatter_dimension=0, tiled=True)
+            sums.append(lax.psum(share.astype(F32), "ctx"))
         share = lax.psum_scatter(packed, "fsdp", scatter_dimension=0, tiled=False)
-        return lax.psum(share, "ctx")
+        return sums, lax.psum(share, "ctx")
 
 
 def layer_forward(resid, weights, links, start, own_segs, segs, layer_index):
@@ -875,16 +1125,17 @@
         collected.append((matrices, terms))
     tokens_grad = links.leave(gradient.astype(BF16))
 
-    sums = []
+    factors = []
     for second, first in zip(collected[0][0], collected[1][0]):
         left = jnp.concatenate([second[0], first[0]], axis=0)
         right = jnp.concatenate([second[1], first[1]], axis=0)
-        sums.append(links.weight_sum(left, right))
-    out_grad, fc_grad, proj_grad, qkv_grad = sums
+        factors.append((left, right))
     shares = packed.shape[0]
     added = [a + b for a, b in zip(collected[0][1], collected[1][1])]
     rows = jnp.concatenate([vector.reshape(shares, -1) for vector in added], axis=1)
-    summed = links.vector_sum(rows.reshape(shares, -1, LANES)).reshape(-1)
+    sums, summed = links.sum_gradients(factors, rows.reshape(shares, -1, LANES))
+    out_grad, fc_grad, proj_grad, qkv_grad = sums
+    summed = summed.reshape(-1)
     small = []
     offset = 0
     for size in sizes:

time: 547 us -> 405 us (0.74); the launches traced: 536 us -> 404 us
  waiting for transfers between devices: 128 us -> 0.01 us
  Pallas kernels: 236 us -> 283 us
  starting transfers between devices: 43.6 us -> 10.6 us
  local copies, waits for them, and re-layouts: 53.2 us -> 42.7 us
  other arithmetic: 22 us -> 15.2 us
    ppermute x42 -> x5, waiting for transfers between devices: 128 us -> 0.01 us  [permute(): return lax.ppermute(value, ('ctx', 'fsdp'), pairs)]
    pallas_call x4 -> x5, Pallas kernels: 75.5 us -> 189 us  [the longest x1 112 us: reduce_gradients(): pl.pallas_call(partial(reduce_gradients_kernel, places, count), in_specs=...]
    pallas_call x1, Pallas kernels: 121 us -> 54.7 us  [gather_weights(): pl.pallas_call(partial(gather_weights_kernel, count), in_specs=[anywhere]...]
    ppermute x42 -> x5, starting transfers between devices: 43.6 us -> 10.6 us  [permute(): return lax.ppermute(value, ('ctx', 'fsdp'), pairs)]
    unnamed x266 -> x231, local copies, waits for them, and re-layouts: 30.1 us -> 26.8 us
    dot_general x12 -> x4, matrix products: 13.6 us -> 11.6 us  [column_products(): lax.dot_general(left, right, (((0,), (0,)), ((), ())), preferred_element_...]
  transfers between devices with their start and end apart: 42 -> 5, of which waited for: 25 -> 0; matrix products, arithmetic and copies ran while one was open for 13% -> 11% of each run, Pallas kernels for 38% -> 53%
where the time goes in v2:
time: 405 us; the launch traced here: 404 us
  Pallas kernels  283 us (70%)
  matrix products  49.9 us (12%)
  local copies, waits for them, and re-layouts  42.7 us (11%)
  other arithmetic  15.2 us (4%)
  starting transfers between devices  10.6 us (3%)
    pallas_call x1, Pallas kernels, reduce_gradients(): pl.pallas_call(partial(reduce_gradients_kernel, places, count), in_specs=...  112 us
    pallas_call x4, Pallas kernels, gather_blocks(): pl.pallas_call(partial(gather_blocks_kernel, count), in_specs=[pl.BlockSp...  77.8 us
    pallas_call x1, Pallas kernels, gather_weights(): pl.pallas_call(partial(gather_weights_kernel, count), in_specs=[anywhere]...  54.7 us
    pallas_call x2, Pallas kernels, attention_backward(): pl.pallas_call(attention_backward_kernel, grid=(PAIRS,), in_specs=[pl.Blo...  29.7 us
    unnamed x231, local copies, waits for them, and re-layouts  26.8 us
    dot_general x8, matrix products, dot_rows(): lax.dot_general(left, right, (((1,), (1,)), ((), ())), preferred_element_...  16.9 us
    dot_general x4, matrix products, column_products(): lax.dot_general(left, right, (((0,), (0,)), ((), ())), preferred_element_...  11.6 us
    ppermute x5, starting transfers between devices, permute(): return lax.ppermute(value, ('ctx', 'fsdp'), pairs)  10.6 us
  transfers between devices with their start and end apart: 5, of which 0 were waited for; matrix products, arithmetic and copies ran while one was open for 11% of the time, Pallas kernels for 53%

profile of v2, /device:TPU:0, one launch (start us, length us, event | category | flops | bytes accessed | tf_op | source)
XLA Modules:
  0.0 403.9 jit_solution(3034094547755694220)
XLA Ops:
  0.6 1.6 collective-permute-start
  2.2 1.3 collective-permute-start.1
  3.5 1.6 collective-permute-start.3
  5.1 5.5 %concatenate.56 = bf16[2304]{0:T(1024)(128)(2,1)S(1)} concatenate(bf16[192]{0:T(256)(128)(2,1)} %param.17, bf16[192]{0:T(256)(128)(2,1)} %param.18, bf16[384]{0:T(512)(128)(2,1)} %param.20, bf16[192]{0:T(256)(128)(2,1)} %param.22, bf16[192]{0:T(256)(128)(2,1)} %param.23, bf16[192]{0:T(256)(128)(2,1)} %param.24, bf16[768]{0:T(1024)(128)(2,1)} %param.26, bf16[192]{0:T(256)(128)(2,1)} %param.28), dimensions={0} | concatenate | bytes 9216 | tf_op jit(solution)/shard_map/concatenate | solution.py:1082
  11.2 54.7 %gather_weights.1 = (bf16[4,192,2304]{2,1,0:T(8,128)(2,1)}, bf16[4,64,256]{2,1,0:T(8,128)(2,1)}, bf16[4,192,768]{2,1,0:T(8,128)(2,1)}, bf16[4,192,3072]{2,1,0:T(8,128)(2,1)}, bf16[4,768,768]{2,1,0:T(8,128)(2,1)}) custom-call(bf16[192,2304]{1,0:T(8,128)(2,1)} %refs_0_.1, bf16[64,256]{1,0:T(8,128)(2,1)} %reshape.241.refs_1_, bf16[192,768]{1,0:T(8,128)(2,1)} %refs_2_.1, ...), custom_call_target="tpu_custom_call" | custom-call | tf_op jit(solution)/shard_map/gather_weights/pallas_call | solution.py:445
  69.6 2.7 fusion
  73.8 20.3 %gather_blocks.4 = (bf16[8,128,1536]{2,1,0:T(8,128)(2,1)}, s32[8,16,128]{2,1,0:T(8,128)}) custom-call(bf16[128,1536]{1,0:T(8,128)(2,1)} %slice.126.refs_0_.k_own_ref.v_own_ref, s32[16,128]{1,0:T(8,128)} %broadcast_in_dim.9.refs_1_), custom_call_target="tpu_custom_call" | custom-call | tf_op jit(solution)/shard_map/gather_blocks/pallas_call | solution.py:552
  94.9 1.9 copy-done.2
  96.8 4.9 %attention_forward.2 = (bf16[128,768]{1,0:T(8,128)(2,1)S(1)}, f32[128,128]{1,0:T(8,128)S(1)}, f32[16,128]{1,0:T(8,128)S(1)}) custom-call(s32[1]{0:T(128)} %bitcast.1.start_ref, bf16[128,768]{1,0:T(8,128)(2,1)S(1)} %slice.125.q_ref.refs_0_, bf16[1024,1536]{1,0:T(8,128)(2,1)S(1)} %bitcast.70, bf16[1024,1536]{1,0:T(8,128)(2,1)S(1)} %bitcast.71, ...), custom_call_target="tpu_custom_call" | custom-call | flops 805306368 | bytes 3145728 | tf_op jit(solution)/shard_map/attention_forward/pallas_call | solution.py:147
  102.5 4.9 %multiply_convert_fusion.1 = (bf16[128,3072]{1,0:T(8,128)(2,1)S(1)}, f32[128,3072]{1,0:T(8,128)}) fusion(f32[3072]{0:T(1024)S(1)} %add.258, bf16[128,768]{1,0:T(8,128)(2,1)S(1)} %add_convert_fusion.2, bf16[768,3072]{1,0:T(8,128)(2,1)} %bitcast.93), kind=kOutput, calls=%fused_computation.37 | convolution fusion | flops 607911936 | bytes 7286784 | tf_op jit(solution)/shard_map/dot_general | solution.py:935
  111.5 18.7 %gather_blocks.5 = bf16[8,128,1536]{2,1,0:T(8,128)(2,1)} custom-call(bf16[128,1536]{1,0:T(8,128)(2,1)} %slice.133.refs_0_.k_own_ref.v_own_ref), custom_call_target="tpu_custom_call" | custom-call | tf_op jit(solution)/shard_map/gather_blocks/pallas_call | solution.py:552
  130.3 1.9 copy-done
  132.1 4.9 %attention_forward.3 = (bf16[128,768]{1,0:T(8,128)(2,1)S(1)}, f32[128,128]{1,0:T(8,128)S(1)}, f32[16,128]{1,0:T(8,128)S(1)}) custom-call(s32[1]{0:T(128)} %bitcast.1.start_ref, bf16[128,768]{1,0:T(8,128)(2,1)S(1)} %slice.132.q_ref.refs_0_, bf16[1024,1536]{1,0:T(8,128)(2,1)S(1)} %bitcast.66, bf16[1024,1536]{1,0:T(8,128)(2,1)S(1)} %bitcast.67, ...), custom_call_target="tpu_custom_call" | custom-call | flops 805306368 | bytes 3145728 | tf_op jit(solution)/shard_map/attention_forward/pallas_call | solution.py:147
  137.9 4.7 %multiply_convert_fusion = (bf16[128,3072]{1,0:T(8,128)(2,1)}, f32[128,3072]{1,0:T(8,128)S(1)}) fusion(f32[3072]{0:T(1024)S(1)} %add.258, bf16[128,768]{1,0:T(8,128)(2,1)S(1)} %add_convert_fusion, bf16[768,3072]{1,0:T(8,128)(2,1)} %bitcast.94), kind=kOutput, calls=%fused_computation.36 | convolution fusion | flops 607911936 | bytes 7286784 | tf_op jit(solution)/shard_map/dot_general | solution.py:935
  142.6 2.6 convert_reduce_fusion.1
  145.3 2.3 multiply_reduce_fusion.1
  147.7 1.6 convert_reduce_fusion.6
  149.8 1.1 fusion.61.delta_ref
  151.8 19.4 %gather_blocks.6 = (bf16[8,128,768]{2,1,0:T(8,128)(2,1)}, bf16[8,128,768]{2,1,0:T(8,128)(2,1)}, f32[8,32,128]{2,1,0:T(8,128)}) custom-call(bf16[128,768]{1,0:T(8,128)(2,1)} %copy-done.10, bf16[128,768]{1,0:T(8,128)(2,1)} %copy-done.14, f32[32,128]{1,0:T(8,128)} %pad_maximum_fusion.refs_2_), custom_call_target="tpu_custom_call" | custom-call | tf_op jit(solution)/shard_map/gather_blocks/pallas_call | solution.py:552
  172.2 0.9 copy-done.15
  173.9 1.4 copy-done.21
  175.3 1.4 copy-done.22
  179.3 15.0 %attention_backward.2 = bf16[128,2304]{1,0:T(8,128)(2,1)S(1)} custom-call(s32[1]{0:T(128)} %bitcast.1.start_ref, bf16[128,768]{1,0:T(8,128)(2,1)S(1)} %copy-done.11, bf16[128,768]{1,0:T(8,128)(2,1)S(1)} %copy-done.15, bf16[128,1536]{1,0:T(8,128)(2,1)S(1)} %copy-done.6, bf16[128,1536]{1,0:T(8,128)(2,1)S(1)} %copy-done.6, f32[128,128]{1,0:T(8,128)S(1)} %copy-done.34, ...), custom_call_target="tpu_custom_call" | custom-call | flops 1610612736 | bytes 6291456 | tf_op jit(solution)/shard_map/attention_backward/pallas_call | solution.py:275
  194.4 1.9 multiply_reduce_fusion.2
  197.7 5.2 %convert_reduce_fusion = (f32[3072]{0:T(1024)}, bf16[128,3072]{1,0:T(8,128)(2,1)S(1)}) fusion(f32[128,3072]{1,0:T(8,128)S(1)} %copy-done.105, bf16[128,768]{1,0:T(8,128)(2,1)S(1)} %get-tuple-element.83, bf16[3072,768]{1,0:T(8,128)(2,1)} %bitcast.85), kind=kOutput, calls=%fused_computation.34 | convolution fusion | flops 612627456 | bytes 7286784 | tf_op jit(solution)/shard_map/dot_general | solution.py:55
  203.0 2.3 multiply_reduce_fusion
  205.4 1.5 convert_reduce_fusion.5
  207.5 1.1 fusion.60.delta_ref
  209.0 3.6 convolution_convert_fusion.1
  212.6 1.5 convolution_convert_fusion.3
  215.4 19.4 %gather_blocks.7 = (bf16[8,128,768]{2,1,0:T(8,128)(2,1)}, bf16[8,128,768]{2,1,0:T(8,128)(2,1)}, f32[8,32,128]{2,1,0:T(8,128)}) custom-call(bf16[128,768]{1,0:T(8,128)(2,1)} %copy-done.8, bf16[128,768]{1,0:T(8,128)(2,1)} %copy-done.12, f32[32,128]{1,0:T(8,128)} %pad_maximum_fusion.1.refs_2_), custom_call_target="tpu_custom_call" | custom-call | tf_op jit(solution)/shard_map/gather_blocks/pallas_call | solution.py:552
  237.5 1.4 copy-done.19
  238.9 1.4 copy-done.20
  242.9 14.7 %attention_backward.3 = bf16[128,2304]{1,0:T(8,128)(2,1)S(1)} custom-call(s32[1]{0:T(128)} %bitcast.1.start_ref, bf16[128,768]{1,0:T(8,128)(2,1)S(1)} %copy-done.9, bf16[128,768]{1,0:T(8,128)(2,1)S(1)} %copy-done.13, bf16[128,1536]{1,0:T(8,128)(2,1)S(1)} %copy-done.7, bf16[128,1536]{1,0:T(8,128)(2,1)S(1)} %copy-done.7, f32[128,128]{1,0:T(8,128)S(1)} %copy-done.32, ...), custom_call_target="tpu_custom_call" | custom-call | flops 1610612736 | bytes 6291456 | tf_op jit(solution)/shard_map/attention_backward/pallas_call | solution.py:275
  257.7 2.9 convolution_convert_fusion
  260.7 4.0 fusion.29
  264.8 3.1 collective-permute-start.2
  268.0 1.4 fusion.43
  270.3 3.0 collective-permute-start.4
  274.7 3.6 convolution_convert_fusion.2
  278.4 111.5 %reduce_gradients.1 = (bf16[768,768]{1,0:T(8,128)(2,1)S(1)}, bf16[192,3072]{1,0:T(8,128)(2,1)S(1)}, bf16[192,768]{1,0:T(8,128)(2,1)S(1)}, bf16[192,2304]{1,0:T(8,128)(2,1)S(1)}, f32[72,128]{1,0:T(8,128)S(1)}) custom-call(bf16[4,768,768]{2,1,0:T(8,128)(2,1)} %bitcast.105, bf16[4,192,3072]{2,1,0:T(8,128)(2,1)} %bitcast.83, bf16[4,192,768]{2,1,0:T(8,128)(2,1)S(1)} %bitcast.78, ...), custom_call_target="tpu_custom_call" | custom-call | tf_op jit(solution)/shard_map/reduce_gradients/pallas_call | solution.py:826
  390.5 1.4 reshape.257
  391.9 1.3 convert_element_type.172
  393.9 1.3 dynamic-slice_bitcast_fusion.1
  396.1 1.7 convert_element_type.174
  398.4 1.6 convert_element_type.175
  400.6 1.6 copy.40
  402.2 1.6 copy.41
  (319 shorter events, 32.6 us)
Async XLA Ops:
  0.6 67.7 %collective-permute-start = (bf16[128,768]{1,0:T(8,128)(2,1)}, bf16[128,768]{1,0:T(8,128)(2,1)S(1)}, u32[]{:S(2)}, u32[]{:S(2)}) collective-permute-start(bf16[128,768]{1,0:T(8,128)(2,1)} %bitcast.111), channel_id=1, source_target_pairs={{0,0},{1,8},{2,16},{3,24},{4,4},{5,12},{6,20},{7,28},{8,1},{9,9},{... | collective-permute-start | bytes 589832 | tf_op jit(solution)/shard_map/ppermute | solution.py:854
  2.2 66.0 %collective-permute-start.1 = (s32[1,128]{1,0:T(1,128)}, s32[1,128]{1,0:T(1,128)S(1)}, u32[]{:S(2)}, u32[]{:S(2)}) collective-permute-start(s32[1,128]{1,0:T(1,128)} %param.16), channel_id=1, source_target_pairs={{0,0},{1,8},{2,16},{3,24},{4,4},{5,12},{6,20},{7,28},{8,1},{9,9},{... | collective-permute-start | bytes 1544 | tf_op jit(solution)/shard_map/ppermute | solution.py:854
  3.5 139.1 %collective-permute-start.3 = (bf16[128,768]{1,0:T(8,128)(2,1)}, bf16[128,768]{1,0:T(8,128)(2,1)S(1)}, u32[]{:S(2)}, u32[]{:S(2)}) collective-permute-start(bf16[128,768]{1,0:T(8,128)(2,1)} %bitcast.112), channel_id=1, source_target_pairs={{0,0},{1,8},{2,16},{3,24},{4,4},{5,12},{6,20},{7,28},{8,1},{9,9},{... | collective-permute-start | bytes 589832 | tf_op jit(solution)/shard_map/ppermute | solution.py:854
  67.3 40.2 %copy-start.78 = (f32[768]{0:T(1024)}, f32[768]{0:T(1024)S(1)}, u32[]{:S(2)}) copy-start(f32[768]{0:T(1024)S(1)} %add.264) | copy-start | bytes 9220
  67.5 41.2 %copy-start.69 = (f32[768]{0:T(1024)}, f32[768]{0:T(1024)S(1)}, u32[]{:S(2)}) copy-start(f32[768]{0:T(1024)S(1)} %mul.286) | copy-start | bytes 9220
  68.4 61.9 %copy-start.16 = (s32[128,1]{1,0:T(8,128)}, s32[128,1]{1,0:T(8,128)S(1)}, u32[]{:S(2)}) copy-start(s32[128,1]{1,0:T(8,128)S(1)} %copy.33.own_segs_ref) | copy-start | bytes 1540
  68.4 33.3 %copy-start.50 = (bf16[128,768]{1,0:T(8,128)(2,1)}, bf16[128,768]{1,0:T(8,128)(2,1)S(1)}, u32[]{:S(2)}) copy-start(bf16[128,768]{1,0:T(8,128)(2,1)S(1)} %collective-permute-done) | copy-start | bytes 589828
  72.3 29.3 %copy-start.8 = (bf16[128,768]{1,0:T(8,128)(2,1)}, bf16[128,768]{1,0:T(8,128)(2,1)S(1)}, u32[]{:S(2)}) copy-start(bf16[128,768]{1,0:T(8,128)(2,1)S(1)} %slice.125.q_ref.refs_0_) | copy-start | bytes 589828
  108.5 28.6 %copy-start.48 = (f32[128,768]{1,0:T(8,128)}, f32[128,768]{1,0:T(8,128)S(1)}, u32[]{:S(2)}) copy-start(f32[128,768]{1,0:T(8,128)S(1)} %get-tuple-element.113) | copy-start | bytes 1179652
  110.7 19.5 %copy-start.10 = (bf16[128,768]{1,0:T(8,128)(2,1)}, bf16[128,768]{1,0:T(8,128)(2,1)S(1)}, u32[]{:S(2)}) copy-start(bf16[128,768]{1,0:T(8,128)(2,1)S(1)} %slice.132.q_ref.refs_0_) | copy-start | bytes 589828
  137.1 13.8 %copy-start.26 = (bf16[128,768]{1,0:T(8,128)(2,1)}, bf16[128,768]{1,0:T(8,128)(2,1)S(1)}, u32[]{:S(2)}) copy-start(bf16[128,768]{1,0:T(8,128)(2,1)S(1)} %get-tuple-element.46) | copy-start | bytes 589828
  137.5 10.1 %copy-start.46 = (f32[128,768]{1,0:T(8,128)}, f32[128,768]{1,0:T(8,128)S(1)}, u32[]{:S(2)}) copy-start(f32[128,768]{1,0:T(8,128)S(1)} %get-tuple-element.115) | copy-start | bytes 1179652
  137.9 7.4 %slice-start.4 = ((s8[4718592]{0:T(1024)(128)(4,1)}), s8[4194304]{0:T(1024)(128)(4,1)S(1)}, s32[]{:S(2)}) async-start(s8[4718592]{0:T(1024)(128)(4,1)} %bitcast.95), calls=%async_computation.4 | async-start | bytes 8388608
  147.7 23.5 %copy-start.1 = (bf16[8,128,1536]{2,1,0:T(8,128)(2,1)S(1)}, bf16[8,128,1536]{2,1,0:T(8,128)(2,1)}, u32[]{:S(2)}) copy-start(bf16[8,128,1536]{2,1,0:T(8,128)(2,1)} %gather_blocks.5) | copy-start | bytes 9437188
  149.2 22.0 %copy-start.6 = (bf16[128,1536]{1,0:T(8,128)(2,1)S(1)}, bf16[128,1536]{1,0:T(8,128)(2,1)}, u32[]{:S(2)}) copy-start(bf16[128,1536]{1,0:T(8,128)(2,1)} %slice.133.refs_0_.k_own_ref.v_own_ref) | copy-start | bytes 1179652
  179.3 15.0 %copy-start.39 = (bf16[4,192,2304]{2,1,0:T(8,128)(2,1)S(1)}, bf16[4,192,2304]{2,1,0:T(8,128)(2,1)}, u32[]{:S(2)}) copy-start(bf16[4,192,2304]{2,1,0:T(8,128)(2,1)} %get-tuple-element.39) | copy-start | bytes 10616836
  179.3 15.0 %copy-start.49 = (f32[128,768]{1,0:T(8,128)S(1)}, f32[128,768]{1,0:T(8,128)}, u32[]{:S(2)}) copy-start(f32[128,768]{1,0:T(8,128)} %copy-done.48) | copy-start | bytes 1179652
  179.3 15.0 %copy-start.70 = (f32[768]{0:T(1024)S(1)}, f32[768]{0:T(1024)}, u32[]{:S(2)}) copy-start(f32[768]{0:T(1024)} %copy-done.69) | copy-start | bytes 9220
  179.3 15.0 %copy-start.98 = (f32[128]{0:T(128)S(1)}, f32[128]{0:T(128)}, u32[]{:S(2)}) copy-start(f32[128]{0:T(128)} %copy-done.97) | copy-start | bytes 1540
  179.3 15.0 %copy-start.104 = (f32[128]{0:T(128)S(1)}, f32[128]{0:T(128)}, u32[]{:S(2)}) copy-start(f32[128]{0:T(128)} %copy-done.103) | copy-start | bytes 1540
  194.4 19.7 %copy-start.4 = (bf16[128,2304]{1,0:T(8,128)(2,1)}, bf16[128,2304]{1,0:T(8,128)(2,1)S(1)}, u32[]{:S(2)}) copy-start(bf16[128,2304]{1,0:T(8,128)(2,1)S(1)} %attention_backward.2) | copy-start | bytes 1769476
  196.3 6.7 %slice-start.6 = ((s8[4718592]{0:T(1024)(128)(4,1)}), s8[4194304]{0:T(1024)(128)(4,1)S(1)}, s32[]{:S(2)}) async-start(s8[4718592]{0:T(1024)(128)(4,1)} %bitcast.98), calls=%async_computation.6 | async-start | bytes 8388608
  197.1 5.8 %copy-start.74 = (bf16[128,768]{1,0:T(8,128)(2,1)}, bf16[128,768]{1,0:T(8,128)(2,1)S(1)}, u32[]{:S(2)}) copy-start(bf16[128,768]{1,0:T(8,128)(2,1)S(1)} %get-tuple-element.83) | copy-start | bytes 589828
  208.9 25.9 %copy-start.3 = (bf16[8,128,1536]{2,1,0:T(8,128)(2,1)S(1)}, bf16[8,128,1536]{2,1,0:T(8,128)(2,1)}, u32[]{:S(2)}) copy-start(bf16[8,128,1536]{2,1,0:T(8,128)(2,1)} %get-tuple-element.40) | copy-start | bytes 9437188
  212.6 22.3 %copy-start.7 = (bf16[128,1536]{1,0:T(8,128)(2,1)S(1)}, bf16[128,1536]{1,0:T(8,128)(2,1)}, u32[]{:S(2)}) copy-start(bf16[128,1536]{1,0:T(8,128)(2,1)} %slice.126.refs_0_.k_own_ref.v_own_ref) | copy-start | bytes 1179652
  242.9 14.7 %copy-start.5 = (bf16[128,2304]{1,0:T(8,128)(2,1)S(1)}, bf16[128,2304]{1,0:T(8,128)(2,1)}, u32[]{:S(2)}) copy-start(bf16[128,2304]{1,0:T(8,128)(2,1)} %copy-done.4) | copy-start | bytes 1769476
  242.9 14.7 %copy-start.55 = (bf16[128,768]{1,0:T(8,128)(2,1)S(1)}, bf16[128,768]{1,0:T(8,128)(2,1)}, u32[]{:S(2)}) copy-start(bf16[128,768]{1,0:T(8,128)(2,1)} %copy-done.54) | copy-start | bytes 589828
  242.9 14.7 %copy-start.57 = (bf16[128,768]{1,0:T(8,128)(2,1)S(1)}, bf16[128,768]{1,0:T(8,128)(2,1)}, u32[]{:S(2)}) copy-start(bf16[128,768]{1,0:T(8,128)(2,1)} %copy-done.56) | copy-start | bytes 589828
  260.7 7.3 %copy-start.40 = (bf16[4,192,2304]{2,1,0:T(8,128)(2,1)S(1)}, bf16[4,192,2304]{2,1,0:T(8,128)(2,1)}, u32[]{:S(2)}) copy-start(bf16[4,192,2304]{2,1,0:T(8,128)(2,1)} %get-tuple-element.39) | copy-start | bytes 10616836
  260.7 7.3 %copy-start.51 = (bf16[128,768]{1,0:T(8,128)(2,1)S(1)}, bf16[128,768]{1,0:T(8,128)(2,1)}, u32[]{:S(2)}) copy-start(bf16[128,768]{1,0:T(8,128)(2,1)} %copy-done.50) | copy-start | bytes 589828
  260.7 7.2 %copy-start.71 = (f32[768]{0:T(1024)S(1)}, f32[768]{0:T(1024)}, u32[]{:S(2)}) copy-start(f32[768]{0:T(1024)} %copy-done.69) | copy-start | bytes 9220
  260.7 7.2 %copy-start.94 = (f32[128]{0:T(128)S(1)}, f32[128]{0:T(128)}, u32[]{:S(2)}) copy-start(f32[128]{0:T(128)} %copy-done.93) | copy-start | bytes 1540
  260.7 7.2 %copy-start.100 = (f32[128]{0:T(128)S(1)}, f32[128]{0:T(128)}, u32[]{:S(2)}) copy-start(f32[128]{0:T(128)} %copy-done.99) | copy-start | bytes 1540
  264.7 8.6 %copy-start.90 = (f32[768]{0:T(1024)S(1)}, f32[768]{0:T(1024)}, u32[]{:S(2)}) copy-start(f32[768]{0:T(1024)} %get-tuple-element.66) | copy-start | bytes 9220
  264.7 8.7 %copy-start.89 = (f32[768]{0:T(1024)S(1)}, f32[768]{0:T(1024)}, u32[]{:S(2)}) copy-start(f32[768]{0:T(1024)} %get-tuple-element.81) | copy-start | bytes 9220
  264.7 8.8 %copy-start.88 = (f32[768]{0:T(1024)S(1)}, f32[768]{0:T(1024)}, u32[]{:S(2)}) copy-start(f32[768]{0:T(1024)} %get-tuple-element.73) | copy-start | bytes 9220
  264.7 8.8 %copy-start.83 = (f32[768]{0:T(1024)S(1)}, f32[768]{0:T(1024)}, u32[]{:S(2)}) copy-start(f32[768]{0:T(1024)} %get-tuple-element.90) | copy-start | bytes 9220
  264.7 8.8 %copy-start.87 = (f32[768]{0:T(1024)S(1)}, f32[768]{0:T(1024)}, u32[]{:S(2)}) copy-start(f32[768]{0:T(1024)} %get-tuple-element.87) | copy-start | bytes 9220
  264.7 8.9 %copy-start.82 = (f32[768]{0:T(1024)S(1)}, f32[768]{0:T(1024)}, u32[]{:S(2)}) copy-start(f32[768]{0:T(1024)} %get-tuple-element.64) | copy-start | bytes 9220
  264.8 8.9 %copy-start.86 = (f32[768]{0:T(1024)S(1)}, f32[768]{0:T(1024)}, u32[]{:S(2)}) copy-start(f32[768]{0:T(1024)} %get-tuple-element.62) | copy-start | bytes 9220
  264.8 9.0 %copy-start.81 = (f32[768]{0:T(1024)S(1)}, f32[768]{0:T(1024)}, u32[]{:S(2)}) copy-start(f32[768]{0:T(1024)} %get-tuple-element.79) | copy-start | bytes 9220
  264.8 9.0 %copy-start.85 = (f32[768]{0:T(1024)S(1)}, f32[768]{0:T(1024)}, u32[]{:S(2)}) copy-start(f32[768]{0:T(1024)} %get-tuple-element.78) | copy-start | bytes 9220
  264.8 9.0 %copy-start.91 = (f32[3072]{0:T(1024)S(1)}, f32[3072]{0:T(1024)}, u32[]{:S(2)}) copy-start(f32[3072]{0:T(1024)} %get-tuple-element.122) | copy-start | bytes 36868
  264.8 9.0 %copy-start.92 = (f32[3072]{0:T(1024)S(1)}, f32[3072]{0:T(1024)}, u32[]{:S(2)}) copy-start(f32[3072]{0:T(1024)} %get-tuple-element.85) | copy-start | bytes 36868
  264.8 9.0 %copy-start.80 = (f32[768]{0:T(1024)S(1)}, f32[768]{0:T(1024)}, u32[]{:S(2)}) copy-start(f32[768]{0:T(1024)} %get-tuple-element.101) | copy-start | bytes 9220
  264.8 9.0 %copy-start.84 = (f32[768]{0:T(1024)S(1)}, f32[768]{0:T(1024)}, u32[]{:S(2)}) copy-start(f32[768]{0:T(1024)} %get-tuple-element.82) | copy-start | bytes 9220
  264.8 135.8 %collective-permute-start.2 = (bf16[128,768]{1,0:T(8,128)(2,1)}, bf16[128,768]{1,0:T(8,128)(2,1)}, u32[]{:S(2)}, u32[]{:S(2)}) collective-permute-start(bf16[128,768]{1,0:T(8,128)(2,1)} %fusion.29), channel_id=1, source_target_pairs={{0,0},{1,8},{2,16},{3,24},{4,4},{5,12},{6,20},{7,28},{8,1},{9,9},{... | collective-permute-start | bytes 589832 | tf_op jit(solution)/shard_map/ppermute | solution.py:854
  270.3 130.3 %collective-permute-start.4 = (bf16[128,768]{1,0:T(8,128)(2,1)}, bf16[128,768]{1,0:T(8,128)(2,1)}, u32[]{:S(2)}, u32[]{:S(2)}) collective-permute-start(bf16[128,768]{1,0:T(8,128)(2,1)} %fusion.42), channel_id=1, source_target_pairs={{0,0},{1,8},{2,16},{3,24},{4,4},{5,12},{6,20},{7,28},{8,1},{9,9},{... | collective-permute-start | bytes 589832 | tf_op jit(solution)/shard_map/ppermute | solution.py:854
  (71 other events, 200.2 us)

commit v3 on v2

--- a/solution.py
+++ b/solution.py
@@ -324,6 +324,39 @@
     return lax.rem(ctx, 2), ctx // 2, fsdp // 2, lax.rem(fsdp, 2)
 
 
+class Place:
+    def __init__(self):
+        self.x, self.z, self.y, self.core = x, z, y, core = place_bits()
+        self.low, self.high = low, high = lax.rem(z, 2), z // 2
+        self.fsdp = fsdp = 2 * y + core
+        self.block = 2 * fsdp + x
+        self.sibling = (2 * z + x, 2 * y + 1 - core)
+        self.over_y = (2 * z + x, 2 * (1 - y) + core)
+        self.over_x = (2 * z + 1 - x, fsdp)
+        self.over_z = (2 * (z + 1 - 2 * low) + x, fsdp)
+        self.over_zz = (2 * (z + 2 - 4 * high) + x, fsdp)
+        self.partner = (2 * fsdp + x, z)
+        self.has_partner = fsdp != z
+
+
+class Copies:
+    def __init__(self, send_sems, recv_sems):
+        self.send_sems, self.recv_sems = send_sems, recv_sems
+        self.used = 0
+
+    def make(self, src, dst, device):
+        slot = self.used
+        self.used += 1
+        return pltpu.make_async_remote_copy(
+            src_ref=src,
+            dst_ref=dst,
+            send_sem=self.send_sems.at[slot],
+            recv_sem=self.recv_sems.at[slot],
+            device_id=device,
+            device_id_type=MESH,
+        )
+
+
 def greet(devices):
     barrier = pltpu.get_barrier_semaphore()
     for device in devices:
@@ -334,89 +367,76 @@
 WEIGHT_COPIES = 11
 
 
-def gather_weights_kernel(count, *refs):
-    shares, fulls = refs[:count], refs[count : 2 * count]
-    send_sems, recv_sems, local_sems = refs[2 * count : 2 * count + 3]
-    stages = refs[2 * count + 3 :]
-    x, z, y, core = place_bits()
-    low = lax.rem(z, 2)
-    z_next = z + 1 - 2 * low
-    sibling = (2 * z + x, 2 * y + 1 - core)
-    over_y = (2 * z + x, 2 * (1 - y) + core)
-    over_x = (2 * z + 1 - x, 2 * y + core)
-    over_z = (2 * z_next + x, 2 * y + core)
-    own = 2 * y + core
-    other = 2 * (1 - y) + core
-    greet((sibling, over_y, over_x, over_z))
-
-    def copy(index, which, src, dst, device):
-        slot = which * WEIGHT_COPIES + index
-        return pltpu.make_async_remote_copy(
-            src_ref=src,
-            dst_ref=dst,
-            send_sem=send_sems.at[slot],
-            recv_sem=recv_sems.at[slot],
-            device_id=device,
-            device_id_type=MESH,
-        )
-
-    started = []
-    locals_started = []
-    plans = []
-    for which in range(count):
-        share, full = shares[which], fulls[which]
-        rows, columns = share.shape
-        part = rows // 4
-        half = columns // 2
-
-        def piece(ref, x_bit, low_bit, part=part):
-            return ref.at[pl.ds((2 * low_bit + x_bit) * part, part), :]
-
-        def piece_half(ref, x_bit, low_bit, side, part=part, half=half):
-            return ref.at[pl.ds((2 * low_bit + x_bit) * part, part), pl.ds(side * half, half)]
-
-        theirs = full.at[other]
-        same = lambda index, view, device, which=which: copy(index, which, view, view, device)
-        mine = piece(theirs, x, low)
-        from_x = piece(theirs, 1 - x, low)
-        from_z = piece(theirs, x, 1 - low)
-        plan = {
-            0: copy(0, which, piece(share, x, low), piece(full.at[own], x, low), over_y),
-            1: same(1, mine, over_x),
-            2: same(2, mine, over_z),
-            3: same(3, mine, sibling),
-            4: same(4, piece_half(theirs, 1 - x, low, 0), over_z),
-            5: same(5, from_x, sibling),
-            6: same(6, piece_half(theirs, x, 1 - low, 1), over_x),
-            7: same(7, from_z, sibling),
-            8: same(8, piece_half(theirs, 1 - x, 1 - low, 0), sibling),
-            9: same(9, piece_half(theirs, 1 - x, 1 - low, 1), sibling),
-            10: copy(10, which, share, full.at[own], sibling),
-        }
-        plans.append(plan)
-        plan[0].start()
-        plan[10].start()
-        pltpu.make_async_copy(share, stages[which], local_sems.at[which]).start()
-        locals_started.append(
-            (
-                pltpu.make_async_copy(share, stages[which], local_sems.at[which]),
-                pltpu.make_async_copy(stages[which], full.at[own], local_sems.at[which]),
+class WeightGather:
+    def __init__(self, place, copies, shares, fulls, stages, local_sems):
+        x, low = place.x, place.low
+        own, other = place.fsdp, 2 * (1 - place.y) + place.core
+        self.plans = []
+        self.locals = []
+        for which, (share, full) in enumerate(zip(shares, fulls)):
+            rows, columns = share.shape
+            part, half = rows // 4, columns // 2
+
+            def piece(ref, x_bit, low_bit, part=part):
+                return ref.at[pl.ds((2 * low_bit + x_bit) * part, part), :]
+
+            def side(ref, x_bit, low_bit, index, part=part, half=half):
+                place_of = pl.ds((2 * low_bit + x_bit) * part, part)
+                return ref.at[place_of, pl.ds(index * half, half)]
+
+            theirs = full.at[other]
+            same = lambda view, device: copies.make(view, view, device)
+            mine = piece(theirs, x, low)
+            from_x, from_z = piece(theirs, 1 - x, low), piece(theirs, x, 1 - low)
+            self.plans.append(
+                [
+                    copies.make(piece(share, x, low), piece(full.at[own], x, low), place.over_y),
+                    same(mine, place.over_x),
+                    same(mine, place.over_z),
+                    same(mine, place.sibling),
+                    same(side(theirs, 1 - x, low, 0), place.over_z),
+                    same(from_x, place.sibling),
+                    same(side(theirs, x, 1 - low, 1), place.over_x),
+                    same(from_z, place.sibling),
+                    same(side(theirs, 1 - x, 1 - low, 0), place.sibling),
+                    same(side(theirs, 1 - x, 1 - low, 1), place.sibling),
+                    copies.make(share, full.at[own], place.sibling),
+                ]
             )
-        )
-
-    for into, out in locals_started:
-        into.wait()
-        out.start()
-
-    for step in range(count + 2):
+            sem = local_sems.at[which]
+            self.locals.append(
+                (
+                    pltpu.make_async_copy(share, stages[which], sem),
+                    pltpu.make_async_copy(stages[which], full.at[own], sem),
+                )
+            )
+
+    def begin(self):
+        for plan, (into, _) in zip(self.plans, self.locals):
+            plan[0].start()
+            plan[10].start()
+            into.start()
+
+    def keep_own(self):
+        for into, out in self.locals:
+            into.wait()
+            out.start()
+
+    def steps(self):
+        count = len(self.plans)
+        for step in range(count + 2):
+            yield step
+
+    def step(self, step):
+        count = len(self.plans)
         if step < count:
-            plan = plans[step]
+            plan = self.plans[step]
             plan[0].wait_recv()
             plan[1].start()
             plan[2].start()
             plan[3].start()
         if 0 <= step - 1 < count:
-            plan = plans[step - 1]
+            plan = self.plans[step - 1]
             plan[1].wait_recv()
             plan[4].start()
             plan[5].start()
@@ -424,144 +444,586 @@
             plan[6].start()
             plan[7].start()
         if 0 <= step - 2 < count:
-            plan = plans[step - 2]
+            plan = self.plans[step - 2]
             plan[4].wait_recv()
             plan[8].start()
             plan[6].wait_recv()
             plan[9].start()
-    for plan in plans:
-        for index in (3, 5, 7, 8, 9, 10):
-            plan[index].wait_recv()
-        for index in range(WEIGHT_COPIES):
-            plan[index].wait_send()
-    for _, out in locals_started:
-        out.wait()
-
-
-def gather_weights(shares, collective_id):
-    count = len(shares)
-    copies = count * WEIGHT_COPIES
+
+    def finish(self):
+        for plan in self.plans:
+            for index in (3, 5, 7, 8, 9, 10):
+                plan[index].wait_recv()
+            for copy in plan:
+                copy.wait_send()
+        for _, out in self.locals:
+            out.wait()
+
+
+BLOCK_COPIES = 13
+
+
+class BlockGather:
+    def __init__(self, place, copies, blocks, fulls):
+        self.own = place.block
+        self.pairs = list(zip(blocks, fulls))
+        self.plans = []
+        for block, full in self.pairs:
+            half = block.shape[0] // 2
+
+            def part(ref, side, half=half):
+                return ref.at[pl.ds(side * half, half), :]
+
+            def slot_of(x_bit, y_bit, full=full):
+                return full.at[4 * y_bit + 2 * place.core + x_bit]
+
+            same = lambda view, device: copies.make(view, view, device)
+            x, y = place.x, place.y
+            mine, from_x = slot_of(x, y), slot_of(1 - x, y)
+            from_y, from_both = slot_of(x, 1 - y), slot_of(1 - x, 1 - y)
+            self.plans.append(
+                [
+                    copies.make(block, mine, place.sibling),
+                    copies.make(part(block, 0), part(mine, 0), place.over_x),
+                    copies.make(part(block, 1), part(mine, 1), place.over_y),
+                    copies.make(part(block, 1), part(mine, 1), place.over_x),
+                    copies.make(part(block, 0), part(mine, 0), place.over_y),
+                    same(part(from_x, 0), place.over_y),
+                    same(part(from_x, 0), place.sibling),
+                    same(part(from_y, 1), place.over_x),
+                    same(part(from_y, 1), place.sibling),
+                    same(part(from_x, 1), place.sibling),
+                    same(part(from_y, 0), place.sibling),
+                    same(part(from_both, 0), place.sibling),
+                    same(part(from_both, 1), place.sibling),
+                ]
+            )
+
+    def begin(self):
+        for index in (1, 2, 3, 4, 0):
+            for plan in self.plans:
+                plan[index].start()
+        for block, full in self.pairs:
+            full[self.own] = block[...]
+
+    def relay(self, *pairs):
+        for arrived, followers in pairs:
+            for plan in self.plans:
+                plan[arrived].wait_recv()
+                for index in followers:
+                    plan[index].start()
+
+    def first_halves(self):
+        self.relay((1, (5, 6)), (2, (7, 8)))
+
+    def second_halves(self):
+        self.relay((3, (9,)), (4, (10,)))
+
+    def corners(self):
+        self.relay((5, (11,)), (7, (12,)))
+
+    def wait(self, *indices):
+        for plan in self.plans:
+            for index in indices:
+                plan[index].wait_recv()
+
+    def wait_near(self):
+        self.wait(0, 6, 9)
+
+    def wait_far(self):
+        self.wait(8, 10, 11, 12)
+
+    def finish(self):
+        for plan in self.plans:
+            for copy in plan:
+                copy.wait_send()
+
+
+def opening_kernel(
+    tokens_ref,
+    segs_ref,
+    cotangent_ref,
+    vectors_ref,
+    weight_ref,
+    tokens_out,
+    segs_out,
+    cotangent_out,
+    vectors_out,
+    weight_out,
+    vectors_all,
+    segs_own,
+    stage,
+    send_sems,
+    recv_sems,
+    local_sems,
+):
+    place = Place()
+    others = (place.sibling, place.over_x, place.over_y, place.over_z)
+    barrier = pltpu.get_barrier_semaphore()
+    for device in others:
+        pl.semaphore_signal(barrier, inc=1, device_id=device, device_id_type=MESH)
+
+    @pl.when(place.has_partner)
+    def _():
+        pl.semaphore_signal(barrier, inc=1, device_id=place.partner, device_id_type=MESH)
+        pl.semaphore_wait(barrier, len(others) + 1)
+
+    @pl.when(jnp.logical_not(place.has_partner))
+    def _():
+        pl.semaphore_wait(barrier, len(others))
+
+    copies = Copies(send_sems, recv_sems)
+    swaps = [
+        copies.make(segs_ref, segs_own, place.partner),
+        copies.make(tokens_ref, tokens_out, place.partner),
+        copies.make(cotangent_ref, cotangent_out, place.partner),
+    ]
+    own, other = place.fsdp, 2 * (1 - place.y) + place.core
+    vector_copies = [
+        copies.make(vectors_ref, vectors_all.at[own], place.over_y),
+        copies.make(vectors_ref, vectors_all.at[own], place.sibling),
+        copies.make(vectors_all.at[other], vectors_all.at[other], place.sibling),
+    ]
+    gather = WeightGather(place, copies, [weight_ref], [weight_out], [stage], local_sems)
+    segs = BlockGather(place, copies, [segs_own], [segs_out])
+
+    @pl.when(place.has_partner)
+    def _():
+        for swap in swaps:
+            swap.start()
+
+    vector_copies[0].start()
+    vector_copies[1].start()
+    vectors_all[own] = vectors_ref[...]
+    gather.begin()
+
+    @pl.when(jnp.logical_not(place.has_partner))
+    def _():
+        segs_own[...] = segs_ref[...]
+        tokens_out[...] = tokens_ref[...]
+        cotangent_out[...] = cotangent_ref[...]
+
+    @pl.when(place.has_partner)
+    def _():
+        swaps[0].wait_recv()
+
+    segs.begin()
+    vector_copies[0].wait_recv()
+    vector_copies[2].start()
+    segs.first_halves()
+    segs.second_halves()
+    segs.corners()
+    gather.keep_own()
+    for step in gather.steps():
+        gather.step(step)
+    segs.wait_near()
+    segs.wait_far()
+    segs.finish()
+    vector_copies[1].wait_recv()
+    vector_copies[2].wait_recv()
+    for copy in vector_copies:
+        copy.wait_send()
+    vectors_out[...] = assemble_vectors([vectors_all[i] for i in range(4)])
+
+    @pl.when(place.has_partner)
+    def _():
+        for swap in swaps[1:]:
+            swap.wait_recv()
+        for swap in swaps:
+            swap.wait_send()
+
+    gather.finish()
+
+
+def pack_vectors(ln1_gain, ln1_bias, ln2_gain, ln2_bias, proj_bias, out_bias, attn_bias, fc_bias):
+    rows = (ln1_gain, ln1_bias, ln2_gain, ln2_bias, proj_bias, out_bias, attn_bias, fc_bias)
+    return jnp.stack([jnp.pad(row.astype(F32), (0, D - row.shape[0])) for row in rows])
+
+
+def assemble_vectors(shares):
+    quarter = D // 4
+    small = jnp.concatenate([share[:6, :quarter] for share in shares], axis=1)
+    query = jnp.concatenate([shares[0][6:7, : 2 * quarter], shares[1][6:7, : 2 * quarter]], axis=1)
+    value = jnp.concatenate([shares[2][6:7, : 2 * quarter], shares[3][6:7, : 2 * quarter]], axis=1)
+    hidden = [share[7:8] for share in shares]
+    return jnp.concatenate([small, query, value, *hidden, jnp.zeros((4, D), F32)], axis=0)
+
+
+def opening(tokens, segs, cotangent, vectors, weight, collective_id):
+    rows, columns = tokens.shape
+    copies = 3 + 3 + WEIGHT_COPIES + BLOCK_COPIES
+    vmem = pl.BlockSpec(memory_space=pltpu.VMEM)
     anywhere = pl.BlockSpec(memory_space=pl.ANY)
-    fulls = pl.pallas_call(
-        partial(gather_weights_kernel, count),
-        in_specs=[anywhere] * count,
-        out_specs=[anywhere] * count,
-        out_shape=[jax.ShapeDtypeStruct((4, *share.shape), share.dtype) for share in shares],
+    return pl.pallas_call(
+        opening_kernel,
+        in_specs=[vmem, vmem, vmem, vmem, anywhere],
+        out_specs=[vmem, vmem, vmem, vmem, anywhere],
+        out_shape=[
+            jax.ShapeDtypeStruct((rows, columns), tokens.dtype),
+            jax.ShapeDtypeStruct((8, *segs.shape), segs.dtype),
+            jax.ShapeDtypeStruct((rows, columns), cotangent.dtype),
+            jax.ShapeDtypeStruct((16, D), F32),
+            jax.ShapeDtypeStruct((4, *weight.shape), weight.dtype),
+        ],
         scratch_shapes=[
+            pltpu.VMEM((4, *vectors.shape), F32),
+            pltpu.VMEM(segs.shape, segs.dtype),
+            pltpu.VMEM(weight.shape, weight.dtype),
             pltpu.SemaphoreType.DMA((copies,)),
             pltpu.SemaphoreType.DMA((copies,)),
-            pltpu.SemaphoreType.DMA((count,)),
+            pltpu.SemaphoreType.DMA((1,)),
+        ],
+        compiler_params=pltpu.CompilerParams(
+            collective_id=collective_id, has_side_effects=True, vmem_limit_bytes=32 << 20
+        ),
+        name="opening",
+    )(tokens, segs, cotangent, vectors, weight)
+
+
+def mask_block(own_segs, segs_ref, block, start, own_is_query):
+    rows = own_segs.shape[0]
+    own_place = start + lax.broadcasted_iota(jnp.int32, (rows, rows), 0)
+    place = block * rows + lax.broadcasted_iota(jnp.int32, (rows, rows), 1)
+    causal = (place <= own_place) if own_is_query else (own_place <= place)
+    same = own_segs == segs_ref[block, 0:1, :]
+    return jnp.where(causal & same, 0.0, NEGATIVE)
+
+
+def own_columns(segs_ref, block):
+    rows = segs_ref.shape[2]
+    return jnp.broadcast_to(segs_ref[block, 0:1, :], (rows, rows)).T
+
+
+def attend_kernel(count, *refs):
+    q_ref, kv_ref, segs_ref = refs[:3]
+    shares = refs[3 : 3 + count]
+    out_ref, lse_ref, lse_rows_ref, kv_out = refs[3 + count : 7 + count]
+    fulls = refs[7 + count : 7 + 2 * count]
+    rest = refs[7 + 2 * count :]
+    kv_all, near_bias, far_bias, top_ref, total_ref, mixed_ref, send_sems, recv_sems, local_sems = rest[:9]
+    stages = rest[9:]
+    place = Place()
+    devices = [place.sibling, place.over_x, place.over_y] + ([place.over_z] if count else [])
+    greet(devices)
+    copies = Copies(send_sems, recv_sems)
+    gather = BlockGather(place, copies, [kv_ref], [kv_all])
+    weights = WeightGather(place, copies, shares, fulls, stages, local_sems)
+    gather.begin()
+
+    rows = q_ref.shape[0]
+    start = place.block * rows
+    near, far = 4 * place.y, 4 * (1 - place.y)
+    own_segs = own_columns(segs_ref, place.block)
+    for i in range(4):
+        near_bias[:, i * rows : (i + 1) * rows] = mask_block(own_segs, segs_ref, near + i, start, True)
+        far_bias[:, i * rows : (i + 1) * rows] = mask_block(own_segs, segs_ref, far + i, start, True)
+    lse_ref[...] = jnp.zeros_like(lse_ref)
+    gather.first_halves()
+    if count:
+        weights.begin()
+        weights.keep_own()
+    gather.second_halves()
+
+    def blocks_of(first, pair, side):
+        lanes = pl.ds(pl.multiple_of(side * D + pair * LANES, LANES), LANES)
+        return kv_all[pl.ds(first, 4), :, lanes].reshape(4 * rows, LANES)
+
+    def queries_of(pair):
+        lanes = pl.ds(pl.multiple_of(pair * LANES, LANES), LANES)
+        return two_heads(q_ref[:, lanes] * jnp.asarray(SCALE, BF16))
+
+    def part(first, bias_ref, pair):
+        bias = bias_ref[...]
+        scores = dot_rows(queries_of(pair), blocks_of(first, pair, 0))
+        scores = scores + jnp.concatenate([bias, bias], axis=0)
+        top = jnp.max(scores, axis=1, keepdims=True)
+        weights_here = jnp.exp(scores - top)
+        total = jnp.sum(weights_here, axis=1, keepdims=True)
+        mixed = jnp.dot(
+            weights_here.astype(BF16), blocks_of(first, pair, 1), preferred_element_type=F32
+        )
+        return top, total, mixed
+
+    def visit_near(pair, carried):
+        top_ref[pair], total_ref[pair], mixed_ref[pair] = part(near, near_bias, pair)
+        return carried
+
+    def visit_far(pair, carried):
+        top, total, mixed = part(far, far_bias, pair)
+        old_top, old_total, old_mixed = top_ref[pair], total_ref[pair], mixed_ref[pair]
+        new_top = jnp.maximum(top, old_top)
+        new, old = jnp.exp(top - new_top), jnp.exp(old_top - new_top)
+        top_ref[pair] = new_top
+        total_ref[pair] = total * new + old_total * old
+        mixed_ref[pair] = mixed * new + old_mixed * old
+        return carried
+
+    def visit_last(pair, carried):
+        top, total, mixed = top_ref[pair], total_ref[pair], mixed_ref[pair]
+        lanes = pl.ds(pl.multiple_of(pair * LANES, LANES), LANES)
+        out_ref[:, lanes] = one_pair(mixed / total).astype(BF16)
+        lse = top + jnp.log(total)
+        lane = lax.broadcasted_iota(jnp.int32, (rows, LANES), 1)
+        kept = jnp.where(lane == 2 * pair, lse[:rows], lse_ref[...])
+        lse_ref[...] = jnp.where(lane == 2 * pair + 1, lse[rows:], kept)
+        return carried
+
+    gather.wait_near()
+    near_out = pltpu.make_async_copy(
+        kv_all.at[pl.ds(near, 4)], kv_out.at[pl.ds(near, 4)], local_sems.at[count]
+    )
+    near_out.start()
+    lax.fori_loop(0, PAIRS, visit_near, 0)
+    gather.corners()
+    if count:
+        weights.step(0)
+    gather.wait_far()
+    far_out = pltpu.make_async_copy(
+        kv_all.at[pl.ds(far, 4)], kv_out.at[pl.ds(far, 4)], local_sems.at[count + 1]
+    )
+    far_out.start()
+
+    @pl.when(place.y == 1)
+    def _():
+        lax.fori_loop(0, PAIRS, visit_far, 0)
+
+    lax.fori_loop(0, PAIRS, visit_last, 0)
+    lse_rows_ref[...] = lse_ref[...].T[:16]
+    for step in weights.steps():
+        if count and step > 0:
+            weights.step(step)
+    weights.finish()
+    gather.finish()
+    near_out.wait()
+    far_out.wait()
+
+
+def attend(queries, kv_own, segs, shares, collective_id):
+    rows = queries.shape[0]
+    count = len(shares)
+    slots = BLOCK_COPIES + count * WEIGHT_COPIES
+    vmem = pl.BlockSpec(memory_space=pltpu.VMEM)
+    anywhere = pl.BlockSpec(memory_space=pl.ANY)
+    return pl.pallas_call(
+        partial(attend_kernel, count),
+        in_specs=[vmem, vmem, vmem] + [anywhere] * count,
+        out_specs=[vmem, vmem, vmem, anywhere] + [anywhere] * count,
+        out_shape=[
+            jax.ShapeDtypeStruct((rows, D), BF16),
+            jax.ShapeDtypeStruct((rows, LANES), F32),
+            jax.ShapeDtypeStruct((16, rows), F32),
+            jax.ShapeDtypeStruct((8, rows, 2 * D), BF16),
+        ]
+        + [jax.ShapeDtypeStruct((4, *share.shape), share.dtype) for share in shares],
+        scratch_shapes=[
+            pltpu.VMEM((8, rows, 2 * D), BF16),
+            pltpu.VMEM((rows, 4 * rows), F32),
+            pltpu.VMEM((rows, 4 * rows), F32),
+            pltpu.VMEM((PAIRS, 2 * rows, 1), F32),
+            pltpu.VMEM((PAIRS, 2 * rows, 1), F32),
+            pltpu.VMEM((PAIRS, 2 * rows, LANES), F32),
+            pltpu.SemaphoreType.DMA((slots,)),
+            pltpu.SemaphoreType.DMA((slots,)),
+            pltpu.SemaphoreType.DMA((count + 2,)),
         ]
         + [pltpu.VMEM(share.shape, share.dtype) for share in shares],
-        compiler_params=pltpu.CompilerParams(collective_id=collective_id, has_side_effects=True),
-        name="gather_weights",
-    )(*shares)
-    return fulls
-
-
-BLOCK_COPIES = 13
-
-
-def gather_blocks_kernel(count, *refs):
-    blocks, fulls = refs[:count], refs[count : 2 * count]
-    send_sems, recv_sems, local_sems = refs[2 * count :]
-    x, z, y, core = place_bits()
-    sibling = (2 * z + x, 2 * y + 1 - core)
-    over_x = (2 * z + 1 - x, 2 * y + core)
-    over_y = (2 * z + x, 2 * (1 - y) + core)
-    greet((sibling, over_x, over_y))
-
-    plans = []
-    locals_started = []
-    for which in range(count):
-        block, full = blocks[which], fulls[which]
-        half = block.shape[0] // 2
-
-        def copy(index, src, dst, device, which=which):
-            slot = which * BLOCK_COPIES + index
-            return pltpu.make_async_remote_copy(
-                src_ref=src,
-                dst_ref=dst,
-                send_sem=send_sems.at[slot],
-                recv_sem=recv_sems.at[slot],
-                device_id=device,
-                device_id_type=MESH,
-            )
-
-        def part(ref, side, half=half):
-            return ref.at[pl.ds(side * half, half), :]
-
-        def slot_of(x_bit, y_bit, full=full):
-            return full.at[4 * y_bit + 2 * core + x_bit]
-
-        same = lambda index, view, device, copy=copy: copy(index, view, view, device)
-        mine = slot_of(x, y)
-        from_x, from_y, from_both = slot_of(1 - x, y), slot_of(x, 1 - y), slot_of(1 - x, 1 - y)
-        plan = {
-            0: copy(0, block, mine, sibling),
-            1: copy(1, part(block, 0), part(mine, 0), over_x),
-            2: copy(2, part(block, 1), part(mine, 1), over_y),
-            3: copy(3, part(block, 1), part(mine, 1), over_x),
-            4: copy(4, part(block, 0), part(mine, 0), over_y),
-            5: same(5, part(from_x, 0), over_y),
-            6: same(6, part(from_x, 0), sibling),
-            7: same(7, part(from_y, 1), over_x),
-            8: same(8, part(from_y, 1), sibling),
-            9: same(9, part(from_x, 1), sibling),
-            10: same(10, part(from_y, 0), sibling),
-            11: same(11, part(from_both, 0), sibling),
-            12: same(12, part(from_both, 1), sibling),
-        }
-        plans.append(plan)
-        for index in (1, 2, 3, 4, 0):
-            plan[index].start()
-        local = pltpu.make_async_copy(block, mine, local_sems.at[which])
-        local.start()
-        locals_started.append(local)
-
-    for plan in plans:
-        plan[1].wait_recv()
-        plan[5].start()
-        plan[6].start()
-        plan[2].wait_recv()
-        plan[7].start()
-        plan[8].start()
-    for plan in plans:
-        plan[3].wait_recv()
-        plan[9].start()
-        plan[4].wait_recv()
-        plan[10].start()
-    for plan in plans:
-        plan[5].wait_recv()
-        plan[11].start()
-        plan[7].wait_recv()
-        plan[12].start()
-    for plan in plans:
-        for index in (0, 6, 8, 9, 10, 11, 12):
-            plan[index].wait_recv()
-        for index in range(BLOCK_COPIES):
-            plan[index].wait_send()
-    for local in locals_started:
-        local.wait()
-
-
-def gather_blocks(blocks, collective_id):
-    count = len(blocks)
-    copies = count * BLOCK_COPIES
-    anywhere = pl.BlockSpec(memory_space=pl.ANY)
+        compiler_params=pltpu.CompilerParams(
+            collective_id=collective_id, has_side_effects=True, vmem_limit_bytes=40 << 20
+        ),
+        name="attend",
+    )(queries, kv_own, segs, *shares)
+
+
+class AttentionGrads:
+    def __init__(self, place, q_ref, grad_ref, lse_ref, delta_ref, segs_ref, kv_all, q_all, grad_all, stats_all, biases, sums):
+        self.place = place
+        self.q_ref, self.grad_ref, self.lse_ref, self.delta_ref = q_ref, grad_ref, lse_ref, delta_ref
+        self.segs_ref, self.kv_all, self.q_all, self.grad_all = segs_ref, kv_all, q_all, grad_all
+        self.stats_all = stats_all
+        self.query_bias, self.key_bias = biases
+        self.query_sum, self.key_sum, self.value_sum = sums
+        self.rows = q_ref.shape[0]
+
+    def masks(self):
+        rows, place = self.rows, self.place
+        start = place.block * rows
+        own_segs = own_columns(self.segs_ref, place.block)
+        for i in range(8):
+            at = slice(i * rows, (i + 1) * rows)
+            self.query_bias[:, at] = mask_block(own_segs, self.segs_ref, i, start, True)
+            self.key_bias[:, at] = mask_block(own_segs, self.segs_ref, i, start, False)
+
+    def lanes(self, pair, side=0):
+        return pl.ds(pl.multiple_of(side * D + pair * LANES, LANES), LANES)
+
+    def two_blocks(self, ref, index, lanes):
+        return ref[pl.ds(2 * index, 2), :, lanes].reshape(2 * self.rows, LANES)
+
+    def bias(self, ref, index):
+        step = 2 * self.rows
+        bias = ref[:, pl.ds(pl.multiple_of(index * step, step), step)]
+        return jnp.concatenate([bias, bias], axis=0)
+
+    def query_grads(self, first_pair, last_pair):
+        scale = jnp.asarray(SCALE, BF16)
+        count = self.place.block // 2 + 1
+
+        def visit_pair(pair, carried):
+            lanes = self.lanes(pair)
+            queries = two_heads(self.q_ref[:, lanes] * scale)
+            grads = two_heads(self.grad_ref[:, lanes])
+            lse = pick_lanes(self.lse_ref[...], pair)
+            delta = pick_lanes(self.delta_ref[...], pair)
+
+            def visit(index, total):
+                keys = self.two_blocks(self.kv_all, index, lanes)
+                values = self.two_blocks(self.kv_all, index, self.lanes(pair, 1))
+                scores = dot_rows(queries, keys) + self.bias(self.query_bias, index)
+                attention = jnp.exp(scores - lse)
+                grad_attention = dot_rows(grads, values)
+                grad_scores = (attention * (grad_attention - delta)).astype(BF16)
+                return total + jnp.dot(grad_scores, keys, preferred_element_type=F32)
+
+            zeros = jnp.zeros((2 * self.rows, LANES), F32)
+            self.query_sum[pair] = lax.fori_loop(0, count, visit, zeros)
+            return carried
+
+        lax.fori_loop(first_pair, last_pair, visit_pair, 0)
+
+    def key_grads(self, first, last, fresh):
+        rows = self.rows
+        scale = jnp.asarray(SCALE, BF16)
+        own = self.place.block
+
+        def visit_pair(pair, carried):
+            lanes = self.lanes(pair)
+            own_keys = two_heads(self.kv_all[own, :, lanes] * scale)
+            own_values = two_heads(self.kv_all[own, :, self.lanes(pair, 1)])
+
+            def stat_rows(index, row):
+                def spread(block, head):
+                    line = self.stats_all[2 * index + block, pl.ds(row + 2 * pair + head, 1), :]
+                    return jnp.broadcast_to(line, (rows, rows))
+
+                heads = [
+                    jnp.concatenate([spread(0, head), spread(1, head)], axis=1) for head in range(2)
+                ]
+                return jnp.concatenate(heads, axis=0)
+
+            def visit(index, totals):
+                key_total, value_total = totals
+                later = self.two_blocks(self.q_all, index, lanes)
+                later_grads = self.two_blocks(self.grad_all, index, lanes)
+                scores = dot_rows(own_keys, later) + self.bias(self.key_bias, index)
+                attention = jnp.exp(scores - stat_rows(index, 0))
+                grad_attention = dot_rows(own_values, later_grads)
+                grad_scores = attention * (grad_attention - stat_rows(index, 16))
+                key_total = key_total + jnp.dot(
+                    grad_scores.astype(BF16), later, preferred_element_type=F32
+                )
+                value_total = value_total + jnp.dot(
+                    attention.astype(BF16), later_grads, preferred_element_type=F32
+                )
+                return key_total, value_total
+
+            if fresh:
+                zeros = jnp.zeros((2 * rows, LANES), F32)
+                totals = (zeros, zeros)
+            else:
+                totals = (self.key_sum[pair], self.value_sum[pair])
+            self.key_sum[pair], self.value_sum[pair] = lax.fori_loop(first, last, visit, totals)
+            return carried
+
+        lax.fori_loop(0, PAIRS, visit_pair, 0)
+
+    def near_keys(self):
+        self.key_grads(self.place.block // 2, 2 * self.place.y + 2, True)
+
+    def far_keys(self):
+        @pl.when(self.place.y == 0)
+        def _():
+            self.key_grads(2, 4, False)
+
+    def store(self, out_ref):
+        def visit(pair, carried):
+            out_ref[:, self.lanes(pair)] = (one_pair(self.query_sum[pair]) * SCALE).astype(BF16)
+            out_ref[:, self.lanes(pair, 1)] = (one_pair(self.key_sum[pair]) * SCALE).astype(BF16)
+            out_ref[:, self.lanes(pair, 2)] = one_pair(self.value_sum[pair]).astype(BF16)
+            return carried
+
+        lax.fori_loop(0, PAIRS, visit, 0)
+
+
+def attention_scratch(rows):
+    return [
+        pltpu.VMEM((8, rows, 2 * D), BF16),
+        pltpu.VMEM((8, rows, D), BF16),
+        pltpu.VMEM((8, rows, D), BF16),
+        pltpu.VMEM((8, 32, rows), F32),
+        pltpu.VMEM((rows, 8 * rows), F32),
+        pltpu.VMEM((rows, 8 * rows), F32),
+        pltpu.VMEM((PAIRS, 2 * rows, LANES), F32),
+        pltpu.VMEM((PAIRS, 2 * rows, LANES), F32),
+        pltpu.VMEM((PAIRS, 2 * rows, LANES), F32),
+    ]
+
+
+ATTENTION_SCRATCH = 9
+
+
+def attend_back_kernel(
+    q_ref, grad_ref, stats_ref, lse_ref, delta_ref, segs_ref, kv_ref, out_ref, *scratch
+):
+    kv_all, q_all, grad_all, stats_all = scratch[:4]
+    biases, sums = scratch[4:6], scratch[6:9]
+    send_sems, recv_sems, local_sem = scratch[9:]
+    place = Place()
+    greet((place.sibling, place.over_x, place.over_y))
+    copies = Copies(send_sems, recv_sems)
+    gather = BlockGather(
+        place, copies, [q_ref, grad_ref, stats_ref], [q_all, grad_all, stats_all]
+    )
+    load = pltpu.make_async_copy(kv_ref, kv_all, local_sem)
+    load.start()
+    gather.begin()
+    grads = AttentionGrads(
+        place, q_ref, grad_ref, lse_ref, delta_ref, segs_ref, kv_all, q_all, grad_all, stats_all, biases, sums
+    )
+    grads.masks()
+    load.wait()
+    grads.query_grads(0, 2)
+    gather.first_halves()
+    grads.query_grads(2, PAIRS)
+    gather.second_halves()
+    gather.wait_near()
+    grads.near_keys()
+    gather.corners()
+    gather.wait_far()
+    grads.far_keys()
+    grads.store(out_ref)
+    gather.finish()
+
+
+def attend_back(queries, grads, stats, lse, delta, segs, kv, collective_id):
+    rows = queries.shape[0]
+    slots = 3 * BLOCK_COPIES
+    vmem = pl.BlockSpec(memory_space=pltpu.VMEM)
     return pl.pallas_call(
-        partial(gather_blocks_kernel, count),
-        in_specs=[pl.BlockSpec(memory_space=pltpu.VMEM)] * count,
-        out_specs=[anywhere] * count,
-        out_shape=[jax.ShapeDtypeStruct((8, *block.shape), block.dtype) for block in blocks],
-        scratch_shapes=[
-            pltpu.SemaphoreType.DMA((copies,)),
-            pltpu.SemaphoreType.DMA((copies,)),
-            pltpu.SemaphoreType.DMA((count,)),
+        attend_back_kernel,
+        in_specs=[vmem] * 6 + [pl.BlockSpec(memory_space=pl.ANY)],
+        out_specs=vmem,
+        out_shape=jax.ShapeDtypeStruct((rows, 3 * D), BF16),
+        scratch_shapes=attention_scratch(rows)
+        + [
+            pltpu.SemaphoreType.DMA((slots,)),
+            pltpu.SemaphoreType.DMA((slots,)),
+            pltpu.SemaphoreType.DMA,
         ],
-        compiler_params=pltpu.CompilerParams(collective_id=collective_id, has_side_effects=True),
-        name="gather_blocks",
-    )(*blocks)
+        compiler_params=pltpu.CompilerParams(
+            collective_id=collective_id, has_side_effects=True, vmem_limit_bytes=40 << 20
+        ),
+        name="attend_back",
+    )(queries, grads, stats, lse, delta, segs, kv)
 
 
 CHUNK_ROWS, CHUNK_COLUMNS = 192, 768
@@ -844,92 +1306,97 @@
 
 
 class PlaneLinks:
-    def __init__(self):
-        self.x, self.z, self.y, self.core = place_bits()
-        self.block = 2 * lax.axis_index("fsdp") + self.x
-        self.count = 8
-
-    def permute(self, value, target):
-        pairs = [(c * 4 + f, target(c, f)) for c in range(8) for f in range(4)]
+    def leave(self, value):
+        pairs = [(c * 4 + f, (2 * f + c % 2) * 4 + c // 2) for c in range(8) for f in range(4)]
         return lax.ppermute(value, ("ctx", "fsdp"), pairs)
 
-    def swap(self, value):
-        return self.permute(value, lambda c, f: (2 * f + c % 2) * 4 + c // 2)
-
-    enter = swap
-    leave = swap
-
-    def weights(self, shares):
-        return gather_weights(shares, 0)
-
-    def blocks(self, blocks, collective_id):
-        return gather_blocks(blocks, collective_id)
-
-    def sum_gradients(self, factors, packed):
+    def open(self, tokens, segs_row, cotangent, vectors, weight):
+        segs = jnp.broadcast_to(segs_row, (16, segs_row.shape[1]))
+        return opening(tokens, segs, cotangent, vectors, weight, 0)
+
+    def attend(self, queries, kv_own, segs, shares):
+        attended, lse, lse_rows, kv, *fulls = attend(
+            queries, kv_own, segs, shares, 1 if shares else 2
+        )
+        return attended, lse, lse_rows, kv, fulls
+
+    def attend_back(self, queries, grads, stats, lse, delta, segs, kv, kv_own):
+        return attend_back(queries, grads, stats, lse, delta, segs, kv, 3)
+
+    def sum_gradients(self, factors, vectors):
         terms = []
         for left, right in factors:
             term = column_products(left, right).astype(BF16)
             terms.append(term.reshape(4, term.shape[0] // 4, term.shape[1]))
-        *sums, vector = reduce_gradients(terms, packed.reshape(-1, LANES), 4)
-        vector = vector.reshape(packed.shape)
-        mine = lax.dynamic_index_in_dim(vector, 2 * self.y + self.core, 0, keepdims=False)
-        return [total.astype(F32) for total in sums], mine
+        *sums, vectors = reduce_gradients(terms, vectors, 4)
+        return [total.astype(F32) for total in sums], vectors
 
 
 class PlainLinks:
-    def __init__(self, ctx_size, fsdp_size):
-        self.block = lax.axis_index("ctx")
-        self.count = ctx_size
-        self.fsdp_size = fsdp_size
-
-    def enter(self, value):
+    def leave(self, value):
         return value
 
-    leave = enter
-
-    def weights(self, shares):
-        return [lax.all_gather(share, "fsdp", axis=0) for share in shares]
-
-    def blocks(self, blocks, collective_id):
-        return [lax.all_gather(block, "ctx", axis=0) for block in blocks]
-
-    def sum_gradients(self, factors, packed):
+    def open(self, tokens, segs_row, cotangent, vectors, weight):
+        segs = lax.all_gather(segs_row, "ctx", axis=1, tiled=True)
+        shares = lax.all_gather(vectors, "fsdp", axis=0)
+        vectors = assemble_vectors([shares[i] for i in range(4)])
+        return tokens, (segs_row, segs), cotangent, vectors, lax.all_gather(weight, "fsdp", axis=0)
+
+    def place(self, segs):
+        own_segs, all_segs = segs
+        rows = own_segs.shape[1]
+        start = (lax.axis_index("ctx") * rows).reshape(1).astype(jnp.int32)
+        return start, own_segs.reshape(rows, 1), all_segs
+
+    def blocks(self, block):
+        return lax.all_gather(block, "ctx", axis=0)
+
+    def attend(self, queries, kv_own, segs, shares):
+        start, own_segs, all_segs = self.place(segs)
+        kv = self.blocks(kv_own).reshape(-1, 2 * D)
+        attended, lse, lse_rows = attention_forward(start, queries, kv, own_segs, all_segs)
+        fulls = [lax.all_gather(share, "fsdp", axis=0) for share in shares]
+        return attended, lse, lse_rows, kv, fulls
+
+    def attend_back(self, queries, grads, stats, lse, delta, segs, kv, kv_own):
+        start, own_segs, all_segs = self.place(segs)
+        q_all = self.blocks(queries).reshape(-1, D)
+        grad_all = self.blocks(grads).reshape(-1, D)
+        return attention_backward(
+            start,
+            queries,
+            grads,
+            kv_own,
+            lse,
+            delta,
+            kv,
+            q_all,
+            grad_all,
+            self.blocks(stats),
+            own_segs,
+            all_segs,
+        )
+
+    def sum_gradients(self, factors, vectors):
         sums = []
         for left, right in factors:
             term = column_products(left, right).astype(BF16)
             share = lax.psum_scatter(term, "fsdp", scatter_dimension=0, tiled=True)
             sums.append(lax.psum(share.astype(F32), "ctx"))
-        share = lax.psum_scatter(packed, "fsdp", scatter_dimension=0, tiled=False)
-        return sums, lax.psum(share, "ctx")
-
-
-def layer_forward(resid, weights, links, start, own_segs, segs, layer_index):
-    (
-        gain_one,
-        bias_one,
-        weight_qkv,
-        bias_qv,
-        weight_proj,
-        bias_proj,
-        gain_two,
-        bias_two,
-        weight_fc,
-        bias_fc,
-        weight_out,
-        bias_out,
-    ) = weights
+        return sums, lax.psum(vectors, ("ctx", "fsdp"))
+
+
+def layer_forward(resid, weights, vectors, links, segs, shares):
+    gain_one, bias_one, gain_two, bias_two, bias_proj, bias_out = (vectors[i : i + 1] for i in range(6))
+    bias_qkv = jnp.concatenate([vectors[6:7], jnp.zeros((1, D), F32), vectors[7:8]], axis=1)
+    bias_fc = vectors[8:12].reshape(1, 4 * D)
     normed_one, normal_one, inverse_one = norm_forward(resid, gain_one, bias_one)
-    projected = jnp.dot(normed_one, weight_qkv, preferred_element_type=F32)
-    biases = jnp.concatenate([bias_qv[:D], jnp.zeros((D,), F32), bias_qv[D:]])
-    projected = (projected + biases).astype(BF16)
+    projected = jnp.dot(normed_one, weights[0], preferred_element_type=F32) + bias_qkv
+    projected = projected.astype(BF16)
     queries, kv_own = projected[:, :D], projected[:, D:]
-    if layer_index == 0:
-        kv, segs = links.blocks([kv_own, segs], 1)
-        segs = segs[:, 0, :].reshape(1, -1)
-    else:
-        (kv,) = links.blocks([kv_own], 2)
-    kv = kv.reshape(-1, 2 * D)
-    attended, lse, lse_rows = attention_forward(start, queries, kv, own_segs, segs)
+    attended, lse, lse_rows, kv, fulls = links.attend(queries, kv_own, segs, shares)
+    weights = weights + tuple(full.reshape(-1, full.shape[-1]) for full in fulls)
+    _, weight_proj, weight_fc, weight_out = weights
     middle = resid + jnp.dot(attended, weight_proj, preferred_element_type=F32) + bias_proj
     normed_two, normal_two, inverse_two = norm_forward(middle, gain_two, bias_two)
     hidden = jnp.dot(normed_two, weight_fc, preferred_element_type=F32) + bias_fc
@@ -951,24 +1418,12 @@
         hidden,
         activated,
     )
-    return result_rows, saved, segs
-
-
-def layer_backward(gradient, weights, saved, links, start, own_segs, segs):
-    (
-        gain_one,
-        _,
-        weight_qkv,
-        _,
-        weight_proj,
-        _,
-        gain_two,
-        _,
-        weight_fc,
-        _,
-        weight_out,
-        _,
-    ) = weights
+    return result_rows, saved, weights
+
+
+def layer_backward(gradient, weights, vectors, saved, links, segs):
+    weight_qkv, weight_proj, weight_fc, weight_out = weights
+    gain_one, gain_two = vectors[0:1], vectors[2:3]
     (
         normed_one,
         normal_one,
@@ -985,7 +1440,6 @@
         hidden,
         activated,
     ) = saved
-    rows = gradient.shape[0]
     total = lambda value: jnp.sum(value.astype(F32), axis=0)
     grad_branch = gradient.astype(BF16)
     grad_activated = dot_rows(grad_branch, weight_out)
@@ -1011,20 +1465,8 @@
         preferred_element_type=F32,
     )
     stats = jnp.concatenate([lse_rows, delta_rows], axis=0)
-    q_all, grad_all, stats = links.blocks([queries, grad_attended, stats], 3)
-    grad_projected = attention_backward(
-        start,
-        queries,
-        grad_attended,
-        kv_own,
-        lse,
-        delta,
-        kv,
-        q_all.reshape(-1, D),
-        grad_all.reshape(-1, D),
-        stats,
-        own_segs,
-        segs,
+    grad_projected = links.attend_back(
+        queries, grad_attended, stats, lse, delta, segs, kv, kv_own
     )
     grad_normed_one = dot_rows(grad_projected, weight_qkv)
     grad_in_one, grad_gain_one, grad_bias_one = norm_backward(
@@ -1037,21 +1479,22 @@
         (attended, grad_proj),
         (normed_one, grad_projected),
     )
-    vectors = (
+    terms = (
         grad_gain_one,
         grad_bias_one,
-        jnp.concatenate([total(grad_projected[:, :D]), total(grad_projected[:, 2 * D :])]),
-        total(grad_proj),
         grad_gain_two,
         grad_bias_two,
-        total(grad_hidden),
+        total(grad_proj),
         total(grad_branch),
-    )
-    return grad_input, matrices, vectors
+        total(grad_projected[:, :D]),
+        total(grad_projected[:, 2 * D :]),
+        total(grad_hidden).reshape(4, D),
+    )
+    return grad_input, matrices, terms
 
 
 def body(
-    links_of,
+    links,
     tokens,
     segment_ids,
     ln1_gain,
@@ -1068,59 +1511,26 @@
     out_bias,
     out_cotangent,
 ):
-    members, seq_dev, features = tokens.shape
-    links = links_of()
-    start = (links.block * seq_dev).reshape(1).astype(jnp.int32)
-    resid = links.enter(tokens[0])
-    segs_row = links.enter(segment_ids)
-    gradient = links.enter(out_cotangent[0])
-    own_segs = segs_row.reshape(seq_dev, 1)
-    segs = jnp.broadcast_to(segs_row, (16, seq_dev))
-
-    vectors = (ln1_gain, ln1_bias, attn_bias, proj_bias, ln2_gain, ln2_bias, fc_bias, out_bias)
-    sizes = [vector.shape[0] for vector in vectors]
-    packed = jnp.concatenate(vectors)
-    padding = -packed.shape[0] % (64 * 2 * LANES)
-    packed = jnp.pad(packed, (0, padding)).reshape(-1, 2 * LANES)
-    qkv_full, packed, proj_full, fc_full, out_full = links.weights(
-        [attn_weight, packed, proj_weight, fc_weight, out_weight]
-    )
-    matrix = lambda full: full.reshape(-1, full.shape[-1])
-    packed = packed.reshape(packed.shape[0], -1).astype(F32)
-    pieces = []
-    offset = 0
-    for size in sizes:
-        pieces.append(packed[:, offset : offset + size].reshape(-1))
-        offset += size
-    gain_one, bias_one, bias_qv, bias_proj, gain_two, bias_two, bias_fc, bias_out = pieces
-    weights = (
-        gain_one,
-        bias_one,
-        matrix(qkv_full),
-        bias_qv,
-        matrix(proj_full),
-        bias_proj,
-        gain_two,
-        bias_two,
-        matrix(fc_full),
-        bias_fc,
-        matrix(out_full),
-        bias_out,
-    )
-
+    vectors = pack_vectors(
+        ln1_gain, ln1_bias, ln2_gain, ln2_bias, proj_bias, out_bias, attn_bias, fc_bias
+    )
+    resid, segs, gradient, vectors, qkv_full = links.open(
+        tokens[0], segment_ids, out_cotangent[0], vectors, attn_weight
+    )
+    weights = (qkv_full.reshape(-1, qkv_full.shape[-1]),)
+    shares = [proj_weight, fc_weight, out_weight]
     resid = resid.astype(F32)
     saved_layers = []
     for layer_index in range(2):
-        resid, saved, segs = layer_forward(
-            resid, weights, links, start, own_segs, segs, layer_index
-        )
+        resid, saved, weights = layer_forward(resid, weights, vectors, links, segs, shares)
         saved_layers.append(saved)
+        shares = []
     output = links.leave(resid.astype(BF16))
     gradient = gradient.astype(F32)
     collected = []
     for layer_index in (1, 0):
         gradient, matrices, terms = layer_backward(
-            gradient, weights, saved_layers[layer_index], links, start, own_segs, segs
+            gradient, weights, vectors, saved_layers[layer_index], links, segs
         )
         collected.append((matrices, terms))
     tokens_grad = links.leave(gradient.astype(BF16))
@@ -1130,42 +1540,35 @@
         left = jnp.concatenate([second[0], first[0]], axis=0)
         right = jnp.concatenate([second[1], first[1]], axis=0)
         factors.append((left, right))
-    shares = packed.shape[0]
-    added = [a + b for a, b in zip(collected[0][1], collected[1][1])]
-    rows = jnp.concatenate([vector.reshape(shares, -1) for vector in added], axis=1)
-    sums, summed = links.sum_gradients(factors, rows.reshape(shares, -1, LANES))
-    out_grad, fc_grad, proj_grad, qkv_grad = sums
-    summed = summed.reshape(-1)
-    small = []
-    offset = 0
-    for size in sizes:
-        small.append(summed[offset : offset + size])
-        offset += size
-    g_gain_one, g_bias_one, g_bias_qv, g_bias_proj, g_gain_two, g_bias_two, g_bias_fc, g_bias_out = small
+    added = [(a + b).reshape(-1, D) for a, b in zip(collected[0][1], collected[1][1])]
+    packed = jnp.concatenate(added + [jnp.zeros((4, D), F32)], axis=0)
+    (out_grad, fc_grad, proj_grad, qkv_grad), summed = links.sum_gradients(factors, packed)
+    own = lax.axis_index("fsdp")
+    pick = lambda value, axis: lax.dynamic_index_in_dim(value, own, axis, keepdims=False)
+    small = pick(summed[:6].reshape(6, 4, -1), 1)
+    bias_qv = pick(summed[6:8].reshape(4, -1), 0)
+    bias_fc = pick(summed[8:12], 0)
+    gain_one, bias_one, gain_two, bias_two, bias_proj, bias_out = (small[i] for i in range(6))
     return (
         output[None],
         tokens_grad[None],
-        g_gain_one,
-        g_bias_one,
+        gain_one,
+        bias_one,
         qkv_grad,
-        g_bias_qv,
+        bias_qv,
         proj_grad,
-        g_bias_proj,
-        g_gain_two,
-        g_bias_two,
+        bias_proj,
+        gain_two,
+        bias_two,
         fc_grad,
-        g_bias_fc,
+        bias_fc,
         out_grad,
-        g_bias_out,
+        bias_out,
     )
 
 
 def solution(mesh):
-    ctx_size, fsdp_size = mesh.shape["ctx"], mesh.shape["fsdp"]
-    if (ctx_size, fsdp_size) == (8, 4):
-        links_of = PlaneLinks
-    else:
-        links_of = partial(PlainLinks, ctx_size, fsdp_size)
+    links = PlaneLinks() if (mesh.shape["ctx"], mesh.shape["fsdp"]) == (8, 4) else PlainLinks()
     rows = P("fsdp", "ctx", None)
     vector, matrix = P("fsdp"), P("fsdp", None)
     in_specs = (
@@ -1202,5 +1605,5 @@
         vector,
     )
     return jax.shard_map(
-        partial(body, links_of), mesh=mesh, in_specs=in_specs, out_specs=out_specs, check_vma=False
-    )
+        partial(body, links), mesh=mesh, in_specs=in_specs, out_specs=out_specs, check_vma=False
+    )

time: 405 us -> 342 us (0.84)
  local copies, waits for them, and re-layouts: 42.7 us -> 22.6 us
  matrix products: 49.9 us -> 35.3 us
  Pallas kernels: 283 us -> 269 us
  starting transfers between devices: 10.6 us -> 1.61 us
    pallas_call x9 -> x5, Pallas kernels: 172 us -> 154 us  [the longest x2 66.6 us: attend(): pl.pallas_call(partial(attend_kernel, count), in_specs=[vmem, vmem, vmem]...]
    unnamed x231 -> x132, local copies, waits for them, and re-layouts: 26.8 us -> 11.8 us
    ppermute x5 -> x2, starting transfers between devices: 10.6 us -> 1.61 us  [leave(): return lax.ppermute(value, ('ctx', 'fsdp'), pairs)]
    concatenate x6 -> x2, local copies, waits for them, and re-layouts: 5.6 us -> 0.09 us  [the longest x1 0.08 us: body(): packed = jnp.concatenate(added + [jnp.zeros((4, D), F32)], axis=0)]
    pad x1 -> x7, local copies, waits for them, and re-layouts: 0.01 us -> 4.64 us  [pack_vectors(): jnp.pad(row.astype(F32), (0, D - row.shape[0]))]
    dot_general x8, matrix products: 16.9 us -> 12.6 us  [dot_rows(): lax.dot_general(left, right, (((1,), (1,)), ((), ())), preferred_element_...]
    pallas_call x1, Pallas kernels: 112 us -> 116 us  [reduce_gradients(): pl.pallas_call(partial(reduce_gradients_kernel, places, count), in_specs=...]
  transfers between devices with their start and end apart: 5 -> 2, of which waited for: 0 -> 0; matrix products, arithmetic and copies ran while one was open for 11% -> 6% of each run, Pallas kernels for 53% -> 34%
where the time goes in v3:
time: 342 us
  Pallas kernels  269 us (79%)
  matrix products  35.3 us (10%)
  local copies, waits for them, and re-layouts  22.6 us (7%)
  other arithmetic  11.4 us (3%)
    pallas_call x1, Pallas kernels, reduce_gradients(): pl.pallas_call(partial(reduce_gradients_kernel, places, count), in_specs=...  116 us
    pallas_call x2, Pallas kernels, attend(): pl.pallas_call(partial(attend_kernel, count), in_specs=[vmem, vmem, vmem]...  66.6 us
    pallas_call x2, Pallas kernels, attend_back(): pl.pallas_call(attend_back_kernel, in_specs=[vmem] * 6 + [pl.BlockSpec(me...  53.8 us
    pallas_call x1, Pallas kernels, opening(): pl.pallas_call(opening_kernel, in_specs=[vmem, vmem, vmem, vmem, anywhere...  33.1 us
    dot_general x8, matrix products, dot_rows(): lax.dot_general(left, right, (((1,), (1,)), ((), ())), preferred_element_...  12.6 us
    unnamed x132, local copies, waits for them, and re-layouts  11.8 us
    dot_general x4, matrix products, column_products(): lax.dot_general(left, right, (((0,), (0,)), ((), ())), preferred_element_...  10.6 us
  transfers between devices with their start and end apart: 2, of which 0 were waited for; matrix products, arithmetic and copies ran while one was open for 6% of the time, Pallas kernels for 34%

profile of v3, /device:TPU:0, one launch (start us, length us, event | category | flops | bytes accessed | tf_op | source)
XLA Modules:
  0.0 341.9 jit_solution(1850249692390398200)
XLA Ops:
  0.6 0.7 pad.30
  1.3 0.7 pad.31
  2.0 0.7 pad.32
  2.7 0.7 pad.33
  3.3 0.7 pad.34
  4.0 0.7 pad.35
  4.7 0.7 pad.36
  5.3 0.7 stack.44
  6.8 1.2 copy-done.13
  7.9 0.9 copy-done.22
  8.8 0.9 copy-done.23
  9.8 33.1 %opening.1 = (bf16[128,768]{1,0:T(8,128)(2,1)S(1)}, s32[8,16,128]{2,1,0:T(8,128)S(1)}, bf16[128,768]{1,0:T(8,128)(2,1)S(1)}, f32[16,768]{1,0:T(8,128)S(1)}, bf16[4,192,2304]{2,1,0:T(8,128)(2,1)S(1)}) custom-call(bf16[128,768]{1,0:T(8,128)(2,1)S(1)} %bitcast.66, s32[16,128]{1,0:T(8,128)S(1)} %broadcast_in_dim.11.segs_ref, bf16[128,768]{1,0:T(8,128)(2,1)S(1)} %bitcast.67, ...), custom_call_target="tpu_custom_call" | custom-call | tf_op jit(solution)/shard_map/opening/pallas_call | solution.py:657
  45.6 0.8 copy-done.9
  46.4 46.2 %attend.2 = (bf16[128,768]{1,0:T(8,128)(2,1)S(1)}, f32[128,128]{1,0:T(8,128)S(1)}, f32[16,128]{1,0:T(8,128)S(1)}, bf16[8,128,1536]{2,1,0:T(8,128)(2,1)S(1)}, bf1...) custom-call(bf16[128,768]{1,0:T(8,128)(2,1)S(1)} %slice.123.refs_0_.q_ref, ...), custom_call_target="tpu_custom_call" | custom-call | tf_op jit(solution)/shard_map/attend/pallas_call | solution.py:807
  92.6 2.1 copy-done
  94.7 1.6 copy-done.5
  96.3 1.0 copy-done.1
  97.8 0.7 copy-done.26
  99.2 1.3 add.326
  100.5 1.3 add_convert_fusion.2
  101.9 4.9 %multiply_convert_fusion.1 = (bf16[128,3072]{1,0:T(8,128)(2,1)S(1)}, f32[128,3072]{1,0:T(8,128)}) fusion(f32[3072]{0:T(1024)} %add.326, bf16[128,768]{1,0:T(8,128)(2,1)S(1)} %add_convert_fusion.2, bf16[768,3072]{1,0:T(8,128)(2,1)} %bitcast.55), kind=kOutput, calls=%fused_computation.36 | convolution fusion | flops 607911936 | bytes 7286784 | tf_op jit(solution)/shard_map/dot_general | solution.py:1402
  106.8 0.9 fusion.82
  108.9 20.4 %attend.3 = (bf16[128,768]{1,0:T(8,128)(2,1)S(1)}, f32[128,128]{1,0:T(8,128)S(1)}, f32[16,128]{1,0:T(8,128)S(1)}, bf16[8,128,1536]{2,1,0:T(8,128)(2,1)S(1)}) custom-call(bf16[128,768]{1,0:T(8,128)(2,1)S(1)} %slice.125.refs_0_.q_ref, bf16[128,1536]{1,0:T(8,128)(2,1)S(1)} %slice.126.refs_1_, s32[8,16,128]{2,1,0:T(8,128)S(1)} %copy-done.12), custom_call_target="tpu_custom_call" | custom-call | tf_op jit(solution)/shard_map/attend/pallas_call | solution.py:807
  130.3 1.6 fusion.84
  132.0 2.0 convert_reduce_fusion.1
  134.0 2.3 multiply_reduce_fusion.1
  136.3 0.8 convert_reduce_fusion.10
  138.5 28.9 %attend_back.2 = bf16[128,2304]{1,0:T(8,128)(2,1)S(1)} custom-call(bf16[128,768]{1,0:T(8,128)(2,1)S(1)} %slice.125.refs_0_.q_ref, bf16[128,768]{1,0:T(8,128)(2,1)S(1)} %convolution_convert_fusion.5.grad_ref, f32[32,128]{1,0:T(8,128)S(1)} %pad_maximum_fusion.stats_ref, f32[128,128]{1,0:T(8,128)S(1)} %get-tuple-element.46.lse_ref, ...), custom_call_target="tpu_custom_call" | custom-call | tf_op jit(solution)/shard_map/attend_back/pallas_call | solution.py:1011
  167.4 1.9 multiply_reduce_fusion.2
  169.3 0.8 convert_reduce_fusion.8
  170.8 2.0 convert_reduce_fusion
  172.7 2.3 multiply_reduce_fusion
  175.1 0.8 convert_reduce_fusion.9
  177.3 24.9 %attend_back.3 = bf16[128,2304]{1,0:T(8,128)(2,1)S(1)} custom-call(bf16[128,768]{1,0:T(8,128)(2,1)S(1)} %copy-done.8, bf16[128,768]{1,0:T(8,128)(2,1)S(1)} %convolution_convert_fusion.4.grad_ref, f32[32,128]{1,0:T(8,128)S(1)} %pad_maximum_fusion.1.stats_ref, f32[128,128]{1,0:T(8,128)S(1)} %copy-done.25, f32[128,128]{1,0:T(8,128)S(1)} %fusion.60.delta_ref, ...), custom_call_target="tpu_custom_call" | custom-call | tf_op jit(solution)/shard_map/attend_back/pallas_call | solution.py:1011
  202.2 1.4 fusion.43
  203.8 0.7 collective-permute-start.1
  204.5 0.8 fusion.29
  205.3 0.9 collective-permute-start
  206.4 2.9 convolution_convert_fusion
  209.4 3.6 %convolution_convert_fusion.1 = bf16[768,3072]{1,0:T(8,128)(2,1)} fusion(bf16[128,3072]{1,0:T(8,128)(2,1)S(1)} %get-tuple-element.83, bf16[128,3072]{1,0:T(8,128)(2,1)S(1)} %get-tuple-element.85, bf16[128,768]{1,0:T(8,128)(2,1)S(1)} %add_convert_fusion.2, bf16[128,768]{1,0:T(8,128)(2,1)S(1)} %add_convert_fusion), kind=kOutput, calls=%fused_computation.1 | convolution fusion | flops 1214251008 | bytes 6684672 | tf_op jit(solution)/shard_map/dot_general | solution.py:59
  213.1 3.6 %convolution_convert_fusion.2 = bf16[3072,768]{1,0:T(8,128)(2,1)} fusion(bf16[128,3072]{1,0:T(8,128)(2,1)S(1)} %get-tuple-element.113, bf16[128,3072]{1,0:T(8,128)(2,1)S(1)} %get-tuple-element.95, bf16[128,768]{1,0:T(8,128)(2,1)S(1)} %get-tuple-element.87, bf16[128,768]{1,0:T(8,128)(2,1)S(1)} %copy-done.15), kind=kOutput, calls=%fused_computation.2 | convolution fusion | flops 1214251008 | bytes 6684672 | tf_op jit(solution)/shard_map/dot_general | solution.py:59
  217.6 115.6 %reduce_gradients.1 = (bf16[768,768]{1,0:T(8,128)(2,1)S(1)}, bf16[192,3072]{1,0:T(8,128)(2,1)S(1)}, bf16[192,768]{1,0:T(8,128)(2,1)S(1)}, bf16[192,2304]{1,0:T(8,128)(2,1)S(1)}, f32[16,768]{1,0:T(8,128)S(1)}) custom-call(bf16[4,768,768]{2,1,0:T(8,128)(2,1)} %bitcast.76, bf16[4,192,3072]{2,1,0:T(8,128)(2,1)} %bitcast.74, bf16[4,192,768]{2,1,0:T(8,128)(2,1)S(1)} %bitcast.65, ...), custom_call_target="tpu_custom_call" | custom-call | tf_op jit(solution)/shard_map/reduce_gradients/pallas_call | solution.py:1288
  333.3 1.7 convert_element_type.181
  334.9 1.6 convert_element_type.182
  336.5 1.3 convert_element_type.179
  337.8 0.9 convert_element_type.180
  340.6 0.7 copy.31
  341.3 0.7 copy.32
  (213 shorter events, 12.9 us)
Async XLA Ops:
  42.9 2.0 copy-start.14
  42.9 2.7 copy-start.11
  42.9 53.4 %copy-start.3 = (bf16[128,768]{1,0:T(8,128)(2,1)}, bf16[128,768]{1,0:T(8,128)(2,1)S(1)}, u32[]{:S(2)}) copy-start(bf16[128,768]{1,0:T(8,128)(2,1)S(1)} %get-tuple-element.35) | copy-start | bytes 589828
  43.0 1.8 copy-start.53
  43.3 1.6 copy-start.57
  43.9 52.4 %copy-start.37 = (f32[768]{0:T(1024)}, f32[768]{0:T(1024)S(1)}, u32[]{:S(2)}) copy-start(f32[768]{0:T(1024)S(1)} %get-tuple-element.101) | copy-start | bytes 9220
  44.2 1.4 copy-start.10
  44.9 1.5 copy-start.9
  44.9 47.6 %copy-start.7 = (bf16[128,768]{1,0:T(8,128)(2,1)}, bf16[128,768]{1,0:T(8,128)(2,1)S(1)}, u32[]{:S(2)}) copy-start(bf16[128,768]{1,0:T(8,128)(2,1)S(1)} %slice.123.refs_0_.q_ref) | copy-start | bytes 589828
  92.6 2.1 copy-start
  94.7 1.6 copy-start.5
  96.3 1.4 copy-start.16
  96.3 1.5 copy-start.24
  100.5 6.2 %slice-start.2 = ((s8[4718592]{0:T(1024)(128)(4,1)}), s8[4194304]{0:T(1024)(128)(4,1)S(1)}, s32[]{:S(2)}) async-start(s8[4718592]{0:T(1024)(128)(4,1)} %bitcast.68), calls=%async_computation.2 | async-start | bytes 8388608
  101.8 4.9 %slice-start.3 = ((s8[4718592]{0:T(1024)(128)(4,1)}), s8[524288]{0:T(1024)(128)(4,1)S(1)}, s32[]{:S(2)}) async-start(s8[4718592]{0:T(1024)(128)(4,1)} %bitcast.68), calls=%async_computation.3 | async-start | bytes 1048576
  101.9 4.9 %copy-start.27 = (f32[128,768]{1,0:T(8,128)S(1)}, f32[128,768]{1,0:T(8,128)}, u32[]{:S(2)}) copy-start(f32[128,768]{1,0:T(8,128)} %copy-done.26) | copy-start | bytes 1179652
  101.9 4.9 %copy-start.41 = (f32[768]{0:T(1024)S(1)}, f32[768]{0:T(1024)}, u32[]{:S(2)}) copy-start(f32[768]{0:T(1024)} %get-tuple-element.104) | copy-start | bytes 9220
  108.1 23.9 %slice-start = ((s8[4718592]{0:T(1024)(128)(4,1)}), s8[4194304]{0:T(1024)(128)(4,1)S(1)}, s32[]{:S(2)}) async-start(s8[4718592]{0:T(1024)(128)(4,1)} %bitcast.56), calls=%async_computation | async-start | bytes 8388608
  108.7 20.6 %copy-start.2 = (bf16[4,192,768]{2,1,0:T(8,128)(2,1)S(1)}, bf16[4,192,768]{2,1,0:T(8,128)(2,1)}, u32[]{:S(2)}) copy-start(bf16[4,192,768]{2,1,0:T(8,128)(2,1)} %copy-done.1) | copy-start | bytes 3538948
  108.7 20.6 %copy-start.38 = (f32[768]{0:T(1024)S(1)}, f32[768]{0:T(1024)}, u32[]{:S(2)}) copy-start(f32[768]{0:T(1024)} %copy-done.37) | copy-start | bytes 9220
  108.9 21.1 %copy-start.36 = (f32[768]{0:T(1024)S(1)}, f32[768]{0:T(1024)}, u32[]{:S(2)}) copy-start(f32[768]{0:T(1024)} %get-tuple-element.103) | copy-start | bytes 9220
  129.3 8.8 %copy-start.19 = (bf16[128,768]{1,0:T(8,128)(2,1)}, bf16[128,768]{1,0:T(8,128)(2,1)S(1)}, u32[]{:S(2)}) copy-start(bf16[128,768]{1,0:T(8,128)(2,1)S(1)} %get-tuple-element.43) | copy-start | bytes 589828
  129.4 2.6 slice-start.1
  130.3 1.6 copy-start.52
  170.7 2.0 copy-start.56
  170.7 2.0 copy-start.59
  175.1 2.2 copy-start.6
  175.9 26.3 %copy-start.32 = (bf16[128,768]{1,0:T(8,128)(2,1)}, bf16[128,768]{1,0:T(8,128)(2,1)S(1)}, u32[]{:S(2)}) copy-start(bf16[128,768]{1,0:T(8,128)(2,1)S(1)} %get-tuple-element.90) | copy-start | bytes 589828
  177.3 24.9 %copy-start.4 = (bf16[128,768]{1,0:T(8,128)(2,1)S(1)}, bf16[128,768]{1,0:T(8,128)(2,1)}, u32[]{:S(2)}) copy-start(bf16[128,768]{1,0:T(8,128)(2,1)} %copy-done.3) | copy-start | bytes 589828
  177.3 24.9 %copy-start.54 = (f32[128]{0:T(128)S(1)}, f32[128]{0:T(128)}, u32[]{:S(2)}) copy-start(f32[128]{0:T(128)} %copy-done.53) | copy-start | bytes 1540
  177.3 25.0 %copy-start.58 = (f32[128]{0:T(128)S(1)}, f32[128]{0:T(128)}, u32[]{:S(2)}) copy-start(f32[128]{0:T(128)} %copy-done.57) | copy-start | bytes 1540
  203.8 136.7 %collective-permute-start.1 = (bf16[128,768]{1,0:T(8,128)(2,1)S(1)}, bf16[128,768]{1,0:T(8,128)(2,1)S(1)}, u32[]{:S(2)}, u32[]{:S(2)}) collective-permute-start(bf16[128,768]{1,0:T(8,128)(2,1)S(1)} %fusion.42), channel_id=1, source_target_pairs={{0,0},{1,8},{2,16},{3,24},{4,4},{5,12},{6,20},{7,28},{8,1},{9,9},{... | collective-permute-start | bytes 589832 | tf_op jit(solution)/shard_map/ppermute | solution.py:1311
  204.5 1.9 copy-start.29
  205.3 135.2 %collective-permute-start = (bf16[128,768]{1,0:T(8,128)(2,1)S(1)}, bf16[128,768]{1,0:T(8,128)(2,1)S(1)}, u32[]{:S(2)}, u32[]{:S(2)}) collective-permute-start(bf16[128,768]{1,0:T(8,128)(2,1)S(1)} %fusion.29), channel_id=1, source_target_pairs={{0,0},{1,8},{2,16},{3,24},{4,4},{5,12},{6,20},{7,28},{8,1},{9,9},{... | collective-permute-start | bytes 589832 | tf_op jit(solution)/shard_map/ppermute | solution.py:1311
  212.9 3.8 %copy-start.45 = (f32[768]{0:T(1024)S(1)}, f32[768]{0:T(1024)}, u32[]{:S(2)}) copy-start(f32[768]{0:T(1024)} %get-tuple-element.96) | copy-start | bytes 9220
  213.0 3.8 %copy-start.47 = (f32[768]{0:T(1024)S(1)}, f32[768]{0:T(1024)}, u32[]{:S(2)}) copy-start(f32[768]{0:T(1024)} %get-tuple-element.86) | copy-start | bytes 9220
  213.0 3.8 %copy-start.44 = (f32[768]{0:T(1024)S(1)}, f32[768]{0:T(1024)}, u32[]{:S(2)}) copy-start(f32[768]{0:T(1024)} %get-tuple-element.92) | copy-start | bytes 9220
  213.0 3.8 %copy-start.49 = (f32[768]{0:T(1024)S(1)}, f32[768]{0:T(1024)}, u32[]{:S(2)}) copy-start(f32[768]{0:T(1024)} %get-tuple-element.89) | copy-start | bytes 9220
  213.0 3.8 %copy-start.43 = (f32[768]{0:T(1024)S(1)}, f32[768]{0:T(1024)}, u32[]{:S(2)}) copy-start(f32[768]{0:T(1024)} %get-tuple-element.73) | copy-start | bytes 9220
  213.0 3.8 %copy-start.48 = (f32[768]{0:T(1024)S(1)}, f32[768]{0:T(1024)}, u32[]{:S(2)}) copy-start(f32[768]{0:T(1024)} %get-tuple-element.72) | copy-start | bytes 9220
  213.0 3.9 %copy-start.42 = (f32[768]{0:T(1024)S(1)}, f32[768]{0:T(1024)}, u32[]{:S(2)}) copy-start(f32[768]{0:T(1024)} %get-tuple-element.58) | copy-start | bytes 9220
  213.0 3.9 %copy-start.46 = (f32[768]{0:T(1024)S(1)}, f32[768]{0:T(1024)}, u32[]{:S(2)}) copy-start(f32[768]{0:T(1024)} %get-tuple-element.56) | copy-start | bytes 9220
  213.0 3.9 %copy-start.51 = (f32[768]{0:T(1024)S(1)}, f32[768]{0:T(1024)}, u32[]{:S(2)}) copy-start(f32[768]{0:T(1024)} %get-tuple-element.75) | copy-start | bytes 9220
  213.0 3.9 %copy-start.50 = (f32[768]{0:T(1024)S(1)}, f32[768]{0:T(1024)}, u32[]{:S(2)}) copy-start(f32[768]{0:T(1024)} %get-tuple-element.60) | copy-start | bytes 9220
  213.0 4.0 %copy-start.18 = (bf16[128,768]{1,0:T(8,128)(2,1)S(1)}, bf16[128,768]{1,0:T(8,128)(2,1)}, u32[]{:S(2)}) copy-start(bf16[128,768]{1,0:T(8,128)(2,1)} %copy-done.16) | copy-start | bytes 589828
  213.0 4.0 %copy-start.20 = (bf16[128,768]{1,0:T(8,128)(2,1)S(1)}, bf16[128,768]{1,0:T(8,128)(2,1)}, u32[]{:S(2)}) copy-start(bf16[128,768]{1,0:T(8,128)(2,1)} %copy-done.19) | copy-start | bytes 589828
  213.0 4.0 %copy-start.31 = (bf16[128,768]{1,0:T(8,128)(2,1)S(1)}, bf16[128,768]{1,0:T(8,128)(2,1)}, u32[]{:S(2)}) copy-start(bf16[128,768]{1,0:T(8,128)(2,1)} %copy-done.30) | copy-start | bytes 589828
  213.1 4.0 %copy-start.33 = (bf16[128,768]{1,0:T(8,128)(2,1)S(1)}, bf16[128,768]{1,0:T(8,128)(2,1)}, u32[]{:S(2)}) copy-start(bf16[128,768]{1,0:T(8,128)(2,1)} %copy-done.32) | copy-start | bytes 589828
  (19 other events, 20.7 us)

commit v4 on v3

--- a/solution.py
+++ b/solution.py
@@ -166,7 +166,7 @@
             jax.ShapeDtypeStruct((16, rows), F32),
         ],
         scratch_shapes=[pltpu.VMEM((rows, keys), F32)],
-        compiler_params=pltpu.CompilerParams(vmem_limit_bytes=40 << 20),
+        compiler_params=pltpu.CompilerParams(vmem_limit_bytes=60 << 20),
         cost_estimate=pl.CostEstimate(
             flops=8 * rows * keys * D, bytes_accessed=4 * keys * D, transcendentals=rows * keys * HEADS
         ),
@@ -294,7 +294,7 @@
         out_specs=whole((rows, 3 * D)),
         out_shape=jax.ShapeDtypeStruct((rows, 3 * D), BF16),
         scratch_shapes=[pltpu.VMEM((rows, tokens), F32), pltpu.VMEM((rows, tokens), F32)],
-        compiler_params=pltpu.CompilerParams(vmem_limit_bytes=44 << 20),
+        compiler_params=pltpu.CompilerParams(vmem_limit_bytes=60 << 20),
         cost_estimate=pl.CostEstimate(
             flops=16 * rows * tokens * D,
             bytes_accessed=8 * tokens * D,
@@ -367,6 +367,13 @@
 WEIGHT_COPIES = 11
 
 
+def weight_cuts(shape):
+    rows, columns = shape
+    if rows * columns <= 192 * 768:
+        return [(0, columns)]
+    return [(0, columns // 2), (columns // 2, columns // 2)]
+
+
 class WeightGather:
     def __init__(self, place, copies, shares, fulls, stages, local_sems):
         x, low = place.x, place.low
@@ -374,35 +381,40 @@
         self.plans = []
         self.locals = []
         for which, (share, full) in enumerate(zip(shares, fulls)):
-            rows, columns = share.shape
-            part, half = rows // 4, columns // 2
-
-            def piece(ref, x_bit, low_bit, part=part):
-                return ref.at[pl.ds((2 * low_bit + x_bit) * part, part), :]
-
-            def side(ref, x_bit, low_bit, index, part=part, half=half):
-                place_of = pl.ds((2 * low_bit + x_bit) * part, part)
-                return ref.at[place_of, pl.ds(index * half, half)]
-
-            theirs = full.at[other]
-            same = lambda view, device: copies.make(view, view, device)
-            mine = piece(theirs, x, low)
-            from_x, from_z = piece(theirs, 1 - x, low), piece(theirs, x, 1 - low)
-            self.plans.append(
-                [
-                    copies.make(piece(share, x, low), piece(full.at[own], x, low), place.over_y),
-                    same(mine, place.over_x),
-                    same(mine, place.over_z),
-                    same(mine, place.sibling),
-                    same(side(theirs, 1 - x, low, 0), place.over_z),
-                    same(from_x, place.sibling),
-                    same(side(theirs, x, 1 - low, 1), place.over_x),
-                    same(from_z, place.sibling),
-                    same(side(theirs, 1 - x, 1 - low, 0), place.sibling),
-                    same(side(theirs, 1 - x, 1 - low, 1), place.sibling),
-                    copies.make(share, full.at[own], place.sibling),
-                ]
-            )
+            part = share.shape[0] // 4
+            for first, width in weight_cuts(share.shape):
+                columns = pl.ds(first, width)
+
+                def piece(ref, x_bit, low_bit, part=part, columns=columns):
+                    return ref.at[pl.ds((2 * low_bit + x_bit) * part, part), columns]
+
+                def side(ref, x_bit, low_bit, index, part=part, first=first, width=width):
+                    start = (2 * low_bit + x_bit) * part
+                    if part % 32 == 0:
+                        rows = pl.ds(start + index * (part // 2), part // 2)
+                        return ref.at[rows, pl.ds(first, width)]
+                    half = width // 2
+                    return ref.at[pl.ds(start, part), pl.ds(first + index * half, half)]
+
+                theirs = full.at[other]
+                same = lambda view, device: copies.make(view, view, device)
+                mine = piece(theirs, x, low)
+                from_x, from_z = piece(theirs, 1 - x, low), piece(theirs, x, 1 - low)
+                self.plans.append(
+                    [
+                        copies.make(piece(share, x, low), piece(full.at[own], x, low), place.over_y),
+                        same(mine, place.over_x),
+                        same(mine, place.over_z),
+                        same(mine, place.sibling),
+                        same(side(theirs, 1 - x, low, 0), place.over_z),
+                        same(from_x, place.sibling),
+                        same(side(theirs, x, 1 - low, 1), place.over_x),
+                        same(from_z, place.sibling),
+                        same(side(theirs, 1 - x, 1 - low, 0), place.sibling),
+                        same(side(theirs, 1 - x, 1 - low, 1), place.sibling),
+                        copies.make(share.at[:, columns], full.at[own, :, columns], place.sibling),
+                    ]
+                )
             sem = local_sems.at[which]
             self.locals.append(
                 (
@@ -412,9 +424,11 @@
             )
 
     def begin(self):
-        for plan, (into, _) in zip(self.plans, self.locals):
+        for plan in self.plans:
             plan[0].start()
+        for plan in self.plans:
             plan[10].start()
+        for into, _ in self.locals:
             into.start()
 
     def keep_own(self):
@@ -539,100 +553,7 @@
                 copy.wait_send()
 
 
-def opening_kernel(
-    tokens_ref,
-    segs_ref,
-    cotangent_ref,
-    vectors_ref,
-    weight_ref,
-    tokens_out,
-    segs_out,
-    cotangent_out,
-    vectors_out,
-    weight_out,
-    vectors_all,
-    segs_own,
-    stage,
-    send_sems,
-    recv_sems,
-    local_sems,
-):
-    place = Place()
-    others = (place.sibling, place.over_x, place.over_y, place.over_z)
-    barrier = pltpu.get_barrier_semaphore()
-    for device in others:
-        pl.semaphore_signal(barrier, inc=1, device_id=device, device_id_type=MESH)
-
-    @pl.when(place.has_partner)
-    def _():
-        pl.semaphore_signal(barrier, inc=1, device_id=place.partner, device_id_type=MESH)
-        pl.semaphore_wait(barrier, len(others) + 1)
-
-    @pl.when(jnp.logical_not(place.has_partner))
-    def _():
-        pl.semaphore_wait(barrier, len(others))
-
-    copies = Copies(send_sems, recv_sems)
-    swaps = [
-        copies.make(segs_ref, segs_own, place.partner),
-        copies.make(tokens_ref, tokens_out, place.partner),
-        copies.make(cotangent_ref, cotangent_out, place.partner),
-    ]
-    own, other = place.fsdp, 2 * (1 - place.y) + place.core
-    vector_copies = [
-        copies.make(vectors_ref, vectors_all.at[own], place.over_y),
-        copies.make(vectors_ref, vectors_all.at[own], place.sibling),
-        copies.make(vectors_all.at[other], vectors_all.at[other], place.sibling),
-    ]
-    gather = WeightGather(place, copies, [weight_ref], [weight_out], [stage], local_sems)
-    segs = BlockGather(place, copies, [segs_own], [segs_out])
-
-    @pl.when(place.has_partner)
-    def _():
-        for swap in swaps:
-            swap.start()
-
-    vector_copies[0].start()
-    vector_copies[1].start()
-    vectors_all[own] = vectors_ref[...]
-    gather.begin()
-
-    @pl.when(jnp.logical_not(place.has_partner))
-    def _():
-        segs_own[...] = segs_ref[...]
-        tokens_out[...] = tokens_ref[...]
-        cotangent_out[...] = cotangent_ref[...]
-
-    @pl.when(place.has_partner)
-    def _():
-        swaps[0].wait_recv()
-
-    segs.begin()
-    vector_copies[0].wait_recv()
-    vector_copies[2].start()
-    segs.first_halves()
-    segs.second_halves()
-    segs.corners()
-    gather.keep_own()
-    for step in gather.steps():
-        gather.step(step)
-    segs.wait_near()
-    segs.wait_far()
-    segs.finish()
-    vector_copies[1].wait_recv()
-    vector_copies[2].wait_recv()
-    for copy in vector_copies:
-        copy.wait_send()
-    vectors_out[...] = assemble_vectors([vectors_all[i] for i in range(4)])
-
-    @pl.when(place.has_partner)
-    def _():
-        for swap in swaps[1:]:
-            swap.wait_recv()
-        for swap in swaps:
-            swap.wait_send()
-
-    gather.finish()
+VECTORS = 8
 
 
 def pack_vectors(ln1_gain, ln1_bias, ln2_gain, ln2_bias, proj_bias, out_bias, attn_bias, fc_bias):
@@ -649,37 +570,6 @@
     return jnp.concatenate([small, query, value, *hidden, jnp.zeros((4, D), F32)], axis=0)
 
 
-def opening(tokens, segs, cotangent, vectors, weight, collective_id):
-    rows, columns = tokens.shape
-    copies = 3 + 3 + WEIGHT_COPIES + BLOCK_COPIES
-    vmem = pl.BlockSpec(memory_space=pltpu.VMEM)
-    anywhere = pl.BlockSpec(memory_space=pl.ANY)
-    return pl.pallas_call(
-        opening_kernel,
-        in_specs=[vmem, vmem, vmem, vmem, anywhere],
-        out_specs=[vmem, vmem, vmem, vmem, anywhere],
-        out_shape=[
-            jax.ShapeDtypeStruct((rows, columns), tokens.dtype),
-            jax.ShapeDtypeStruct((8, *segs.shape), segs.dtype),
-            jax.ShapeDtypeStruct((rows, columns), cotangent.dtype),
-            jax.ShapeDtypeStruct((16, D), F32),
-            jax.ShapeDtypeStruct((4, *weight.shape), weight.dtype),
-        ],
-        scratch_shapes=[
-            pltpu.VMEM((4, *vectors.shape), F32),
-            pltpu.VMEM(segs.shape, segs.dtype),
-            pltpu.VMEM(weight.shape, weight.dtype),
-            pltpu.SemaphoreType.DMA((copies,)),
-            pltpu.SemaphoreType.DMA((copies,)),
-            pltpu.SemaphoreType.DMA((1,)),
-        ],
-        compiler_params=pltpu.CompilerParams(
-            collective_id=collective_id, has_side_effects=True, vmem_limit_bytes=32 << 20
-        ),
-        name="opening",
-    )(tokens, segs, cotangent, vectors, weight)
-
-
 def mask_block(own_segs, segs_ref, block, start, own_is_query):
     rows = own_segs.shape[0]
     own_place = start + lax.broadcasted_iota(jnp.int32, (rows, rows), 0)
@@ -694,144 +584,483 @@
     return jnp.broadcast_to(segs_ref[block, 0:1, :], (rows, rows)).T
 
 
-def attend_kernel(count, *refs):
-    q_ref, kv_ref, segs_ref = refs[:3]
-    shares = refs[3 : 3 + count]
-    out_ref, lse_ref, lse_rows_ref, kv_out = refs[3 + count : 7 + count]
-    fulls = refs[7 + count : 7 + 2 * count]
-    rest = refs[7 + 2 * count :]
-    kv_all, near_bias, far_bias, top_ref, total_ref, mixed_ref, send_sems, recv_sems, local_sems = rest[:9]
-    stages = rest[9:]
+class AttentionForward:
+    def __init__(self, place, q_ref, segs_ref, kv_all, out_ref, lse_ref, lse_rows_ref, kv_out, scratch, sems):
+        self.place = place
+        self.q_ref, self.segs_ref, self.kv_all = q_ref, segs_ref, kv_all
+        self.out_ref, self.lse_ref, self.lse_rows_ref = out_ref, lse_ref, lse_rows_ref
+        self.near_bias, self.far_bias, self.top, self.total, self.mixed = scratch
+        self.rows = q_ref.shape[0]
+        self.near, self.far = 4 * place.y, 4 * (1 - place.y)
+        self.saves = [
+            pltpu.make_async_copy(kv_all.at[pl.ds(first, 4)], kv_out.at[pl.ds(first, 4)], sem)
+            for first, sem in zip((self.near, self.far), sems)
+        ]
+
+    def masks(self, far):
+        rows = self.rows
+        start = self.place.block * rows
+        own_segs = own_columns(self.segs_ref, self.place.block)
+        first, bias = (self.far, self.far_bias) if far else (self.near, self.near_bias)
+        for i in range(4):
+            at = slice(i * rows, (i + 1) * rows)
+            bias[:, at] = mask_block(own_segs, self.segs_ref, first + i, start, True)
+
+    def lanes(self, pair, side=0):
+        return pl.ds(pl.multiple_of(side * D + pair * LANES, LANES), LANES)
+
+    def part(self, first, bias_ref, pair):
+        rows = self.rows
+        queries = two_heads(self.q_ref[:, self.lanes(pair)] * jnp.asarray(SCALE, BF16))
+        keys = self.kv_all[pl.ds(first, 4), :, self.lanes(pair)].reshape(4 * rows, LANES)
+        values = self.kv_all[pl.ds(first, 4), :, self.lanes(pair, 1)].reshape(4 * rows, LANES)
+        bias = bias_ref[...]
+        scores = dot_rows(queries, keys) + jnp.concatenate([bias, bias], axis=0)
+        top = jnp.max(scores, axis=1, keepdims=True)
+        shares = jnp.exp(scores - top)
+        total = jnp.sum(shares, axis=1, keepdims=True)
+        return top, total, jnp.dot(shares.astype(BF16), values, preferred_element_type=F32)
+
+    def near_part(self):
+        self.saves[0].start()
+        self.lse_ref[...] = jnp.zeros_like(self.lse_ref)
+
+        def visit(pair, carried):
+            self.top[pair], self.total[pair], self.mixed[pair] = self.part(
+                self.near, self.near_bias, pair
+            )
+            return carried
+
+        lax.fori_loop(0, PAIRS, visit, 0)
+
+    def far_part(self):
+        self.saves[1].start()
+
+        def visit(pair, carried):
+            top, total, mixed = self.part(self.far, self.far_bias, pair)
+            old_top = self.top[pair]
+            new_top = jnp.maximum(top, old_top)
+            new, old = jnp.exp(top - new_top), jnp.exp(old_top - new_top)
+            self.top[pair] = new_top
+            self.total[pair] = total * new + self.total[pair] * old
+            self.mixed[pair] = mixed * new + self.mixed[pair] * old
+            return carried
+
+        @pl.when(self.place.y == 1)
+        def _():
+            lax.fori_loop(0, PAIRS, visit, 0)
+
+    def store(self):
+        rows = self.rows
+
+        def visit(pair, carried):
+            total = self.total[pair]
+            self.out_ref[:, self.lanes(pair)] = one_pair(self.mixed[pair] / total).astype(BF16)
+            lse = self.top[pair] + jnp.log(total)
+            lane = lax.broadcasted_iota(jnp.int32, (rows, LANES), 1)
+            kept = jnp.where(lane == 2 * pair, lse[:rows], self.lse_ref[...])
+            self.lse_ref[...] = jnp.where(lane == 2 * pair + 1, lse[rows:], kept)
+            return carried
+
+        lax.fori_loop(0, PAIRS, visit, 0)
+        self.lse_rows_ref[...] = self.lse_ref[...].T[:16]
+
+    def finish(self):
+        for save in self.saves:
+            save.wait()
+
+
+def forward_scratch(rows):
+    return [
+        pltpu.VMEM((8, rows, 2 * D), BF16),
+        pltpu.VMEM((rows, 4 * rows), F32),
+        pltpu.VMEM((rows, 4 * rows), F32),
+        pltpu.VMEM((PAIRS, 2 * rows, 1), F32),
+        pltpu.VMEM((PAIRS, 2 * rows, 1), F32),
+        pltpu.VMEM((PAIRS, 2 * rows, LANES), F32),
+    ]
+
+
+FORWARD_SCRATCH = 6
+
+
+def forward_shapes(rows):
+    return [
+        jax.ShapeDtypeStruct((rows, D), BF16),
+        jax.ShapeDtypeStruct((rows, LANES), F32),
+        jax.ShapeDtypeStruct((16, rows), F32),
+        jax.ShapeDtypeStruct((8, rows, 2 * D), BF16),
+    ]
+
+
+def greet_with_partner(place, others):
+    barrier = pltpu.get_barrier_semaphore()
+    for device in others:
+        pl.semaphore_signal(barrier, inc=1, device_id=device, device_id_type=MESH)
+
+    @pl.when(place.has_partner)
+    def _():
+        pl.semaphore_signal(barrier, inc=1, device_id=place.partner, device_id_type=MESH)
+        pl.semaphore_wait(barrier, len(others) + 1)
+
+    @pl.when(jnp.logical_not(place.has_partner))
+    def _():
+        pl.semaphore_wait(barrier, len(others))
+
+
+def attend_kernel(
+    q_ref, kv_ref, segs_ref, cotangent_ref, out_ref, lse_ref, lse_rows_ref, kv_out, cotangent_out, *scratch
+):
+    kv_all, send_sems, recv_sems, local_sems = scratch[0], *scratch[FORWARD_SCRATCH:]
     place = Place()
-    devices = [place.sibling, place.over_x, place.over_y] + ([place.over_z] if count else [])
-    greet(devices)
+    greet_with_partner(place, (place.sibling, place.over_x, place.over_y))
     copies = Copies(send_sems, recv_sems)
     gather = BlockGather(place, copies, [kv_ref], [kv_all])
-    weights = WeightGather(place, copies, shares, fulls, stages, local_sems)
+    swap = copies.make(cotangent_ref, cotangent_out, place.partner)
+    keep = pltpu.make_async_copy(cotangent_ref, cotangent_out, local_sems.at[2])
     gather.begin()
 
-    rows = q_ref.shape[0]
-    start = place.block * rows
-    near, far = 4 * place.y, 4 * (1 - place.y)
-    own_segs = own_columns(segs_ref, place.block)
-    for i in range(4):
-        near_bias[:, i * rows : (i + 1) * rows] = mask_block(own_segs, segs_ref, near + i, start, True)
-        far_bias[:, i * rows : (i + 1) * rows] = mask_block(own_segs, segs_ref, far + i, start, True)
-    lse_ref[...] = jnp.zeros_like(lse_ref)
+    @pl.when(place.has_partner)
+    def _():
+        swap.start()
+
+    @pl.when(jnp.logical_not(place.has_partner))
+    def _():
+        keep.start()
+
+    attention = AttentionForward(
+        place,
+        q_ref,
+        segs_ref,
+        kv_all,
+        out_ref,
+        lse_ref,
+        lse_rows_ref,
+        kv_out,
+        scratch[1:FORWARD_SCRATCH],
+        (local_sems.at[0], local_sems.at[1]),
+    )
+    attention.masks(False)
+    attention.masks(True)
     gather.first_halves()
-    if count:
-        weights.begin()
-        weights.keep_own()
     gather.second_halves()
-
-    def blocks_of(first, pair, side):
-        lanes = pl.ds(pl.multiple_of(side * D + pair * LANES, LANES), LANES)
-        return kv_all[pl.ds(first, 4), :, lanes].reshape(4 * rows, LANES)
-
-    def queries_of(pair):
-        lanes = pl.ds(pl.multiple_of(pair * LANES, LANES), LANES)
-        return two_heads(q_ref[:, lanes] * jnp.asarray(SCALE, BF16))
-
-    def part(first, bias_ref, pair):
-        bias = bias_ref[...]
-        scores = dot_rows(queries_of(pair), blocks_of(first, pair, 0))
-        scores = scores + jnp.concatenate([bias, bias], axis=0)
-        top = jnp.max(scores, axis=1, keepdims=True)
-        weights_here = jnp.exp(scores - top)
-        total = jnp.sum(weights_here, axis=1, keepdims=True)
-        mixed = jnp.dot(
-            weights_here.astype(BF16), blocks_of(first, pair, 1), preferred_element_type=F32
-        )
-        return top, total, mixed
-
-    def visit_near(pair, carried):
-        top_ref[pair], total_ref[pair], mixed_ref[pair] = part(near, near_bias, pair)
-        return carried
-
-    def visit_far(pair, carried):
-        top, total, mixed = part(far, far_bias, pair)
-        old_top, old_total, old_mixed = top_ref[pair], total_ref[pair], mixed_ref[pair]
-        new_top = jnp.maximum(top, old_top)
-        new, old = jnp.exp(top - new_top), jnp.exp(old_top - new_top)
-        top_ref[pair] = new_top
-        total_ref[pair] = total * new + old_total * old
-        mixed_ref[pair] = mixed * new + old_mixed * old
-        return carried
-
-    def visit_last(pair, carried):
-        top, total, mixed = top_ref[pair], total_ref[pair], mixed_ref[pair]
-        lanes = pl.ds(pl.multiple_of(pair * LANES, LANES), LANES)
-        out_ref[:, lanes] = one_pair(mixed / total).astype(BF16)
-        lse = top + jnp.log(total)
-        lane = lax.broadcasted_iota(jnp.int32, (rows, LANES), 1)
-        kept = jnp.where(lane == 2 * pair, lse[:rows], lse_ref[...])
-        lse_ref[...] = jnp.where(lane == 2 * pair + 1, lse[rows:], kept)
-        return carried
-
     gather.wait_near()
-    near_out = pltpu.make_async_copy(
-        kv_all.at[pl.ds(near, 4)], kv_out.at[pl.ds(near, 4)], local_sems.at[count]
-    )
-    near_out.start()
-    lax.fori_loop(0, PAIRS, visit_near, 0)
+    attention.near_part()
     gather.corners()
-    if count:
-        weights.step(0)
     gather.wait_far()
-    far_out = pltpu.make_async_copy(
-        kv_all.at[pl.ds(far, 4)], kv_out.at[pl.ds(far, 4)], local_sems.at[count + 1]
-    )
-    far_out.start()
-
-    @pl.when(place.y == 1)
+    attention.far_part()
+    attention.store()
+    attention.finish()
+    gather.finish()
+
+    @pl.when(place.has_partner)
     def _():
-        lax.fori_loop(0, PAIRS, visit_far, 0)
-
-    lax.fori_loop(0, PAIRS, visit_last, 0)
-    lse_rows_ref[...] = lse_ref[...].T[:16]
-    for step in weights.steps():
-        if count and step > 0:
-            weights.step(step)
-    weights.finish()
-    gather.finish()
-    near_out.wait()
-    far_out.wait()
-
-
-def attend(queries, kv_own, segs, shares, collective_id):
+        swap.wait()
+
+    @pl.when(jnp.logical_not(place.has_partner))
+    def _():
+        keep.wait()
+
+
+def attend(queries, kv_own, segs, cotangent, collective_id):
     rows = queries.shape[0]
-    count = len(shares)
-    slots = BLOCK_COPIES + count * WEIGHT_COPIES
     vmem = pl.BlockSpec(memory_space=pltpu.VMEM)
     anywhere = pl.BlockSpec(memory_space=pl.ANY)
     return pl.pallas_call(
-        partial(attend_kernel, count),
-        in_specs=[vmem, vmem, vmem] + [anywhere] * count,
-        out_specs=[vmem, vmem, vmem, anywhere] + [anywhere] * count,
+        attend_kernel,
+        in_specs=[vmem, vmem, vmem, anywhere],
+        out_specs=[vmem, vmem, vmem, anywhere, vmem],
+        out_shape=forward_shapes(rows) + [jax.ShapeDtypeStruct((rows, D), BF16)],
+        scratch_shapes=forward_scratch(rows)
+        + [
+            pltpu.SemaphoreType.DMA((BLOCK_COPIES + 1,)),
+            pltpu.SemaphoreType.DMA((BLOCK_COPIES + 1,)),
+            pltpu.SemaphoreType.DMA((3,)),
+        ],
+        compiler_params=pltpu.CompilerParams(
+            collective_id=collective_id, has_side_effects=True, vmem_limit_bytes=32 << 20
+        ),
+        name="attend",
+    )(queries, kv_own, segs, cotangent)
+
+
+class FirstWeightGather:
+    def __init__(self, place, copies, share, full, columns, part, sem):
+        x = place.x
+        own, other = place.fsdp, 2 * (1 - place.y) + place.core
+        half = share.shape[0] // 2
+        self.steps = []
+        for index in range(half // part):
+            mine = pl.ds(pl.multiple_of(x * half + index * part, 16), part)
+            theirs = pl.ds(pl.multiple_of((1 - x) * half + index * part, 16), part)
+            got, from_x = full.at[other, mine, columns], full.at[other, theirs, columns]
+            self.steps.append(
+                [
+                    copies.make(share.at[mine, columns], full.at[own, mine, columns], place.over_y),
+                    copies.make(got, got, place.over_x),
+                    copies.make(got, got, place.sibling),
+                    copies.make(from_x, from_x, place.sibling),
+                ]
+            )
+        whole = full.at[own, :, columns]
+        self.to_sibling = copies.make(share.at[:, columns], whole, place.sibling)
+        self.load = pltpu.make_async_copy(share.at[:, columns], whole, sem)
+
+    def begin(self):
+        for step in self.steps:
+            step[0].start()
+        self.to_sibling.start()
+        self.load.start()
+
+    def relay_y(self):
+        for step in self.steps:
+            step[0].wait_recv()
+            step[1].start()
+            step[2].start()
+
+    def relay_x(self):
+        for step in self.steps:
+            step[1].wait_recv()
+            step[3].start()
+
+    def wait_near(self):
+        self.load.wait()
+        self.to_sibling.wait_recv()
+
+    def wait_far(self):
+        for step in self.steps:
+            step[2].wait_recv()
+            step[3].wait_recv()
+
+    def finish(self):
+        self.to_sibling.wait_send()
+        for step in self.steps:
+            for copy in step:
+                copy.wait_send()
+
+
+def opening_kernel(count, *refs):
+    tokens_ref, segs_ref, first_ref = refs[:3]
+    vector_refs = refs[3 : 3 + VECTORS]
+    shares = refs[3 + VECTORS : 3 + VECTORS + count]
+    refs = refs[3 + VECTORS + count :]
+    (
+        tokens_out,
+        segs_out,
+        vectors_out,
+        normed_out,
+        normal_out,
+        inverse_out,
+        q_out,
+        kv_own_out,
+        attended_out,
+        lse_out,
+        lse_rows_out,
+        kv_out,
+        first_out,
+    ) = refs[:13]
+    fulls = refs[13 : 13 + count]
+    refs = refs[13 + count :]
+    kv_all = refs[0]
+    forward = refs[1:FORWARD_SCRATCH]
+    vectors_own, vectors_all, segs_row, segs_sent, segs_own = refs[FORWARD_SCRATCH : FORWARD_SCRATCH + 5]
+    refs = refs[FORWARD_SCRATCH + 5 :]
+    first_full, projected, send_sems, recv_sems, local_sems = refs[:5]
+    stages, vector_rows = refs[5 : 5 + count], refs[5 + count :]
+    place = Place()
+    own, other = place.fsdp, 2 * (1 - place.y) + place.core
+    loads = [
+        pltpu.make_async_copy(src, dst, local_sems.at[count + 6 + i])
+        for i, (src, dst) in enumerate(zip((segs_ref, *vector_refs), (segs_row, *vector_rows)))
+    ]
+    for load in loads:
+        load.start()
+    for load in loads:
+        load.wait()
+    vectors_own[...] = jnp.zeros_like(vectors_own)
+    for i, row in enumerate(vector_rows):
+        size = row.shape[0]
+        vectors_own[i : i + 1, :size] = row[...].astype(F32).reshape(1, size)
+    segs_sent[...] = jnp.broadcast_to(segs_row[...], segs_sent.shape)
+    greet_with_partner(place, (place.sibling, place.over_x, place.over_y, place.over_z))
+    copies = Copies(send_sems, recv_sems)
+    swap_tokens = copies.make(tokens_ref, tokens_out, place.partner)
+    swap_segs = copies.make(segs_sent, segs_own, place.partner)
+    vector_copies = [
+        copies.make(vectors_own, vectors_all.at[own], place.over_y),
+        copies.make(vectors_own, vectors_all.at[own], place.sibling),
+        copies.make(vectors_all.at[other], vectors_all.at[other], place.sibling),
+    ]
+    keys = FirstWeightGather(
+        place, copies, first_ref, first_full, pl.ds(D, 2 * D), 32, local_sems.at[count]
+    )
+    queries = FirstWeightGather(
+        place, copies, first_ref, first_full, pl.ds(0, D), 48, local_sems.at[count + 5]
+    )
+    weights = WeightGather(place, copies, shares, fulls, stages, local_sems)
+    gather = BlockGather(place, copies, [kv_own_out, segs_own], [kv_all, segs_out])
+    save_first = pltpu.make_async_copy(first_full, first_out, local_sems.at[count + 1])
+    attention = AttentionForward(
+        place,
+        q_out,
+        segs_out,
+        kv_all,
+        attended_out,
+        lse_out,
+        lse_rows_out,
+        kv_out,
+        forward,
+        (local_sems.at[count + 2], local_sems.at[count + 3]),
+    )
+
+    keep_tokens = pltpu.make_async_copy(tokens_ref, tokens_out, local_sems.at[count + 7 + VECTORS])
+    vector_copies[0].start()
+    vector_copies[1].start()
+
+    @pl.when(place.has_partner)
+    def _():
+        swap_segs.start()
+
+    keys.begin()
+
+    @pl.when(place.has_partner)
+    def _():
+        swap_tokens.start()
+
+    @pl.when(jnp.logical_not(place.has_partner))
+    def _():
+        keep_tokens.start()
+
+    queries.begin()
+    weights.begin()
+    vectors_all[own] = vectors_own[...]
+
+    @pl.when(jnp.logical_not(place.has_partner))
+    def _():
+        segs_own[...] = segs_sent[...]
+
+    vector_copies[0].wait_recv()
+    vector_copies[2].start()
+    keys.relay_y()
+    vector_copies[1].wait_recv()
+    vector_copies[2].wait_recv()
+    vectors_out[...] = assemble_vectors([vectors_all[i] for i in range(4)])
+
+    @pl.when(place.has_partner)
+    def _():
+        swap_tokens.wait_recv()
+        swap_segs.wait_recv()
+
+    @pl.when(jnp.logical_not(place.has_partner))
+    def _():
+        keep_tokens.wait()
+
+    normed, normal, inverse = norm_forward(
+        tokens_out[...].astype(F32), vectors_out[0:1, :], vectors_out[1:2, :]
+    )
+    normed_out[...] = normed
+    normal_out[...] = normal
+    inverse_out[...] = inverse
+
+    def half_product(y_bit, start, width):
+        depth = D // 2
+        rows = normed_out[:, pl.ds(pl.multiple_of(y_bit * depth, LANES), depth)]
+        weight = first_full[pl.ds(2 * y_bit, 2), :, start : start + width].reshape(depth, width)
+        return jnp.dot(rows, weight, preferred_element_type=F32)
+
+    keys.wait_near()
+    projected[...] = half_product(place.y, D, 2 * D)
+    keys.relay_x()
+    keys.wait_far()
+    total = projected[...] + half_product(1 - place.y, D, 2 * D)
+    kv_own_out[:, :D] = total[:, :D].astype(BF16)
+    kv_own_out[:, D:] = (total[:, D:] + vectors_out[7:8, :]).astype(BF16)
+    gather.begin()
+    queries.relay_y()
+    weights.step(0)
+    weights.step(1)
+    queries.relay_x()
+    queries.wait_near()
+    queries.wait_far()
+    total = half_product(place.y, 0, D) + half_product(1 - place.y, 0, D)
+    q_out[...] = (total + vectors_out[6:7, :]).astype(BF16)
+    save_first.start()
+    gather.first_halves()
+    weights.keep_own()
+    weights.step(2)
+    gather.second_halves()
+    gather.wait_near()
+    attention.masks(False)
+    weights.step(3)
+    attention.near_part()
+    gather.corners()
+    weights.step(4)
+    gather.wait_far()
+    attention.masks(True)
+    attention.far_part()
+    weights.step(5)
+    weights.step(6)
+    attention.store()
+    save_first.wait()
+    attention.finish()
+    keys.finish()
+    queries.finish()
+    gather.finish()
+    for copy in vector_copies:
+        copy.wait_send()
+
+    @pl.when(place.has_partner)
+    def _():
+        swap_segs.wait_send()
+        swap_tokens.wait_send()
+
+    weights.finish()
+
+
+def opening(tokens, segs_row, vectors, first, shares, collective_id):
+    rows, columns = tokens.shape
+    count = len(shares)
+    slots = 2 + 3 + (3 + 2) * 4 + 2 + sum(len(weight_cuts(share.shape)) for share in shares) * WEIGHT_COPIES + 2 * BLOCK_COPIES
+    vmem = pl.BlockSpec(memory_space=pltpu.VMEM)
+    anywhere = pl.BlockSpec(memory_space=pl.ANY)
+    shape = jax.ShapeDtypeStruct
+    segs_shape = (16, segs_row.shape[1])
+    return pl.pallas_call(
+        partial(opening_kernel, count),
+        in_specs=[anywhere] * (3 + VECTORS + count),
+        out_specs=[vmem] * 11 + [anywhere] * (2 + count),
         out_shape=[
-            jax.ShapeDtypeStruct((rows, D), BF16),
-            jax.ShapeDtypeStruct((rows, LANES), F32),
-            jax.ShapeDtypeStruct((16, rows), F32),
-            jax.ShapeDtypeStruct((8, rows, 2 * D), BF16),
+            shape((rows, columns), tokens.dtype),
+            shape((8, *segs_shape), segs_row.dtype),
+            shape((16, D), F32),
+            shape((rows, D), BF16),
+            shape((rows, D), F32),
+            shape((rows, 1), F32),
+            shape((rows, D), BF16),
+            shape((rows, 2 * D), BF16),
         ]
-        + [jax.ShapeDtypeStruct((4, *share.shape), share.dtype) for share in shares],
-        scratch_shapes=[
-            pltpu.VMEM((8, rows, 2 * D), BF16),
-            pltpu.VMEM((rows, 4 * rows), F32),
-            pltpu.VMEM((rows, 4 * rows), F32),
-            pltpu.VMEM((PAIRS, 2 * rows, 1), F32),
-            pltpu.VMEM((PAIRS, 2 * rows, 1), F32),
-            pltpu.VMEM((PAIRS, 2 * rows, LANES), F32),
+        + forward_shapes(rows)
+        + [shape((4, *share.shape), share.dtype) for share in [first, *shares]],
+        scratch_shapes=forward_scratch(rows)
+        + [
+            pltpu.VMEM((8, D), F32),
+            pltpu.VMEM((4, 8, D), F32),
+            pltpu.VMEM(segs_row.shape, segs_row.dtype),
+            pltpu.VMEM(segs_shape, segs_row.dtype),
+            pltpu.VMEM(segs_shape, segs_row.dtype),
+            pltpu.VMEM((4, *first.shape), first.dtype),
+            pltpu.VMEM((rows, 2 * D), F32),
             pltpu.SemaphoreType.DMA((slots,)),
             pltpu.SemaphoreType.DMA((slots,)),
-            pltpu.SemaphoreType.DMA((count + 2,)),
+            pltpu.SemaphoreType.DMA((count + 8 + VECTORS,)),
         ]
-        + [pltpu.VMEM(share.shape, share.dtype) for share in shares],
+        + [pltpu.VMEM(share.shape, share.dtype) for share in shares]
+        + [pltpu.VMEM(vector.shape, vector.dtype) for vector in vectors],
         compiler_params=pltpu.CompilerParams(
-            collective_id=collective_id, has_side_effects=True, vmem_limit_bytes=40 << 20
+            collective_id=collective_id, has_side_effects=True, vmem_limit_bytes=60 << 20
         ),
-        name="attend",
-    )(queries, kv_own, segs, *shares)
+        name="opening",
+    )(tokens, segs_row, first, *vectors, *shares)
 
 
 class AttentionGrads:
@@ -1020,7 +1249,7 @@
             pltpu.SemaphoreType.DMA,
         ],
         compiler_params=pltpu.CompilerParams(
-            collective_id=collective_id, has_side_effects=True, vmem_limit_bytes=40 << 20
+            collective_id=collective_id, has_side_effects=True, vmem_limit_bytes=32 << 20
         ),
         name="attend_back",
     )(queries, grads, stats, lse, delta, segs, kv)
@@ -1040,49 +1269,94 @@
     ]
 
 
-def reduce_gradients_kernel(places, count, *refs):
-    partials, vector = refs[:count], refs[count]
-    sums, vector_out = refs[count + 1 : 2 * count + 1], refs[2 * count + 1]
-    (
-        own,
-        got_core,
-        got_y,
-        to_x,
-        got_x,
-        to_z,
-        got_z,
-        to_zz,
-        got_zz,
-        vector_got,
-        send_sems,
-        recv_sems,
-        local_sems,
-    ) = refs[2 * count + 2 :]
-    x, z, y, core = place_bits()
-    low, high = lax.rem(z, 2), z // 2
-    fsdp = 2 * y + core
-    sibling = (2 * z + x, 2 * y + 1 - core)
-    over_y = (2 * z + x, 2 * (1 - y) + core)
-    over_x = (2 * z + 1 - x, fsdp)
-    over_z = (2 * (z + 1 - 2 * low) + x, fsdp)
-    over_zz = (2 * (z + 2 - 4 * high) + x, fsdp)
-    greet((sibling, over_y, over_x, over_z, over_zz))
-
-    def copy(slot, src, dst, device):
-        return pltpu.make_async_remote_copy(
-            src_ref=src,
-            dst_ref=dst,
-            send_sem=send_sems.at[slot],
-            recv_sem=recv_sems.at[slot],
-            device_id=device,
-            device_id_type=MESH,
+REDUCE_STAGES = ("core0", "core1", "y", "x", "z", "zz", "zz_back", "z_back", "x_back")
+
+
+class GradientSum:
+    def __init__(self, place, copies, places, terms, sums, buffers, local_sems):
+        self.place = place
+        (
+            self.own,
+            self.got_core,
+            self.got_y,
+            self.to_x,
+            self.got_x,
+            self.to_z,
+            self.got_z,
+            self.to_zz,
+            self.got_zz,
+            to_core,
+        ) = buffers
+        self.to_core = to_core
+        self.x_rows, self.z_rows = CHUNK_ROWS // 2, CHUNK_ROWS // 4
+        self.zz_columns = CHUNK_COLUMNS // 2
+        x, y, core, low, high = place.x, place.y, place.core, place.low, place.high
+        self.plans = []
+        self.finals = []
+        self.loads = []
+        self.filled = []
+        for k, (which, row, column) in enumerate(places):
+            term, out = terms[which], sums[which]
+
+            def piece(first, rows, start, width, out=out, row=row, column=column):
+                return out.at[
+                    pl.ds(pl.multiple_of(row + first, 16), rows),
+                    pl.ds(pl.multiple_of(column + start, LANES), width),
+                ]
+
+            def quarter(index, term=term, row=row, column=column):
+                return term.at[index, pl.ds(row, CHUNK_ROWS), pl.ds(column, CHUNK_COLUMNS)]
+
+            if term is None:
+                sent = [to_core.at[len(self.filled), i] for i in range(2)]
+                self.filled.append((k, column))
+                loads = []
+            else:
+                sent = [quarter(1 - core), quarter(3 - core)]
+                loads = [
+                    pltpu.make_async_copy(
+                        quarter(2 * i + core), self.own.at[k, i], local_sems.at[2 * k + i]
+                    )
+                    for i in range(2)
+                ]
+            final = piece(
+                x * self.x_rows + low * self.z_rows, self.z_rows, high * self.zz_columns, self.zz_columns
+            )
+            wide = piece(x * self.x_rows + low * self.z_rows, self.z_rows, 0, CHUNK_COLUMNS)
+            tall = piece(x * self.x_rows, self.x_rows, 0, CHUNK_COLUMNS)
+            moves = (
+                (sent[0], self.got_core.at[k, 0], place.sibling),
+                (sent[1], self.got_core.at[k, 1], place.sibling),
+                (self.own.at[k, 1 - y], self.got_y.at[k], place.over_y),
+                (self.to_x.at[k], self.got_x.at[k], place.over_x),
+                (self.to_z.at[k], self.got_z.at[k], place.over_z),
+                (self.to_zz.at[k], self.got_zz.at[k], place.over_zz),
+                (final, final, place.over_zz),
+                (wide, wide, place.over_z),
+                (tall, tall, place.over_x),
+            )
+            self.plans.append(
+                {name: copies.make(*move) for name, move in zip(REDUCE_STAGES, moves)}
+            )
+            self.finals.append(final)
+            self.loads.append(loads)
+        self.stages = (
+            self.stage_x,
+            self.stage_z,
+            self.stage_zz,
+            self.stage_final,
+            self.stage_z_back,
+            self.stage_x_back,
         )
 
-    x_rows, z_rows, zz_columns = CHUNK_ROWS // 2, CHUNK_ROWS // 4, CHUNK_COLUMNS // 2
-    chunks = len(places)
-
-    def add_up(store, loads, rows):
-        step = z_rows
+    def begin(self, k):
+        self.plans[k]["core0"].start()
+        self.plans[k]["core1"].start()
+        for load in self.loads[k]:
+            load.start()
+
+    def add_up(self, store, loads, rows):
+        step = self.z_rows
 
         def visit(index, carried):
             offset = pl.multiple_of(index * step, 16)
@@ -1097,58 +1371,7 @@
         else:
             lax.fori_loop(0, rows // step, visit, 0)
 
-    vector_devices = (over_y, sibling, over_x, over_z, over_zz)
-    vector_copies = [
-        copy(chunks * REDUCE_COPIES + i, vector_out, vector_got.at[i], vector_devices[i])
-        for i in range(VECTOR_AXES)
-    ]
-    vector_out[...] = vector[...]
-    vector_copies[0].start()
-
-    plans = []
-    loads = []
-    for k, (which, row, column) in enumerate(places):
-        partial_sum, out = partials[which], sums[which]
-
-        def term(quarter, partial_sum=partial_sum, row=row, column=column):
-            return partial_sum.at[quarter, pl.ds(row, CHUNK_ROWS), pl.ds(column, CHUNK_COLUMNS)]
-
-        def piece(first, rows, start, width, out=out, row=row, column=column):
-            return out.at[
-                pl.ds(pl.multiple_of(row + first, 16), rows),
-                pl.ds(pl.multiple_of(column + start, LANES), width),
-            ]
-
-        final = piece(x * x_rows + low * z_rows, z_rows, high * zz_columns, zz_columns)
-        wide = piece(x * x_rows + low * z_rows, z_rows, 0, CHUNK_COLUMNS)
-        tall = piece(x * x_rows, x_rows, 0, CHUNK_COLUMNS)
-        base = k * REDUCE_COPIES
-        plans.append(
-            {
-                "core0": copy(base, term(1 - core), got_core.at[k, 0], sibling),
-                "core1": copy(base + 1, term(3 - core), got_core.at[k, 1], sibling),
-                "y": copy(base + 2, own.at[k, 1 - y], got_y.at[k], over_y),
-                "x": copy(base + 3, to_x.at[k], got_x.at[k], over_x),
-                "z": copy(base + 4, to_z.at[k], got_z.at[k], over_z),
-                "zz": copy(base + 5, to_zz.at[k], got_zz.at[k], over_zz),
-                "zz_back": copy(base + 6, final, final, over_zz),
-                "z_back": copy(base + 7, wide, wide, over_z),
-                "x_back": copy(base + 8, tall, tall, over_x),
-                "final": final,
-            }
-        )
-        loads.append(
-            [
-                pltpu.make_async_copy(term(2 * i + core), own.at[k, i], local_sems.at[2 * k + i])
-                for i in range(2)
-            ]
-        )
-        plans[k]["core0"].start()
-        plans[k]["core1"].start()
-        loads[k][0].start()
-        loads[k][1].start()
-
-    def slab(ref, *index, first=0, start=None, width=None):
+    def slab(self, ref, *index, first=0, start=None, width=None):
         def load(offset, rows):
             place = pl.ds(pl.multiple_of(first + offset, 16), rows)
             if width is None:
@@ -1157,94 +1380,253 @@
 
         return load
 
-    def stage_y(k):
-        plan = plans[k]
-        for load in loads[k]:
+    def stage_y(self, k):
+        plan, y = self.plans[k], self.place.y
+        for load in self.loads[k]:
             load.wait()
         plan["core0"].wait_recv()
         plan["core1"].wait_recv()
 
         def store(offset, rows, value):
-            own[k, 1 - y, pl.ds(offset, rows)] = value
-
-        add_up(store, [slab(own, k, 1 - y), slab(got_core, k, 1 - y)], CHUNK_ROWS)
+            self.own[k, 1 - y, pl.ds(offset, rows)] = value
+
+        loads = [self.slab(self.own, k, 1 - y), self.slab(self.got_core, k, 1 - y)]
+        self.add_up(store, loads, CHUNK_ROWS)
         plan["y"].start()
 
-    def stage_x(k):
-        plan = plans[k]
+    def terms_at(self, k, first, depth, inner=0, **part):
+        y = self.place.y
+        loads = [
+            self.slab(self.own, k, y, first=first, **part),
+            self.slab(self.got_core, k, y, first=first, **part),
+            self.slab(self.got_y, k, first=first, **part),
+        ]
+        if depth > 0:
+            loads.append(self.slab(self.got_x, k, first=inner, **part))
+        if depth > 1:
+            loads.append(self.slab(self.got_z, k, **part))
+        return loads
+
+    def stage_x(self, k):
+        plan = self.plans[k]
         plan["y"].wait_recv()
-        first = (1 - x) * x_rows
 
         def store(offset, rows, value):
-            to_x[k, pl.ds(offset, rows)] = value
-
-        add_up(
-            store,
-            [slab(own, k, y, first=first), slab(got_core, k, y, first=first), slab(got_y, k, first=first)],
-            x_rows,
-        )
+            self.to_x[k, pl.ds(offset, rows)] = value
+
+        self.add_up(store, self.terms_at(k, (1 - self.place.x) * self.x_rows, 0), self.x_rows)
         plan["x"].start()
 
-    def stage_z(k):
-        plan = plans[k]
+    def stage_z(self, k):
+        plan = self.plans[k]
         plan["x"].wait_recv()
-        inner = (1 - low) * z_rows
-        first = x * x_rows + inner
+        inner = (1 - self.place.low) * self.z_rows
 
         def store(offset, rows, value):
-            to_z[k] = value
-
-        add_up(
-            store,
-            [
-                slab(own, k, y, first=first),
-                slab(got_core, k, y, first=first),
-                slab(got_y, k, first=first),
-                slab(got_x, k, first=inner),
-            ],
-            z_rows,
-        )
+            self.to_z[k] = value
+
+        first = self.place.x * self.x_rows + inner
+        self.add_up(store, self.terms_at(k, first, 1, inner), self.z_rows)
         plan["z"].start()
 
-    def last_loads(k, start):
-        inner = low * z_rows
-        first = x * x_rows + inner
-        part = {"start": start, "width": zz_columns}
-        return [
-            slab(own, k, y, first=first, **part),
-            slab(got_core, k, y, first=first, **part),
-            slab(got_y, k, first=first, **part),
-            slab(got_x, k, first=inner, **part),
-            slab(got_z, k, **part),
-        ]
-
-    def stage_zz(k):
-        plan = plans[k]
+    def last_terms(self, k, start):
+        inner = self.place.low * self.z_rows
+        first = self.place.x * self.x_rows + inner
+        return self.terms_at(k, first, 2, inner, start=start, width=self.zz_columns)
+
+    def stage_zz(self, k):
+        plan = self.plans[k]
         plan["z"].wait_recv()
 
         def store(offset, rows, value):
-            to_zz[k] = value
-
-        add_up(store, last_loads(k, (1 - high) * zz_columns), z_rows)
+            self.to_zz[k] = value
+
+        self.add_up(store, self.last_terms(k, (1 - self.place.high) * self.zz_columns), self.z_rows)
         plan["zz"].start()
 
-    def stage_final(k):
-        plan = plans[k]
+    def stage_final(self, k):
+        plan = self.plans[k]
         plan["zz"].wait_recv()
 
         def store(offset, rows, value):
-            plan["final"][...] = value
-
-        add_up(store, last_loads(k, high * zz_columns) + [slab(got_zz, k)], z_rows)
+            self.finals[k][...] = value
+
+        terms = self.last_terms(k, self.place.high * self.zz_columns)
+        self.add_up(store, terms + [self.slab(self.got_zz, k)], self.z_rows)
         plan["zz_back"].start()
 
-    def stage_z_back(k):
-        plans[k]["zz_back"].wait_recv()
-        plans[k]["z_back"].start()
-
-    def stage_x_back(k):
-        plans[k]["z_back"].wait_recv()
-        plans[k]["x_back"].start()
+    def stage_z_back(self, k):
+        self.plans[k]["zz_back"].wait_recv()
+        self.plans[k]["z_back"].start()
+
+    def stage_x_back(self, k):
+        self.plans[k]["z_back"].wait_recv()
+        self.plans[k]["x_back"].start()
+
+    def ticks(self):
+        return len(self.plans) + len(self.stages) - 1
+
+    def tick(self, tick):
+        for lag, stage in enumerate(self.stages):
+            if 0 <= tick - lag < len(self.plans):
+                stage(tick - lag)
+
+    def finish(self):
+        for plan in self.plans:
+            plan["x_back"].wait_recv()
+            for name in REDUCE_STAGES:
+                plan[name].wait_send()
+
+
+def reduce_scratch(chunks, filled):
+    rows, columns = CHUNK_ROWS, CHUNK_COLUMNS
+    shapes = [
+        (chunks, 2, rows, columns),
+        (chunks, 2, rows, columns),
+        (chunks, rows, columns),
+        (chunks, rows // 2, columns),
+        (chunks, rows // 2, columns),
+        (chunks, rows // 4, columns),
+        (chunks, rows // 4, columns),
+        (chunks, rows // 4, columns // 2),
+        (chunks, rows // 4, columns // 2),
+        (filled, 2, rows, columns),
+    ]
+    return [pltpu.VMEM(shape, BF16) for shape in shapes]
+
+
+REDUCE_SCRATCH = 10
+CLOSING_INPUTS = 14
+
+
+def closing_kernel(places, count, *refs):
+    (
+        q_ref,
+        grad_ref,
+        stats_ref,
+        lse_ref,
+        delta_ref,
+        segs_ref,
+        normal_ref,
+        inverse_ref,
+        gain_ref,
+        middle_ref,
+        left_ref,
+        later_ref,
+        terms_ref,
+    ) = refs[: CLOSING_INPUTS - 1]
+    kv_ref, weight_ref = refs[CLOSING_INPUTS - 1 : CLOSING_INPUTS + 1]
+    partials = refs[CLOSING_INPUTS + 1 : CLOSING_INPUTS + 1 + count]
+    refs = refs[CLOSING_INPUTS + 1 + count :]
+    sums, vector_out, tokens_out = refs[: count + 1], refs[count + 1], refs[count + 2]
+    refs = refs[count + 3 :]
+    kv_all, q_all, grad_all, stats_all = refs[:4]
+    biases, attention_sums = refs[4:6], refs[6:9]
+    refs = refs[ATTENTION_SCRATCH:]
+    buffers = refs[:REDUCE_SCRATCH]
+    grads_ref, weight, turned, vector_got, tokens_own, send_sems, recv_sems, local_sems = refs[REDUCE_SCRATCH:]
+
+    place = Place()
+    greet_with_partner(
+        place, (place.sibling, place.over_x, place.over_y, place.over_z, place.over_zz)
+    )
+    copies = Copies(send_sems, recv_sems)
+    gather = BlockGather(
+        place, copies, [q_ref, grad_ref, stats_ref], [q_all, grad_all, stats_all]
+    )
+    swap = copies.make(tokens_own, tokens_out, place.partner)
+    reduce = GradientSum(
+        place, copies, places, list(partials) + [None], sums, buffers, local_sems
+    )
+    chunks = len(places)
+    filled = len(reduce.filled)
+    early = chunks - filled
+    vector_devices = (place.over_x, place.over_z, place.over_zz, place.sibling, place.over_y)
+    vector_copies = [
+        copies.make(vector_out, vector_got.at[i], device)
+        for i, device in enumerate(vector_devices)
+    ]
+    load_kv = pltpu.make_async_copy(kv_ref, kv_all, local_sems.at[2 * chunks])
+    load_weight = pltpu.make_async_copy(weight_ref, weight, local_sems.at[2 * chunks + 1])
+
+    load_kv.start()
+    gather.begin()
+    for k in range(early):
+        reduce.begin(k)
+    load_weight.start()
+    grads = AttentionGrads(
+        place,
+        q_ref,
+        grad_ref,
+        lse_ref,
+        delta_ref,
+        segs_ref,
+        kv_all,
+        q_all,
+        grad_all,
+        stats_all,
+        biases,
+        attention_sums,
+    )
+    grads.masks()
+    turned[...] = left_ref[...].T
+    load_kv.wait()
+    grads.query_grads(0, 2)
+    gather.first_halves()
+    reduce.stage_y(0)
+    grads.query_grads(2, PAIRS)
+    gather.second_halves()
+    for k in range(1, 4):
+        reduce.stage_y(k)
+    gather.wait_near()
+    grads.near_keys()
+    gather.corners()
+    for k in range(4, early):
+        reduce.stage_y(k)
+    gather.wait_far()
+    reduce.tick(0)
+    grads.far_keys()
+    grads.store(grads_ref)
+    reduce.tick(1)
+
+    own_grads = grads_ref[...]
+    right = jnp.concatenate([later_ref[...], own_grads], axis=0)
+    for index, (k, column) in enumerate(reduce.filled):
+        columns = right[:, column : column + CHUNK_COLUMNS]
+
+        def term(quarter):
+            rows = turned[pl.ds(pl.multiple_of(quarter * CHUNK_ROWS, 16), CHUNK_ROWS), :]
+            return jnp.dot(rows, columns, preferred_element_type=F32).astype(BF16)
+
+        for i in range(2):
+            reduce.to_core[index, i] = term(2 * i + 1 - place.core)
+            reduce.own[k, i] = term(2 * i + place.core)
+        reduce.begin(k)
+    reduce.tick(2)
+    load_weight.wait()
+    grad_normed = dot_rows(own_grads, weight[...])
+    grad_input, grad_gain, grad_bias = norm_backward(
+        grad_normed, normal_ref[...], inverse_ref[...], gain_ref[...]
+    )
+    swapped = (middle_ref[...] + grad_input).astype(BF16)
+    tokens_own[...] = swapped
+
+    @pl.when(place.has_partner)
+    def _():
+        swap.start()
+
+    @pl.when(jnp.logical_not(place.has_partner))
+    def _():
+        tokens_out[...] = swapped
+
+    vector_out[...] = terms_ref[...]
+    query_bias = jnp.sum(own_grads[:, :D].astype(F32), axis=0, keepdims=True)
+    value_bias = jnp.sum(own_grads[:, 2 * D :].astype(F32), axis=0, keepdims=True)
+    for row, value in ((0, grad_gain[None]), (1, grad_bias[None]), (6, query_bias), (7, value_bias)):
+        vector_out[row : row + 1, :] = vector_out[row : row + 1, :] + value
+    vector_copies[0].start()
+    for k in range(early, chunks):
+        reduce.stage_y(k)
 
     def vector_step(index):
         vector_copies[index].wait()
@@ -1252,57 +1634,88 @@
         if index + 1 < VECTOR_AXES:
             vector_copies[index + 1].start()
 
-    for k in range(chunks):
-        stage_y(k)
-    stages = (stage_x, stage_z, stage_zz, stage_final, stage_z_back, stage_x_back)
-    for tick in range(chunks + len(stages) - 1):
-        if tick < VECTOR_AXES:
-            vector_step(tick)
-        for lag, stage in enumerate(stages):
-            if 0 <= tick - lag < chunks:
-                stage(tick - lag)
-    for plan in plans:
-        plan["x_back"].wait_recv()
-        for name in ("core0", "core1", "y", "x", "z", "zz", "zz_back", "z_back", "x_back"):
-            plan[name].wait_send()
-
-
-def reduce_gradients(partials, vector, collective_id):
+    for tick in range(3, reduce.ticks()):
+        reduce.tick(tick)
+        if tick - 3 < VECTOR_AXES - 1:
+            vector_step(tick - 3)
+    vector_step(VECTOR_AXES - 1)
+    reduce.finish()
+    gather.finish()
+
+    @pl.when(place.has_partner)
+    def _():
+        swap.wait_recv()
+        swap.wait_send()
+
+
+def closing(
+    queries,
+    grads,
+    stats,
+    lse,
+    delta,
+    segs,
+    normal,
+    inverse,
+    gain,
+    middle,
+    left,
+    later,
+    terms,
+    kv,
+    weight,
+    partials,
+    collective_id,
+):
+    rows = queries.shape[0]
     count = len(partials)
-    places = chunk_places([partial_sum.shape[1:] for partial_sum in partials])
+    shapes = [term.shape[1:] for term in partials] + [(weight.shape[0] // 4, weight.shape[1])]
+    places = chunk_places(shapes)
     chunks = len(places)
-    slots = chunks * REDUCE_COPIES + VECTOR_AXES
-    rows, columns = CHUNK_ROWS, CHUNK_COLUMNS
-    buffers = [
-        (2, rows, columns),
-        (2, rows, columns),
-        (rows, columns),
-        (rows // 2, columns),
-        (rows // 2, columns),
-        (rows // 4, columns),
-        (rows // 4, columns),
-        (rows // 4, columns // 2),
-        (rows // 4, columns // 2),
-    ]
+    filled = len(chunk_places(shapes[-1:]))
+    slots = chunks * REDUCE_COPIES + VECTOR_AXES + 3 * BLOCK_COPIES + 1
     vmem = pl.BlockSpec(memory_space=pltpu.VMEM)
+    anywhere = pl.BlockSpec(memory_space=pl.ANY)
     return pl.pallas_call(
-        partial(reduce_gradients_kernel, places, count),
-        in_specs=[pl.BlockSpec(memory_space=pl.ANY)] * count + [vmem],
-        out_specs=[vmem] * (count + 1),
-        out_shape=[jax.ShapeDtypeStruct(p.shape[1:], BF16) for p in partials]
-        + [jax.ShapeDtypeStruct(vector.shape, F32)],
-        scratch_shapes=[pltpu.VMEM((chunks, *shape), BF16) for shape in buffers]
+        partial(closing_kernel, places, count),
+        in_specs=[vmem] * (CLOSING_INPUTS - 1) + [anywhere] * (2 + count),
+        out_specs=[vmem] * (count + 3),
+        out_shape=[jax.ShapeDtypeStruct(shape, BF16) for shape in shapes]
+        + [jax.ShapeDtypeStruct(terms.shape, F32), jax.ShapeDtypeStruct((rows, D), BF16)],
+        scratch_shapes=attention_scratch(rows)
+        + reduce_scratch(chunks, filled)
         + [
-            pltpu.VMEM((VECTOR_AXES, *vector.shape), F32),
+            pltpu.VMEM((rows, 3 * D), BF16),
+            pltpu.VMEM(weight.shape, BF16),
+            pltpu.VMEM(left.shape[::-1], BF16),
+            pltpu.VMEM((VECTOR_AXES, *terms.shape), F32),
+            pltpu.VMEM((rows, D), BF16),
             pltpu.SemaphoreType.DMA((slots,)),
             pltpu.SemaphoreType.DMA((slots,)),
-            pltpu.SemaphoreType.DMA((2 * chunks,)),
+            pltpu.SemaphoreType.DMA((2 * chunks + 2,)),
         ],
         compiler_params=pltpu.CompilerParams(
-            collective_id=collective_id, has_side_effects=True, vmem_limit_bytes=48 << 20
+            collective_id=collective_id, has_side_effects=True, vmem_limit_bytes=60 << 20
         ),
-        name="reduce_gradients",
-    )(*partials, vector)
+        name="closing",
+    )(
+        queries,
+        grads,
+        stats,
+        lse,
+        delta,
+        segs,
+        normal,
+        inverse,
+        gain,
+        middle,
+        left,
+        later,
+        terms,
+        kv,
+        weight,
+        *partials,
+    )
 
 
 class PlaneLinks:
@@ -1310,37 +1723,59 @@
         pairs = [(c * 4 + f, (2 * f + c % 2) * 4 + c // 2) for c in range(8) for f in range(4)]
         return lax.ppermute(value, ("ctx", "fsdp"), pairs)
 
-    def open(self, tokens, segs_row, cotangent, vectors, weight):
-        segs = jnp.broadcast_to(segs_row, (16, segs_row.shape[1]))
-        return opening(tokens, segs, cotangent, vectors, weight, 0)
-
-    def attend(self, queries, kv_own, segs, shares):
-        attended, lse, lse_rows, kv, *fulls = attend(
-            queries, kv_own, segs, shares, 1 if shares else 2
-        )
-        return attended, lse, lse_rows, kv, fulls
+    def open(self, tokens, segs_row, vectors, shares):
+        tokens, segs, vectors, *results = opening(tokens, segs_row, vectors, shares[0], shares[1:], 0)
+        return tokens.astype(F32), segs, vectors, as_matrices(results[9:]), results[:9]
+
+    def attend(self, queries, kv_own, segs, cotangent):
+        *results, cotangent = attend(queries, kv_own, segs, cotangent, 2)
+        return results, cotangent
 
     def attend_back(self, queries, grads, stats, lse, delta, segs, kv, kv_own):
         return attend_back(queries, grads, stats, lse, delta, segs, kv, 3)
 
-    def sum_gradients(self, factors, vectors):
+    def close(self, attention, norm, factors, later, vectors, weight):
+        queries, grads, stats, lse, delta, segs, kv, _ = attention
+        normal, inverse, gain, middle = norm
         terms = []
-        for left, right in factors:
+        for left, right in factors[:-1]:
             term = column_products(left, right).astype(BF16)
             terms.append(term.reshape(4, term.shape[0] // 4, term.shape[1]))
-        *sums, vectors = reduce_gradients(terms, vectors, 4)
-        return [total.astype(F32) for total in sums], vectors
+        *sums, vectors, tokens_grad = closing(
+            queries,
+            grads,
+            stats,
+            lse,
+            delta,
+            segs,
+            normal,
+            inverse,
+            gain,
+            middle,
+            factors[-1],
+            later,
+            vectors,
+            kv,
+            weight,
+            terms,
+            4,
+        )
+        return [total.astype(F32) for total in sums], vectors, tokens_grad
 
 
 class PlainLinks:
     def leave(self, value):
         return value
 
-    def open(self, tokens, segs_row, cotangent, vectors, weight):
-        segs = lax.all_gather(segs_row, "ctx", axis=1, tiled=True)
-        shares = lax.all_gather(vectors, "fsdp", axis=0)
-        vectors = assemble_vectors([shares[i] for i in range(4)])
-        return tokens, (segs_row, segs), cotangent, vectors, lax.all_gather(weight, "fsdp", axis=0)
+    def open(self, tokens, segs_row, vectors, shares):
+        segs = (segs_row, lax.all_gather(segs_row, "ctx", axis=1, tiled=True))
+        gathered = lax.all_gather(pack_vectors(*vectors), "fsdp", axis=0)
+        vectors = assemble_vectors([gathered[i] for i in range(4)])
+        weights = as_matrices([lax.all_gather(share, "fsdp", axis=0) for share in shares])
+        resid = tokens.astype(F32)
+        first = project_rows(resid, vectors, weights[0])
+        first = first + self.attend(*first[3:], segs, None)[0]
+        return resid, segs, vectors, weights, first
 
     def place(self, segs):
         own_segs, all_segs = segs
@@ -1351,12 +1786,10 @@
     def blocks(self, block):
         return lax.all_gather(block, "ctx", axis=0)
 
-    def attend(self, queries, kv_own, segs, shares):
+    def attend(self, queries, kv_own, segs, cotangent):
         start, own_segs, all_segs = self.place(segs)
         kv = self.blocks(kv_own).reshape(-1, 2 * D)
-        attended, lse, lse_rows = attention_forward(start, queries, kv, own_segs, all_segs)
-        fulls = [lax.all_gather(share, "fsdp", axis=0) for share in shares]
-        return attended, lse, lse_rows, kv, fulls
+        return (*attention_forward(start, queries, kv, own_segs, all_segs), kv), cotangent
 
     def attend_back(self, queries, grads, stats, lse, delta, segs, kv, kv_own):
         start, own_segs, all_segs = self.place(segs)
@@ -1377,26 +1810,37 @@
             all_segs,
         )
 
-    def sum_gradients(self, factors, vectors):
+    def close(self, attention, norm, factors, later, vectors, weight):
+        grad_projected = self.attend_back(*attention)
+        grad_input, terms = input_gradient(grad_projected, weight, *norm)
+        vectors = vectors + jnp.concatenate(
+            [terms[:2], jnp.zeros((4, D), F32), terms[2:], jnp.zeros((8, D), F32)], axis=0
+        )
+        right = jnp.concatenate([later, grad_projected], axis=0)
         sums = []
-        for left, right in factors:
+        for left, right in factors[:-1] + [(factors[-1], right)]:
             term = column_products(left, right).astype(BF16)
             share = lax.psum_scatter(term, "fsdp", scatter_dimension=0, tiled=True)
             sums.append(lax.psum(share.astype(F32), "ctx"))
-        return sums, lax.psum(vectors, ("ctx", "fsdp"))
-
-
-def layer_forward(resid, weights, vectors, links, segs, shares):
-    gain_one, bias_one, gain_two, bias_two, bias_proj, bias_out = (vectors[i : i + 1] for i in range(6))
-    bias_qkv = jnp.concatenate([vectors[6:7], jnp.zeros((1, D), F32), vectors[7:8]], axis=1)
+        return sums, lax.psum(vectors, ("ctx", "fsdp")), grad_input.astype(BF16)
+
+
+def as_matrices(fulls):
+    return tuple(full.reshape(-1, full.shape[-1]) for full in fulls)
+
+
+def project_rows(resid, vectors, weight_qkv):
+    bias = jnp.concatenate([vectors[6:7], jnp.zeros((1, D), F32), vectors[7:8]], axis=1)
+    normed, normal, inverse = norm_forward(resid, vectors[0:1], vectors[1:2])
+    projected = (jnp.dot(normed, weight_qkv, preferred_element_type=F32) + bias).astype(BF16)
+    return normed, normal, inverse, projected[:, :D], projected[:, D:]
+
+
+def layer_forward(resid, weights, vectors, first):
+    gain_two, bias_two, bias_proj, bias_out = (vectors[i : i + 1] for i in range(2, 6))
     bias_fc = vectors[8:12].reshape(1, 4 * D)
-    normed_one, normal_one, inverse_one = norm_forward(resid, gain_one, bias_one)
-    projected = jnp.dot(normed_one, weights[0], preferred_element_type=F32) + bias_qkv
-    projected = projected.astype(BF16)
-    queries, kv_own = projected[:, :D], projected[:, D:]
-    attended, lse, lse_rows, kv, fulls = links.attend(queries, kv_own, segs, shares)
-    weights = weights + tuple(full.reshape(-1, full.shape[-1]) for full in fulls)
     _, weight_proj, weight_fc, weight_out = weights
+    normed_one, normal_one, inverse_one, queries, kv_own, attended, lse, lse_rows, kv = first
     middle = resid + jnp.dot(attended, weight_proj, preferred_element_type=F32) + bias_proj
     normed_two, normal_two, inverse_two = norm_forward(middle, gain_two, bias_two)
     hidden = jnp.dot(normed_two, weight_fc, preferred_element_type=F32) + bias_fc
@@ -1418,7 +1862,7 @@
         hidden,
         activated,
     )
-    return result_rows, saved, weights
+    return result_rows, saved
 
 
 def layer_backward(gradient, weights, vectors, saved, links, segs):
@@ -1465,32 +1909,25 @@
         preferred_element_type=F32,
     )
     stats = jnp.concatenate([lse_rows, delta_rows], axis=0)
-    grad_projected = links.attend_back(
-        queries, grad_attended, stats, lse, delta, segs, kv, kv_own
-    )
-    grad_normed_one = dot_rows(grad_projected, weight_qkv)
-    grad_in_one, grad_gain_one, grad_bias_one = norm_backward(
-        grad_normed_one, normal_one, inverse_one, gain_one
-    )
-    grad_input = grad_middle + grad_in_one
-    matrices = (
-        (activated, grad_branch),
-        (normed_two, grad_hidden),
-        (attended, grad_proj),
-        (normed_one, grad_projected),
-    )
-    terms = (
-        grad_gain_one,
-        grad_bias_one,
-        grad_gain_two,
-        grad_bias_two,
-        total(grad_proj),
-        total(grad_branch),
+    attention = (queries, grad_attended, stats, lse, delta, segs, kv, kv_own)
+    norm = (normal_one, inverse_one, gain_one, grad_middle)
+    matrices = ((activated, grad_branch), (normed_two, grad_hidden), (attended, grad_proj))
+    upper = jnp.stack([grad_gain_two, grad_bias_two, total(grad_proj), total(grad_branch)])
+    lower = total(grad_hidden).reshape(4, D)
+    return attention, norm, matrices, (upper, lower)
+
+
+def input_gradient(grad_projected, weight_qkv, normal, inverse, gain, middle):
+    total = lambda value: jnp.sum(value.astype(F32), axis=0)
+    grad_normed = dot_rows(grad_projected, weight_qkv)
+    grad_in, grad_gain, grad_bias = norm_backward(grad_normed, normal, inverse, gain)
+    terms = [
+        grad_gain,
+        grad_bias,
         total(grad_projected[:, :D]),
         total(grad_projected[:, 2 * D :]),
-        total(grad_hidden).reshape(4, D),
-    )
-    return grad_input, matrices, terms
+    ]
+    return middle + grad_in, jnp.stack(terms)
 
 
 def body(
@@ -1511,38 +1948,43 @@
     out_bias,
     out_cotangent,
 ):
-    vectors = pack_vectors(
-        ln1_gain, ln1_bias, ln2_gain, ln2_bias, proj_bias, out_bias, attn_bias, fc_bias
-    )
-    resid, segs, gradient, vectors, qkv_full = links.open(
-        tokens[0], segment_ids, out_cotangent[0], vectors, attn_weight
-    )
-    weights = (qkv_full.reshape(-1, qkv_full.shape[-1]),)
-    shares = [proj_weight, fc_weight, out_weight]
-    resid = resid.astype(F32)
-    saved_layers = []
-    for layer_index in range(2):
-        resid, saved, weights = layer_forward(resid, weights, vectors, links, segs, shares)
-        saved_layers.append(saved)
-        shares = []
+    vectors = (
+        ln1_gain,
+        ln1_bias,
+        ln2_gain,
+        ln2_bias,
+        proj_bias,
+        out_bias,
+        attn_bias,
+        fc_bias,
+    )
+    shares = [attn_weight, proj_weight, fc_weight, out_weight]
+    resid, segs, vectors, weights, first = links.open(tokens[0], segment_ids, vectors, shares)
+    resid, saved = layer_forward(resid, weights, vectors, first)
+    saved_layers = [saved]
+    first = project_rows(resid, vectors, weights[0])
+    attended, gradient = links.attend(*first[3:], segs, out_cotangent[0])
+    resid, saved = layer_forward(resid, weights, vectors, first + tuple(attended))
+    saved_layers.append(saved)
     output = links.leave(resid.astype(BF16))
     gradient = gradient.astype(F32)
-    collected = []
-    for layer_index in (1, 0):
-        gradient, matrices, terms = layer_backward(
-            gradient, weights, vectors, saved_layers[layer_index], links, segs
-        )
-        collected.append((matrices, terms))
-    tokens_grad = links.leave(gradient.astype(BF16))
-
-    factors = []
-    for second, first in zip(collected[0][0], collected[1][0]):
-        left = jnp.concatenate([second[0], first[0]], axis=0)
-        right = jnp.concatenate([second[1], first[1]], axis=0)
-        factors.append((left, right))
-    added = [(a + b).reshape(-1, D) for a, b in zip(collected[0][1], collected[1][1])]
-    packed = jnp.concatenate(added + [jnp.zeros((4, D), F32)], axis=0)
-    (out_grad, fc_grad, proj_grad, qkv_grad), summed = links.sum_gradients(factors, packed)
+    attention, norm, later, (upper, lower) = layer_backward(
+        gradient, weights, vectors, saved_layers[1], links, segs
+    )
+    later_projected = links.attend_back(*attention)
+    gradient, terms = input_gradient(later_projected, weights[0], *norm)
+    attention, norm, first, (more_upper, more_lower) = layer_backward(
+        gradient, weights, vectors, saved_layers[0], links, segs
+    )
+    both = lambda a, b: jnp.concatenate([a, b], axis=0)
+    factors = [(both(a[0], b[0]), both(a[1], b[1])) for a, b in zip(later, first)]
+    factors.append(both(saved_layers[1][0], saved_layers[0][0]))
+    packed = jnp.concatenate(
+        [terms[:2], upper + more_upper, terms[2:], lower + more_lower, jnp.zeros((4, D), F32)], axis=0
+    )
+    (out_grad, fc_grad, proj_grad, qkv_grad), summed, tokens_grad = links.close(
+        attention, norm, factors, later_projected, packed, weights[0]
+    )
     own = lax.axis_index("fsdp")
     pick = lambda value, axis: lax.dynamic_index_in_dim(value, own, axis, keepdims=False)
     small = pick(summed[:6].reshape(6, 4, -1), 1)

time: 342 us -> 310 us (0.906)
  Pallas kernels: 269 us -> 256 us
  local copies, waits for them, and re-layouts: 22.6 us -> 10.2 us
  matrix products: 35.3 us -> 30.8 us
    pallas_call x2 -> x1, Pallas kernels: 53.8 us -> 34 us  [attend_back(): pl.pallas_call(attend_back_kernel, in_specs=[vmem] * 6 + [pl.BlockSpec(me...]
    unnamed x132 -> x36, local copies, waits for them, and re-layouts: 11.8 us -> 2.34 us
    pallas_call x4 -> x3, Pallas kernels: 215 us -> 222 us  [the longest x1 132 us: closing(): pl.pallas_call(partial(closing_kernel, places, count), in_specs=[vmem] *...]
    pad x7 -> x0, local copies, waits for them, and re-layouts: 4.64 us -> none  [pack_vectors(): jnp.pad(row.astype(F32), (0, D - row.shape[0]))]
    dot_general x8 -> x7, matrix products: 12.6 us -> 9.73 us  [dot_rows(): lax.dot_general(left, right, (((1,), (1,)), ((), ())), preferred_element_...]
    dot_general x4 -> x3, matrix products: 10.6 us -> 8.69 us  [column_products(): lax.dot_general(left, right, (((0,), (0,)), ((), ())), preferred_element_...]
  transfers between devices with their start and end apart: 2 -> 1, of which waited for: 0 -> 0; matrix products, arithmetic and copies ran while one was open for 6% -> 11% of each run, Pallas kernels for 34% -> 54%
where the time goes in v4:
time: 310 us
  Pallas kernels  256 us (83%)
  matrix products  30.8 us (10%)
  other arithmetic  10.7 us (3%)
  local copies, waits for them, and re-layouts  10.2 us (3%)
    pallas_call x1, Pallas kernels, closing(): pl.pallas_call(partial(closing_kernel, places, count), in_specs=[vmem] *...  132 us
    pallas_call x1, Pallas kernels, opening(): pl.pallas_call(partial(opening_kernel, count), in_specs=[anywhere] * (3 +...  65.8 us
    pallas_call x1, Pallas kernels, attend_back(): pl.pallas_call(attend_back_kernel, in_specs=[vmem] * 6 + [pl.BlockSpec(me...  34 us
    pallas_call x1, Pallas kernels, attend(): pl.pallas_call(attend_kernel, in_specs=[vmem, vmem, vmem, anywhere], out_...  23.8 us
    dot_general x7, matrix products, dot_rows(): lax.dot_general(left, right, (((1,), (1,)), ((), ())), preferred_element_...  9.73 us
    dot_general x3, matrix products, column_products(): lax.dot_general(left, right, (((0,), (0,)), ((), ())), preferred_element_...  8.69 us
    convert_element_type x4, other arithmetic, close(): return ([total.astype(F32) for total in sums], vectors, tokens_grad)  6.78 us
  transfers between devices with their start and end apart: 1, of which 0 were waited for; matrix products, arithmetic and copies ran while one was open for 11% of the time, Pallas kernels for 54%

profile of v4, /device:TPU:0, one launch (start us, length us, event | category | flops | bytes accessed | tf_op | source)
XLA Modules:
  0.0 309.5 jit_solution(13456769205571979472)
XLA Ops:
  0.7 65.8 %opening.1 = (bf16[128,768]{1,0:T(8,128)(2,1)}, s32[8,16,128]{2,1,0:T(8,128)}, f32[16,768]{1,0:T(8,128)}, bf16[128,768]{1,0:T(8,128)(2,1)}, f32[128,768]{1,0:T(8...) custom-call(bf16[128,768]{1,0:T(8,128)(2,1)} %bitcast.68, ...), custom_call_target="tpu_custom_call" | custom-call | tf_op jit(solution)/shard_map/opening/pallas_call | solution.py:1028
  66.4 1.6 fusion.57
  68.1 0.7 slice.88
  68.8 1.8 fusion.58
  71.0 3.8 %multiply_convert_fusion.1 = (bf16[128,3072]{1,0:T(8,128)(2,1)S(1)}, f32[128,3072]{1,0:T(8,128)S(1)}) fusion(f32[3072]{0:T(1024)S(1)} %add.181, bf16[128,768]{1,0:T(8,128)(2,1)S(1)} %add_convert_fusion.2, bf16[768,3072]{1,0:T(8,128)(2,1)} %bitcast.56), kind=kOutput, calls=%fused_computation.33 | convolution fusion | flops 607911936 | bytes 7286784 | tf_op jit(solution)/shard_map/dot_general | solution.py:1846
  74.8 0.9 fusion.59
  75.7 0.2 multiply_reduce_fusion.7
  76.1 0.7 copy-done.3
  76.8 0.6 fusion
  77.7 23.8 %attend.1 = (bf16[128,768]{1,0:T(8,128)(2,1)S(1)}, f32[128,128]{1,0:T(8,128)S(1)}, f32[16,128]{1,0:T(8,128)S(1)}, bf16[8,128,1536]{2,1,0:T(8,128)(2,1)S(1)}, bf16[128,768]{1,0:T(8,128)(2,1)S(1)}) custom-call(bf16[128,768]{1,0:T(8,128)(2,1)S(1)} %slice.107.q_ref, bf16[128,1536]{1,0:T(8,128)(2,1)S(1)} %slice.108.kv_ref, s32[8,16,128]{2,1,0:T(8,128)S(1)} %copy-done.1, ...), custom_call_target="tpu_custom_call" | custom-call | tf_op jit(solution)/shard_map/attend/pallas_call | solution.py:769
  101.6 0.4 fusion.60
  102.4 1.6 fusion.61
  104.1 2.0 convert_reduce_fusion.1
  106.0 0.8 fusion.25
  106.8 0.7 collective-permute-start
  107.5 1.8 multiply_reduce_fusion.1
  109.4 0.2 convert_reduce_fusion.7
  109.6 0.5 convolution_convert_fusion.4.grad_ref
  110.1 0.5 fusion.39.delta_ref
  110.6 0.3 fusion.40
  110.9 34.0 %attend_back.1.refs_11_ = bf16[128,2304]{1,0:T(8,128)(2,1)S(1)} custom-call(bf16[128,768]{1,0:T(8,128)(2,1)S(1)} %slice.107.q_ref, bf16[128,768]{1,0:T(8,128)(2,1)S(1)} %convolution_convert_fusion.4.grad_ref, f32[32,128]{1,0:T(8,128)S(1)} %pad_maximum_fusion.1.stats_ref, f32[128,128]{1,0:T(8,128)S(1)} %get-tuple-element.52.lse_ref, ...), custom_call_target="tpu_custom_call" | custom-call | tf_op jit(solution)/shard_map/attend_back/pallas_call | solution.py:1240
  144.9 1.4 multiply_reduce_fusion.2
  146.4 0.2 convert_reduce_fusion.5
  146.6 2.0 convert_reduce_fusion
  148.5 1.9 multiply_reduce_fusion
  150.4 3.6 %convolution_convert_fusion = bf16[768,3072]{1,0:T(8,128)(2,1)} fusion(bf16[128,3072]{1,0:T(8,128)(2,1)S(1)} %get-tuple-element.87, bf16[128,3072]{1,0:T(8,128)(2,1)S(1)} %get-tuple-element.89, bf16[128,768]{1,0:T(8,128)(2,1)S(1)} %add_convert_fusion.2, bf16[128,768]{1,0:T(8,128)(2,1)S(1)} %add_convert_fusion), kind=kOutput, calls=%fused_computation | convolution fusion | flops 1214251008 | bytes 6684672 | tf_op jit(solution)/shard_map/dot_general | solution.py:59
  154.0 3.6 %convolution_convert_fusion.1 = bf16[3072,768]{1,0:T(8,128)(2,1)} fusion(bf16[128,3072]{1,0:T(8,128)(2,1)S(1)} %get-tuple-element.118, bf16[128,3072]{1,0:T(8,128)(2,1)S(1)} %get-tuple-element.99, bf16[128,768]{1,0:T(8,128)(2,1)S(1)} %get-tuple-element.94, bf16[128,768]{1,0:T(8,128)(2,1)S(1)} %get-tuple-element.50), kind=kOutput, calls=%fused_computation.1 | convolution fusion | flops 1214251008 | bytes 6684672 | tf_op jit(solution)/shard_map/dot_general | solution.py:59
  157.7 0.9 convert_reduce_fusion.6
  158.6 1.5 convolution_convert_fusion.2
  160.1 0.5 convolution_convert_fusion.3.refs_1_
  160.7 1.1 fusion.38.refs_4_
  161.8 0.3 fusion.41
  162.3 0.8 pad_maximum_fusion.refs_10_
  163.1 1.2 concatenate.40.refs_12_
  164.4 0.6 pad_maximum_fusion.2.refs_2_
  165.0 132.3 %closing.1 = (bf16[768,768]{1,0:T(8,128)(2,1)}, bf16[192,3072]{1,0:T(8,128)(2,1)}, bf16[192,768]{1,0:T(8,128)(2,1)}, bf16[192,2304]{1,0:T(8,128)(2,1)}, f32[16,768]{1,0:T(8,128)}, /*index=5*/bf16[128,768]{1,0:T(8,128)(2,1)}) custom-call(bf16[128,768]{1,0:T(8,128)(2,1)} %get-tuple-element.49.refs_0_, bf16[128,768]{1,0:T(8,128)(2,1)} %copy-done.5, ...), custom_call_target="tpu_custom_call" | custom-call | tf_op jit(solution)/shard_map/closing/pallas_call | solution.py:1679
  297.2 0.7 slice.98
  298.0 0.7 slice.105
  298.7 0.7 slice.101
  299.5 3.0 convert_element_type.140
  302.5 1.6 convert_element_type.141
  304.1 1.3 convert_element_type.138
  305.4 0.9 convert_element_type.139
  306.4 0.6 fusion.51
  307.0 0.6 dynamic-slice_reduce_fusion
  307.6 0.6 constant_dynamic-slice_fusion.6
  308.2 0.7 copy.31
  308.8 0.7 copy.32
  (79 shorter events, 1.6 us)
Async XLA Ops:
  70.8 3.9 %slice-start = ((s8[4718592]{0:T(1024)(128)(4,1)}), s8[4194304]{0:T(1024)(128)(4,1)S(1)}, s32[]{:S(2)}) async-start(s8[4718592]{0:T(1024)(128)(4,1)} %bitcast.46), calls=%async_computation | async-start | bytes 8388608
  71.0 3.8 %slice-start.1 = ((s8[4718592]{0:T(1024)(128)(4,1)}), s8[524288]{0:T(1024)(128)(4,1)S(1)}, s32[]{:S(2)}) async-start(s8[4718592]{0:T(1024)(128)(4,1)} %bitcast.46), calls=%async_computation.1 | async-start | bytes 1048576
  74.8 2.0 copy-start.3
  76.8 0.8 copy-start.1
  76.8 1.0 copy-start.2
  76.8 27.3 %slice-start.2 = ((s8[4718592]{0:T(1024)(128)(4,1)}), s8[4194304]{0:T(1024)(128)(4,1)S(1)}, s32[]{:S(2)}) async-start(s8[4718592]{0:T(1024)(128)(4,1)} %bitcast.57), calls=%async_computation.2 | async-start | bytes 8388608
  77.4 24.2 %copy-start.4 = (bf16[4,192,768]{2,1,0:T(8,128)(2,1)S(1)}, bf16[4,192,768]{2,1,0:T(8,128)(2,1)}, u32[]{:S(2)}) copy-start(bf16[4,192,768]{2,1,0:T(8,128)(2,1)} %get-tuple-element.42) | copy-start | bytes 3538948
  101.6 2.4 slice-start.3
  106.8 201.3 %collective-permute-start = (bf16[128,768]{1,0:T(8,128)(2,1)S(1)}, bf16[128,768]{1,0:T(8,128)(2,1)S(1)}, u32[]{:S(2)}, u32[]{:S(2)}) collective-permute-start(bf16[128,768]{1,0:T(8,128)(2,1)S(1)} %fusion.25), channel_id=1, source_target_pairs={{0,0},{1,8},{2,16},{3,24},{4,4},{5,12},{6,20},{7,28},{8,1},{9,9},{... | collective-permute-start | bytes 589832 | tf_op jit(solution)/shard_map/ppermute | solution.py:1724
  144.9 12.6 %copy-start = (bf16[128,2304]{1,0:T(8,128)(2,1)}, bf16[128,2304]{1,0:T(8,128)(2,1)S(1)}, u32[]{:S(2)}) copy-start(bf16[128,2304]{1,0:T(8,128)(2,1)S(1)} %attend_back.1.refs_11_) | copy-start | bytes 1769476
  157.6 1.0 copy-start.8
  160.1 2.1 copy-start.11
  160.1 4.2 %copy-start.12 = (f32[16,128]{1,0:T(8,128)S(1)}, f32[16,128]{1,0:T(8,128)}, u32[]{:S(2)}) copy-start(f32[16,128]{1,0:T(8,128)} %get-tuple-element.54) | copy-start | bytes 24580
  160.7 4.3 %copy-start.5 = (bf16[128,768]{1,0:T(8,128)(2,1)}, bf16[128,768]{1,0:T(8,128)(2,1)S(1)}, u32[]{:S(2)}) copy-start(bf16[128,768]{1,0:T(8,128)(2,1)S(1)} %convolution_convert_fusion.3.refs_1_) | copy-start | bytes 589828
  299.5 3.0 copy-start.6
  302.5 1.6 copy-start.7
  304.1 1.3 copy-start.9
  304.1 4.8 %copy-start.10 = (bf16[128,768]{1,0:T(8,128)(2,1)S(1)}, bf16[128,768]{1,0:T(8,128)(2,1)}, u32[]{:S(2)}) copy-start(bf16[128,768]{1,0:T(8,128)(2,1)} %get-tuple-element.60) | copy-start | bytes 589828

commit v5 on v4

--- a/solution.py
+++ b/solution.py
@@ -1201,18 +1201,30 @@
 
 
 def attend_back_kernel(
-    q_ref, grad_ref, stats_ref, lse_ref, delta_ref, segs_ref, kv_ref, out_ref, *scratch
+    q_ref,
+    grad_ref,
+    stats_ref,
+    lse_ref,
+    delta_ref,
+    segs_ref,
+    next_q_ref,
+    kv_ref,
+    out_ref,
+    next_q_out,
+    *scratch,
 ):
     kv_all, q_all, grad_all, stats_all = scratch[:4]
     biases, sums = scratch[4:6], scratch[6:9]
-    send_sems, recv_sems, local_sem = scratch[9:]
+    next_q_all, send_sems, recv_sems, local_sems = scratch[ATTENTION_SCRATCH:]
     place = Place()
     greet((place.sibling, place.over_x, place.over_y))
     copies = Copies(send_sems, recv_sems)
     gather = BlockGather(
         place, copies, [q_ref, grad_ref, stats_ref], [q_all, grad_all, stats_all]
     )
-    load = pltpu.make_async_copy(kv_ref, kv_all, local_sem)
+    ahead = BlockGather(place, copies, [next_q_ref], [next_q_all])
+    load = pltpu.make_async_copy(kv_ref, kv_all, local_sems.at[0])
+    save = pltpu.make_async_copy(next_q_all, next_q_out, local_sems.at[1])
     load.start()
     gather.begin()
     grads = AttentionGrads(
@@ -1222,37 +1234,51 @@
     load.wait()
     grads.query_grads(0, 2)
     gather.first_halves()
+    ahead.begin()
     grads.query_grads(2, PAIRS)
     gather.second_halves()
     gather.wait_near()
     grads.near_keys()
     gather.corners()
     gather.wait_far()
+    ahead.first_halves()
     grads.far_keys()
+    ahead.second_halves()
+    ahead.corners()
     grads.store(out_ref)
+    ahead.wait_near()
+    ahead.wait_far()
+    save.start()
     gather.finish()
-
-
-def attend_back(queries, grads, stats, lse, delta, segs, kv, collective_id):
+    ahead.finish()
+    save.wait()
+
+
+def attend_back(queries, grads, stats, lse, delta, segs, next_queries, kv, collective_id):
     rows = queries.shape[0]
-    slots = 3 * BLOCK_COPIES
+    slots = 4 * BLOCK_COPIES
     vmem = pl.BlockSpec(memory_space=pltpu.VMEM)
+    anywhere = pl.BlockSpec(memory_space=pl.ANY)
     return pl.pallas_call(
         attend_back_kernel,
-        in_specs=[vmem] * 6 + [pl.BlockSpec(memory_space=pl.ANY)],
-        out_specs=vmem,
-        out_shape=jax.ShapeDtypeStruct((rows, 3 * D), BF16),
+        in_specs=[vmem] * 7 + [anywhere],
+        out_specs=[vmem, anywhere],
+        out_shape=[
+            jax.ShapeDtypeStruct((rows, 3 * D), BF16),
+            jax.ShapeDtypeStruct((8, rows, D), BF16),
+        ],
         scratch_shapes=attention_scratch(rows)
         + [
+            pltpu.VMEM((8, rows, D), BF16),
             pltpu.SemaphoreType.DMA((slots,)),
             pltpu.SemaphoreType.DMA((slots,)),
-            pltpu.SemaphoreType.DMA,
+            pltpu.SemaphoreType.DMA((2,)),
         ],
         compiler_params=pltpu.CompilerParams(
             collective_id=collective_id, has_side_effects=True, vmem_limit_bytes=32 << 20
         ),
         name="attend_back",
-    )(queries, grads, stats, lse, delta, segs, kv)
+    )(queries, grads, stats, lse, delta, segs, next_queries, kv)
 
 
 CHUNK_ROWS, CHUNK_COLUMNS = 192, 768
@@ -1261,19 +1287,23 @@
 
 
 def chunk_places(shapes):
-    return [
-        (which, row, column)
+    places = [
+        (which, row, column, CHUNK_COLUMNS)
         for which, (rows, columns) in enumerate(shapes)
         for row in range(0, rows, CHUNK_ROWS)
         for column in range(0, columns, CHUNK_COLUMNS)
     ]
-
-
+    which, row, column, width = places.pop()
+    cut = 2 * width // 3
+    return places + [(which, row, column, cut), (which, row, column + cut, width - cut)]
+
+
+CORE_SLOTS = 4
 REDUCE_STAGES = ("core0", "core1", "y", "x", "z", "zz", "zz_back", "z_back", "x_back")
 
 
 class GradientSum:
-    def __init__(self, place, copies, places, terms, sums, buffers, local_sems):
+    def __init__(self, place, copies, places, sums, buffers):
         self.place = place
         (
             self.own,
@@ -1285,52 +1315,41 @@
             self.got_z,
             self.to_zz,
             self.got_zz,
-            to_core,
+            self.to_core,
         ) = buffers
-        self.to_core = to_core
+        self.places = places
         self.x_rows, self.z_rows = CHUNK_ROWS // 2, CHUNK_ROWS // 4
-        self.zz_columns = CHUNK_COLUMNS // 2
-        x, y, core, low, high = place.x, place.y, place.core, place.low, place.high
+        x, y, low, high = place.x, place.y, place.low, place.high
         self.plans = []
         self.finals = []
-        self.loads = []
-        self.filled = []
-        for k, (which, row, column) in enumerate(places):
-            term, out = terms[which], sums[which]
-
-            def piece(first, rows, start, width, out=out, row=row, column=column):
+        for k, (which, row, column, width) in enumerate(places):
+            out = sums[which]
+            half = width // 2
+
+            def piece(first, rows, start, columns, out=out, row=row, column=column):
                 return out.at[
                     pl.ds(pl.multiple_of(row + first, 16), rows),
-                    pl.ds(pl.multiple_of(column + start, LANES), width),
+                    pl.ds(pl.multiple_of(column + start, LANES), columns),
                 ]
 
-            def quarter(index, term=term, row=row, column=column):
-                return term.at[index, pl.ds(row, CHUNK_ROWS), pl.ds(column, CHUNK_COLUMNS)]
-
-            if term is None:
-                sent = [to_core.at[len(self.filled), i] for i in range(2)]
-                self.filled.append((k, column))
-                loads = []
-            else:
-                sent = [quarter(1 - core), quarter(3 - core)]
-                loads = [
-                    pltpu.make_async_copy(
-                        quarter(2 * i + core), self.own.at[k, i], local_sems.at[2 * k + i]
-                    )
-                    for i in range(2)
-                ]
-            final = piece(
-                x * self.x_rows + low * self.z_rows, self.z_rows, high * self.zz_columns, self.zz_columns
-            )
-            wide = piece(x * self.x_rows + low * self.z_rows, self.z_rows, 0, CHUNK_COLUMNS)
-            tall = piece(x * self.x_rows, self.x_rows, 0, CHUNK_COLUMNS)
+            def wide_part(ref, *index, columns=width):
+                return ref.at[(*index, slice(None), pl.ds(0, columns))]
+
+            final = piece(x * self.x_rows + low * self.z_rows, self.z_rows, high * half, half)
+            wide = piece(x * self.x_rows + low * self.z_rows, self.z_rows, 0, width)
+            tall = piece(x * self.x_rows, self.x_rows, 0, width)
+            slot = k % CORE_SLOTS
             moves = (
-                (sent[0], self.got_core.at[k, 0], place.sibling),
-                (sent[1], self.got_core.at[k, 1], place.sibling),
-                (self.own.at[k, 1 - y], self.got_y.at[k], place.over_y),
-                (self.to_x.at[k], self.got_x.at[k], place.over_x),
-                (self.to_z.at[k], self.got_z.at[k], place.over_z),
-                (self.to_zz.at[k], self.got_zz.at[k], place.over_zz),
+                (wide_part(self.to_core, slot, 0), wide_part(self.got_core, k, 0), place.sibling),
+                (wide_part(self.to_core, slot, 1), wide_part(self.got_core, k, 1), place.sibling),
+                (wide_part(self.own, k, 1 - y), wide_part(self.got_y, k), place.over_y),
+                (wide_part(self.to_x, k), wide_part(self.got_x, k), place.over_x),
+                (wide_part(self.to_z, k), wide_part(self.got_z, k), place.over_z),
+                (
+                    wide_part(self.to_zz, k, columns=half),
+                    wide_part(self.got_zz, k, columns=half),
+                    place.over_zz,
+                ),
                 (final, final, place.over_zz),
                 (wide, wide, place.over_z),
                 (tall, tall, place.over_x),
@@ -1339,7 +1358,6 @@
                 {name: copies.make(*move) for name, move in zip(REDUCE_STAGES, moves)}
             )
             self.finals.append(final)
-            self.loads.append(loads)
         self.stages = (
             self.stage_x,
             self.stage_z,
@@ -1349,11 +1367,28 @@
             self.stage_x_back,
         )
 
-    def begin(self, k):
-        self.plans[k]["core0"].start()
-        self.plans[k]["core1"].start()
-        for load in self.loads[k]:
-            load.start()
+    def make(self, which, left, right):
+        core = self.place.core
+        for k, (owner, row, column, width) in enumerate(self.places):
+            if owner != which:
+                continue
+            quarter_rows = left.shape[0] // 4
+
+            def term(quarter):
+                first = pl.multiple_of(quarter * quarter_rows + row, 16)
+                rows = left[pl.ds(first, CHUNK_ROWS), :]
+                columns = right[:, column : column + width]
+                return jnp.dot(rows, columns, preferred_element_type=F32).astype(BF16)
+
+            if k >= CORE_SLOTS:
+                for name in ("core0", "core1"):
+                    self.plans[k - CORE_SLOTS][name].wait_send()
+            for i in range(2):
+                self.to_core[k % CORE_SLOTS, i, :, :width] = term(2 * i + 1 - core)
+            self.plans[k]["core0"].start()
+            self.plans[k]["core1"].start()
+            for i in range(2):
+                self.own[k, i, :, :width] = term(2 * i + core)
 
     def add_up(self, store, loads, rows):
         step = self.z_rows
@@ -1371,31 +1406,31 @@
         else:
             lax.fori_loop(0, rows // step, visit, 0)
 
-    def slab(self, ref, *index, first=0, start=None, width=None):
+    def slab(self, ref, *index, first=0, start=0, width=None):
         def load(offset, rows):
             place = pl.ds(pl.multiple_of(first + offset, 16), rows)
-            if width is None:
-                return ref[(*index, place)]
             return ref[(*index, place, pl.ds(pl.multiple_of(start, LANES), width))]
 
         return load
 
     def stage_y(self, k):
-        plan, y = self.plans[k], self.place.y
-        for load in self.loads[k]:
-            load.wait()
+        plan, y, width = self.plans[k], self.place.y, self.places[k][3]
         plan["core0"].wait_recv()
         plan["core1"].wait_recv()
 
         def store(offset, rows, value):
-            self.own[k, 1 - y, pl.ds(offset, rows)] = value
-
-        loads = [self.slab(self.own, k, 1 - y), self.slab(self.got_core, k, 1 - y)]
+            self.own[k, 1 - y, pl.ds(offset, rows), :width] = value
+
+        loads = [
+            self.slab(self.own, k, 1 - y, width=width),
+            self.slab(self.got_core, k, 1 - y, width=width),
+        ]
         self.add_up(store, loads, CHUNK_ROWS)
         plan["y"].start()
 
-    def terms_at(self, k, first, depth, inner=0, **part):
+    def terms_at(self, k, first, depth, inner=0, start=0, width=None):
         y = self.place.y
+        part = {"start": start, "width": self.places[k][3] if width is None else width}
         loads = [
             self.slab(self.own, k, y, first=first, **part),
             self.slab(self.got_core, k, y, first=first, **part),
@@ -1408,51 +1443,52 @@
         return loads
 
     def stage_x(self, k):
-        plan = self.plans[k]
+        plan, width = self.plans[k], self.places[k][3]
         plan["y"].wait_recv()
 
         def store(offset, rows, value):
-            self.to_x[k, pl.ds(offset, rows)] = value
+            self.to_x[k, pl.ds(offset, rows), :width] = value
 
         self.add_up(store, self.terms_at(k, (1 - self.place.x) * self.x_rows, 0), self.x_rows)
         plan["x"].start()
 
     def stage_z(self, k):
-        plan = self.plans[k]
+        plan, width = self.plans[k], self.places[k][3]
         plan["x"].wait_recv()
         inner = (1 - self.place.low) * self.z_rows
 
         def store(offset, rows, value):
-            self.to_z[k] = value
+            self.to_z[k, :, :width] = value
 
         first = self.place.x * self.x_rows + inner
         self.add_up(store, self.terms_at(k, first, 1, inner), self.z_rows)
         plan["z"].start()
 
-    def last_terms(self, k, start):
+    def last_terms(self, k, side):
         inner = self.place.low * self.z_rows
         first = self.place.x * self.x_rows + inner
-        return self.terms_at(k, first, 2, inner, start=start, width=self.zz_columns)
+        half = self.places[k][3] // 2
+        return self.terms_at(k, first, 2, inner, side * half, half)
 
     def stage_zz(self, k):
-        plan = self.plans[k]
+        plan, half = self.plans[k], self.places[k][3] // 2
         plan["z"].wait_recv()
 
         def store(offset, rows, value):
-            self.to_zz[k] = value
-
-        self.add_up(store, self.last_terms(k, (1 - self.place.high) * self.zz_columns), self.z_rows)
+            self.to_zz[k, :, :half] = value
+
+        self.add_up(store, self.last_terms(k, 1 - self.place.high), self.z_rows)
         plan["zz"].start()
 
     def stage_final(self, k):
-        plan = self.plans[k]
+        plan, half = self.plans[k], self.places[k][3] // 2
         plan["zz"].wait_recv()
 
         def store(offset, rows, value):
             self.finals[k][...] = value
 
-        terms = self.last_terms(k, self.place.high * self.zz_columns)
-        self.add_up(store, terms + [self.slab(self.got_zz, k)], self.z_rows)
+        terms = self.last_terms(k, self.place.high)
+        self.add_up(store, terms + [self.slab(self.got_zz, k, width=half)], self.z_rows)
         plan["zz_back"].start()
 
     def stage_z_back(self, k):
@@ -1472,13 +1508,14 @@
                 stage(tick - lag)
 
     def finish(self):
-        for plan in self.plans:
+        for k, plan in enumerate(self.plans):
             plan["x_back"].wait_recv()
-            for name in REDUCE_STAGES:
+            waited = k + CORE_SLOTS < len(self.plans)
+            for name in REDUCE_STAGES[2:] if waited else REDUCE_STAGES:
                 plan[name].wait_send()
 
 
-def reduce_scratch(chunks, filled):
+def reduce_scratch(chunks):
     rows, columns = CHUNK_ROWS, CHUNK_COLUMNS
     shapes = [
         (chunks, 2, rows, columns),
@@ -1490,18 +1527,17 @@
         (chunks, rows // 4, columns),
         (chunks, rows // 4, columns // 2),
         (chunks, rows // 4, columns // 2),
-        (filled, 2, rows, columns),
+        (CORE_SLOTS, 2, rows, columns),
     ]
     return [pltpu.VMEM(shape, BF16) for shape in shapes]
 
 
 REDUCE_SCRATCH = 10
-CLOSING_INPUTS = 14
+CLOSING_INPUTS = 10
 
 
 def closing_kernel(places, count, *refs):
     (
-        q_ref,
         grad_ref,
         stats_ref,
         lse_ref,
@@ -1511,49 +1547,67 @@
         inverse_ref,
         gain_ref,
         middle_ref,
-        left_ref,
-        later_ref,
         terms_ref,
-    ) = refs[: CLOSING_INPUTS - 1]
-    kv_ref, weight_ref = refs[CLOSING_INPUTS - 1 : CLOSING_INPUTS + 1]
-    partials = refs[CLOSING_INPUTS + 1 : CLOSING_INPUTS + 1 + count]
-    refs = refs[CLOSING_INPUTS + 1 + count :]
-    sums, vector_out, tokens_out = refs[: count + 1], refs[count + 1], refs[count + 2]
-    refs = refs[count + 3 :]
+    ) = refs[:CLOSING_INPUTS]
+    refs = refs[CLOSING_INPUTS:]
+    factors = refs[: 4 * count - 1]
+    q_ref, q_saved, kv_ref, weight_ref = refs[4 * count - 1 : 4 * count + 3]
+    refs = refs[4 * count + 3 :]
+    sums, vector_out, tokens_out = refs[:count], refs[count], refs[count + 1]
+    refs = refs[count + 2 :]
     kv_all, q_all, grad_all, stats_all = refs[:4]
     biases, attention_sums = refs[4:6], refs[6:9]
     refs = refs[ATTENTION_SCRATCH:]
     buffers = refs[:REDUCE_SCRATCH]
-    grads_ref, weight, turned, vector_got, tokens_own, send_sems, recv_sems, local_sems = refs[REDUCE_SCRATCH:]
+    (
+        grads_ref,
+        weight,
+        left,
+        right,
+        vector_got,
+        tokens_own,
+        send_sems,
+        recv_sems,
+        local_sems,
+    ) = refs[REDUCE_SCRATCH:]
 
     place = Place()
+    load_kv = pltpu.make_async_copy(kv_ref, kv_all, local_sems.at[0])
+    load_weight = pltpu.make_async_copy(weight_ref, weight, local_sems.at[1])
+    load_q = pltpu.make_async_copy(q_saved, q_all, local_sems.at[2])
+    load_kv.start()
+    load_q.start()
+    load_weight.start()
     greet_with_partner(
         place, (place.sibling, place.over_x, place.over_y, place.over_z, place.over_zz)
     )
     copies = Copies(send_sems, recv_sems)
-    gather = BlockGather(
-        place, copies, [q_ref, grad_ref, stats_ref], [q_all, grad_all, stats_all]
-    )
+    gather = BlockGather(place, copies, [grad_ref, stats_ref], [grad_all, stats_all])
     swap = copies.make(tokens_own, tokens_out, place.partner)
-    reduce = GradientSum(
-        place, copies, places, list(partials) + [None], sums, buffers, local_sems
-    )
+    reduce = GradientSum(place, copies, places, sums, buffers)
     chunks = len(places)
-    filled = len(reduce.filled)
-    early = chunks - filled
+    by_weight = [[k for k in range(chunks) if places[k][0] == which] for which in range(count)]
     vector_devices = (place.over_x, place.over_z, place.over_zz, place.sibling, place.over_y)
     vector_copies = [
         copies.make(vector_out, vector_got.at[i], device)
         for i, device in enumerate(vector_devices)
     ]
-    load_kv = pltpu.make_async_copy(kv_ref, kv_all, local_sems.at[2 * chunks])
-    load_weight = pltpu.make_async_copy(weight_ref, weight, local_sems.at[2 * chunks + 1])
-
-    load_kv.start()
+    tokens = grad_ref.shape[0]
+
+    def make_terms(which, last_right=None):
+        later_left, later_right, first_left = factors[4 * which : 4 * which + 3]
+        rows, columns = later_left.shape[1], later_right.shape[1]
+        left[:rows, :tokens] = later_left[...].T
+        left[:rows, tokens:] = first_left[...].T
+        right[:tokens, :columns] = later_right[...]
+        if last_right is None:
+            right[tokens:, :columns] = factors[4 * which + 3][...]
+        else:
+            right[tokens:, :columns] = last_right
+        reduce.make(which, left.at[pl.ds(0, rows), :], right)
+
     gather.begin()
-    for k in range(early):
-        reduce.begin(k)
-    load_weight.start()
+    make_terms(0)
     grads = AttentionGrads(
         place,
         q_ref,
@@ -1568,41 +1622,32 @@
         biases,
         attention_sums,
     )
+    gather.first_halves()
+    for k in by_weight[0]:
+        reduce.stage_y(k)
+    gather.second_halves()
     grads.masks()
-    turned[...] = left_ref[...].T
     load_kv.wait()
-    grads.query_grads(0, 2)
-    gather.first_halves()
-    reduce.stage_y(0)
-    grads.query_grads(2, PAIRS)
-    gather.second_halves()
-    for k in range(1, 4):
+    grads.query_grads(0, PAIRS)
+    gather.corners()
+    load_q.wait()
+    gather.wait_near()
+    make_terms(1)
+    for k in by_weight[1]:
         reduce.stage_y(k)
-    gather.wait_near()
+    reduce.tick(0)
     grads.near_keys()
-    gather.corners()
-    for k in range(4, early):
-        reduce.stage_y(k)
     gather.wait_far()
-    reduce.tick(0)
+    reduce.tick(1)
     grads.far_keys()
     grads.store(grads_ref)
-    reduce.tick(1)
-
+    reduce.tick(2)
+    make_terms(2)
+    for k in by_weight[2]:
+        reduce.stage_y(k)
     own_grads = grads_ref[...]
-    right = jnp.concatenate([later_ref[...], own_grads], axis=0)
-    for index, (k, column) in enumerate(reduce.filled):
-        columns = right[:, column : column + CHUNK_COLUMNS]
-
-        def term(quarter):
-            rows = turned[pl.ds(pl.multiple_of(quarter * CHUNK_ROWS, 16), CHUNK_ROWS), :]
-            return jnp.dot(rows, columns, preferred_element_type=F32).astype(BF16)
-
-        for i in range(2):
-            reduce.to_core[index, i] = term(2 * i + 1 - place.core)
-            reduce.own[k, i] = term(2 * i + place.core)
-        reduce.begin(k)
-    reduce.tick(2)
+    make_terms(3, own_grads)
+    reduce.tick(3)
     load_weight.wait()
     grad_normed = dot_rows(own_grads, weight[...])
     grad_input, grad_gain, grad_bias = norm_backward(
@@ -1625,7 +1670,7 @@
     for row, value in ((0, grad_gain[None]), (1, grad_bias[None]), (6, query_bias), (7, value_bias)):
         vector_out[row : row + 1, :] = vector_out[row : row + 1, :] + value
     vector_copies[0].start()
-    for k in range(early, chunks):
+    for k in by_weight[3]:
         reduce.stage_y(k)
 
     def vector_step(index):
@@ -1634,10 +1679,10 @@
         if index + 1 < VECTOR_AXES:
             vector_copies[index + 1].start()
 
-    for tick in range(3, reduce.ticks()):
+    for tick in range(4, reduce.ticks()):
         reduce.tick(tick)
-        if tick - 3 < VECTOR_AXES - 1:
-            vector_step(tick - 3)
+        if tick - 4 < VECTOR_AXES - 1:
+            vector_step(tick - 4)
     vector_step(VECTOR_AXES - 1)
     reduce.finish()
     gather.finish()
@@ -1648,74 +1693,43 @@
         swap.wait_send()
 
 
-def closing(
-    queries,
-    grads,
-    stats,
-    lse,
-    delta,
-    segs,
-    normal,
-    inverse,
-    gain,
-    middle,
-    left,
-    later,
-    terms,
-    kv,
-    weight,
-    partials,
-    collective_id,
-):
+def closing(attention, queries_saved, norm, terms, factors, weight, collective_id):
+    queries, grads, stats, lse, delta, segs, kv, _ = attention
     rows = queries.shape[0]
-    count = len(partials)
-    shapes = [term.shape[1:] for term in partials] + [(weight.shape[0] // 4, weight.shape[1])]
+    count = len(factors)
+    shapes = [(group[0].shape[1] // 4, group[1].shape[1]) for group in factors]
     places = chunk_places(shapes)
     chunks = len(places)
-    filled = len(chunk_places(shapes[-1:]))
-    slots = chunks * REDUCE_COPIES + VECTOR_AXES + 3 * BLOCK_COPIES + 1
+    slots = chunks * REDUCE_COPIES + VECTOR_AXES + 2 * BLOCK_COPIES + 1
+    flat = [factor for group in factors for factor in group]
+    tallest = max(group[0].shape[1] for group in factors)
+    widest = max(group[1].shape[1] for group in factors)
     vmem = pl.BlockSpec(memory_space=pltpu.VMEM)
     anywhere = pl.BlockSpec(memory_space=pl.ANY)
     return pl.pallas_call(
         partial(closing_kernel, places, count),
-        in_specs=[vmem] * (CLOSING_INPUTS - 1) + [anywhere] * (2 + count),
-        out_specs=[vmem] * (count + 3),
+        in_specs=[vmem] * (CLOSING_INPUTS + len(flat) + 1) + [anywhere] * 3,
+        out_specs=[vmem] * (count + 2),
         out_shape=[jax.ShapeDtypeStruct(shape, BF16) for shape in shapes]
         + [jax.ShapeDtypeStruct(terms.shape, F32), jax.ShapeDtypeStruct((rows, D), BF16)],
         scratch_shapes=attention_scratch(rows)
-        + reduce_scratch(chunks, filled)
+        + reduce_scratch(chunks)
         + [
             pltpu.VMEM((rows, 3 * D), BF16),
             pltpu.VMEM(weight.shape, BF16),
-            pltpu.VMEM(left.shape[::-1], BF16),
+            pltpu.VMEM((tallest, 2 * rows), BF16),
+            pltpu.VMEM((2 * rows, widest), BF16),
             pltpu.VMEM((VECTOR_AXES, *terms.shape), F32),
             pltpu.VMEM((rows, D), BF16),
             pltpu.SemaphoreType.DMA((slots,)),
             pltpu.SemaphoreType.DMA((slots,)),
-            pltpu.SemaphoreType.DMA((2 * chunks + 2,)),
+            pltpu.SemaphoreType.DMA((3,)),
         ],
         compiler_params=pltpu.CompilerParams(
             collective_id=collective_id, has_side_effects=True, vmem_limit_bytes=60 << 20
         ),
         name="closing",
-    )(
-        queries,
-        grads,
-        stats,
-        lse,
-        delta,
-        segs,
-        normal,
-        inverse,
-        gain,
-        middle,
-        left,
-        later,
-        terms,
-        kv,
-        weight,
-        *partials,
-    )
+    )(grads, stats, lse, delta, segs, *norm, terms, *flat, queries, queries_saved, kv, weight)
 
 
 class PlaneLinks:
@@ -1731,34 +1745,12 @@
         *results, cotangent = attend(queries, kv_own, segs, cotangent, 2)
         return results, cotangent
 
-    def attend_back(self, queries, grads, stats, lse, delta, segs, kv, kv_own):
-        return attend_back(queries, grads, stats, lse, delta, segs, kv, 3)
-
-    def close(self, attention, norm, factors, later, vectors, weight):
-        queries, grads, stats, lse, delta, segs, kv, _ = attention
-        normal, inverse, gain, middle = norm
-        terms = []
-        for left, right in factors[:-1]:
-            term = column_products(left, right).astype(BF16)
-            terms.append(term.reshape(4, term.shape[0] // 4, term.shape[1]))
+    def attend_back(self, attention, next_queries):
+        return attend_back(*attention[:6], next_queries, attention[6], 3)
+
+    def close(self, attention, queries_saved, norm, factors, vectors, weight):
         *sums, vectors, tokens_grad = closing(
-            queries,
-            grads,
-            stats,
-            lse,
-            delta,
-            segs,
-            normal,
-            inverse,
-            gain,
-            middle,
-            factors[-1],
-            later,
-            vectors,
-            kv,
-            weight,
-            terms,
-            4,
+            attention, queries_saved, norm, vectors, factors, weight, 4
         )
         return [total.astype(F32) for total in sums], vectors, tokens_grad
 
@@ -1791,7 +1783,8 @@
         kv = self.blocks(kv_own).reshape(-1, 2 * D)
         return (*attention_forward(start, queries, kv, own_segs, all_segs), kv), cotangent
 
-    def attend_back(self, queries, grads, stats, lse, delta, segs, kv, kv_own):
+    def attend_back(self, attention, next_queries):
+        queries, grads, stats, lse, delta, segs, kv, kv_own = attention
         start, own_segs, all_segs = self.place(segs)
         q_all = self.blocks(queries).reshape(-1, D)
         grad_all = self.blocks(grads).reshape(-1, D)
@@ -1808,17 +1801,18 @@
             self.blocks(stats),
             own_segs,
             all_segs,
-        )
-
-    def close(self, attention, norm, factors, later, vectors, weight):
-        grad_projected = self.attend_back(*attention)
+        ), None
+
+    def close(self, attention, queries_saved, norm, factors, vectors, weight):
+        grad_projected, _ = self.attend_back(attention, None)
         grad_input, terms = input_gradient(grad_projected, weight, *norm)
         vectors = vectors + jnp.concatenate(
             [terms[:2], jnp.zeros((4, D), F32), terms[2:], jnp.zeros((8, D), F32)], axis=0
         )
-        right = jnp.concatenate([later, grad_projected], axis=0)
         sums = []
-        for left, right in factors[:-1] + [(factors[-1], right)]:
+        for later_left, later_right, first_left, *first_right in factors:
+            left = jnp.concatenate([later_left, first_left], axis=0)
+            right = jnp.concatenate([later_right, *(first_right or [grad_projected])], axis=0)
             term = column_products(left, right).astype(BF16)
             share = lax.psum_scatter(term, "fsdp", scatter_dimension=0, tiled=True)
             sums.append(lax.psum(share.astype(F32), "ctx"))
@@ -1971,19 +1965,18 @@
     attention, norm, later, (upper, lower) = layer_backward(
         gradient, weights, vectors, saved_layers[1], links, segs
     )
-    later_projected = links.attend_back(*attention)
+    later_projected, queries_saved = links.attend_back(attention, saved_layers[0][3])
     gradient, terms = input_gradient(later_projected, weights[0], *norm)
     attention, norm, first, (more_upper, more_lower) = layer_backward(
         gradient, weights, vectors, saved_layers[0], links, segs
     )
-    both = lambda a, b: jnp.concatenate([a, b], axis=0)
-    factors = [(both(a[0], b[0]), both(a[1], b[1])) for a, b in zip(later, first)]
-    factors.append(both(saved_layers[1][0], saved_layers[0][0]))
+    factors = [(*a, *b) for a, b in zip(later, first)]
+    factors.append((saved_layers[1][0], later_projected, saved_layers[0][0]))
     packed = jnp.concatenate(
         [terms[:2], upper + more_upper, terms[2:], lower + more_lower, jnp.zeros((4, D), F32)], axis=0
     )
     (out_grad, fc_grad, proj_grad, qkv_grad), summed, tokens_grad = links.close(
-        attention, norm, factors, later_projected, packed, weights[0]
+        attention, queries_saved, norm, factors, packed, weights[0]
     )
     own = lax.axis_index("fsdp")
     pick = lambda value, axis: lax.dynamic_index_in_dim(value, own, axis, keepdims=False)

time: 310 us -> 297 us (0.958)
  matrix products: 30.8 us -> 22.1 us
  Pallas kernels: 256 us -> 252 us
    pallas_call x1, Pallas kernels: 132 us -> 122 us  [closing(): pl.pallas_call(partial(closing_kernel, places, count), in_specs=[vmem] *...]
    dot_general x3 -> x0, matrix products: 8.69 us -> none  [column_products(): lax.dot_general(left, right, (((0,), (0,)), ((), ())), preferred_element_...]
    pallas_call x1, Pallas kernels: 34 us -> 40 us  [attend_back(): pl.pallas_call(attend_back_kernel, in_specs=[vmem] * 7 + [anywhere], out_...]
  transfers between devices with their start and end apart: 1 -> 1, of which waited for: 0 -> 0; matrix products, arithmetic and copies ran while one was open for 11% -> 8% of each run, Pallas kernels for 54% -> 55%
where the time goes in v5:
time: 297 us; the launch traced here: 296 us
  Pallas kernels  252 us (85%)
  matrix products  22.1 us (7%)
  local copies, waits for them, and re-layouts  10.7 us (4%)
  other arithmetic  9.83 us (3%)
    pallas_call x1, Pallas kernels, closing(): pl.pallas_call(partial(closing_kernel, places, count), in_specs=[vmem] *...  122 us
    pallas_call x1, Pallas kernels, opening(): pl.pallas_call(partial(opening_kernel, count), in_specs=[anywhere] * (3 +...  65.8 us
    pallas_call x1, Pallas kernels, attend_back(): pl.pallas_call(attend_back_kernel, in_specs=[vmem] * 7 + [anywhere], out_...  40 us
    pallas_call x1, Pallas kernels, attend(): pl.pallas_call(attend_kernel, in_specs=[vmem, vmem, vmem, anywhere], out_...  23.9 us
    dot_general x7, matrix products, dot_rows(): lax.dot_general(left, right, (((1,), (1,)), ((), ())), preferred_element_...  9.67 us
    convert_element_type x4, other arithmetic, close(): return ([total.astype(F32) for total in sums], vectors, tokens_grad)  6.68 us
  transfers between devices with their start and end apart: 1, of which 0 were waited for; matrix products, arithmetic and copies ran while one was open for 8% of the time, Pallas kernels for 55%

profile of v5, /device:TPU:0, one launch (start us, length us, event | category | flops | bytes accessed | tf_op | source)
XLA Modules:
  0.0 296.4 jit_solution(10715278543988476357)
XLA Ops:
  0.7 65.8 %opening.1 = (bf16[128,768]{1,0:T(8,128)(2,1)}, s32[8,16,128]{2,1,0:T(8,128)}, f32[16,768]{1,0:T(8,128)}, bf16[128,768]{1,0:T(8,128)(2,1)}, f32[128,768]{1,0:T(8...) custom-call(bf16[128,768]{1,0:T(8,128)(2,1)} %bitcast.62, ...), custom_call_target="tpu_custom_call" | custom-call | tf_op jit(solution)/shard_map/opening/pallas_call | solution.py:1028
  66.4 1.6 fusion.36
  68.0 0.7 slice.88
  68.8 1.8 fusion.37
  70.6 0.2 multiply_reduce_fusion.8
  70.8 0.1 add_convert_fusion.2.refs_16_
  71.0 3.8 %multiply_convert_fusion.1 = (bf16[128,3072]{1,0:T(8,128)(2,1)S(1)}, f32[128,3072]{1,0:T(8,128)S(1)}) fusion(f32[3072]{0:T(1024)S(1)} %add.181, bf16[128,768]{1,0:T(8,128)(2,1)S(1)} %add_convert_fusion.2.refs_16_, bf16[768,3072]{1,0:T(8,128)(2,1)} %bitcast.52), kind=kOutput, calls=%fused_computation.25 | convolution fusion | flops 607911936 | bytes 7286784 | tf_op jit(solution)/shard_map/dot_general | solution.py:1840
  74.8 0.9 fusion.38
  75.7 0.2 multiply_reduce_fusion.7
  76.1 1.0 copy-done.7
  77.1 0.6 fusion
  78.1 23.9 %attend.1 = (bf16[128,768]{1,0:T(8,128)(2,1)S(1)}, f32[128,128]{1,0:T(8,128)S(1)}, f32[16,128]{1,0:T(8,128)S(1)}, bf16[8,128,1536]{2,1,0:T(8,128)(2,1)S(1)}, bf16[128,768]{1,0:T(8,128)(2,1)S(1)}) custom-call(bf16[128,768]{1,0:T(8,128)(2,1)S(1)} %slice.107.q_ref, bf16[128,1536]{1,0:T(8,128)(2,1)S(1)} %slice.108.kv_ref, s32[8,16,128]{2,1,0:T(8,128)S(1)} %copy-done.5, ...), custom_call_target="tpu_custom_call" | custom-call | tf_op jit(solution)/shard_map/attend/pallas_call | solution.py:769
  102.0 0.4 fusion.39
  102.4 1.6 fusion.40
  104.0 0.2 multiply_reduce_fusion.6
  104.2 0.1 add_convert_fusion.refs_14_
  104.4 2.0 convert_reduce_fusion.1
  106.4 0.8 fusion.19
  107.3 0.7 collective-permute-start
  108.0 1.8 multiply_reduce_fusion.1
  109.8 0.2 convert_reduce_fusion.7
  110.1 0.5 convolution_convert_fusion.1.grad_ref
  110.6 0.3 fusion.22
  110.9 0.5 fusion.21.delta_ref
  111.5 40.0 %attend_back.1 = (bf16[128,2304]{1,0:T(8,128)(2,1)S(1)}, bf16[8,128,768]{2,1,0:T(8,128)(2,1)S(1)}) custom-call(bf16[128,768]{1,0:T(8,128)(2,1)S(1)} %slice.107.q_ref, bf16[128,768]{1,0:T(8,128)(2,1)S(1)} %convolution_convert_fusion.1.grad_ref, f32[32,128]{1,0:T(8,128)S(1)} %pad_maximum_fusion.stats_ref, f32[128,128]{1,0:T(8,128)S(1)} %get-tuple-element.53.lse_ref, ...), custom_call_target="tpu_custom_call" | custom-call | tf_op jit(solution)/shard_map/attend_back/pallas_call | solution.py:1262
  151.5 1.4 multiply_reduce_fusion.2
  152.9 0.2 convert_reduce_fusion.5
  153.1 2.0 convert_reduce_fusion
  155.1 1.8 multiply_reduce_fusion
  157.0 1.0 convert_reduce_fusion.6
  157.9 0.5 convolution_convert_fusion.refs_0_
  158.5 0.3 fusion.23
  158.8 1.1 fusion.20.refs_3_
  160.2 1.3 concatenate.18.refs_9_
  161.5 0.6 pad_maximum_fusion.1.refs_1_
  162.1 122.1 %closing.1 = (bf16[768,768]{1,0:T(8,128)(2,1)}, bf16[192,3072]{1,0:T(8,128)(2,1)}, bf16[192,768]{1,0:T(8,128)(2,1)}, bf16[192,2304]{1,0:T(8,128)(2,1)}, f32[16,768]{1,0:T(8,128)}, /*index=5*/bf16[128,768]{1,0:T(8,128)(2,1)}) custom-call(bf16[128,768]{1,0:T(8,128)(2,1)} %copy-done.16, f32[32,128]{1,0:T(8,128)} %pad_maximum_fusion.1.refs_1_, ...), custom_call_target="tpu_custom_call" | custom-call | tf_op jit(solution)/shard_map/closing/pallas_call | solution.py:1709
  284.2 0.8 slice.98
  284.9 0.7 slice.101
  285.7 0.7 slice.105
  286.5 2.6 convert_element_type.126
  289.1 0.9 convert_element_type.127
  290.0 1.7 convert_element_type.128
  291.7 1.6 convert_element_type.129
  293.2 0.6 fusion.33
  293.8 0.6 dynamic-slice_reduce_fusion
  294.4 0.6 constant_dynamic-slice_fusion.6
  295.0 0.7 copy.31
  295.7 0.7 copy.32
  (101 shorter events, 1.0 us)
Async XLA Ops:
  70.8 4.0 %slice-start = ((s8[4718592]{0:T(1024)(128)(4,1)}), s8[4194304]{0:T(1024)(128)(4,1)S(1)}, s32[]{:S(2)}) async-start(s8[4718592]{0:T(1024)(128)(4,1)} %bitcast.43), calls=%async_computation | async-start | bytes 8388608
  70.9 3.8 %copy-start.20 = (bf16[128,768]{1,0:T(8,128)(2,1)}, bf16[128,768]{1,0:T(8,128)(2,1)S(1)}, u32[]{:S(2)}) copy-start(bf16[128,768]{1,0:T(8,128)(2,1)S(1)} %add_convert_fusion.2.refs_16_) | copy-start | bytes 589828
  70.9 3.8 %slice-start.1 = ((s8[4718592]{0:T(1024)(128)(4,1)}), s8[524288]{0:T(1024)(128)(4,1)S(1)}, s32[]{:S(2)}) async-start(s8[4718592]{0:T(1024)(128)(4,1)} %bitcast.43), calls=%async_computation.1 | async-start | bytes 1048576
  74.7 0.9 copy-start.11
  74.8 2.3 copy-start.7
  76.1 1.7 copy-start.13
  77.1 0.8 copy-start.5
  77.1 1.0 copy-start.6
  77.1 27.3 %slice-start.2 = ((s8[4718592]{0:T(1024)(128)(4,1)}), s8[4194304]{0:T(1024)(128)(4,1)S(1)}, s32[]{:S(2)}) async-start(s8[4718592]{0:T(1024)(128)(4,1)} %bitcast.53), calls=%async_computation.2 | async-start | bytes 8388608
  77.8 24.2 %copy-start.8 = (bf16[4,192,768]{2,1,0:T(8,128)(2,1)S(1)}, bf16[4,192,768]{2,1,0:T(8,128)(2,1)}, u32[]{:S(2)}) copy-start(bf16[4,192,768]{2,1,0:T(8,128)(2,1)} %get-tuple-element.44) | copy-start | bytes 3538948
  101.9 7.9 %copy-start.1 = (bf16[128,768]{1,0:T(8,128)(2,1)}, bf16[128,768]{1,0:T(8,128)(2,1)S(1)}, u32[]{:S(2)}) copy-start(bf16[128,768]{1,0:T(8,128)(2,1)S(1)} %get-tuple-element.51.refs_11_) | copy-start | bytes 589828
  102.0 9.0 %copy-start.2 = (bf16[128,768]{1,0:T(8,128)(2,1)}, bf16[128,768]{1,0:T(8,128)(2,1)S(1)}, u32[]{:S(2)}) copy-start(bf16[128,768]{1,0:T(8,128)(2,1)S(1)} %get-tuple-element.50.refs_18_) | copy-start | bytes 589828
  102.0 2.4 slice-start.3
  104.4 2.0 copy-start.21
  106.4 0.9 copy-start.12
  106.4 1.6 copy-start.9
  107.3 187.7 %collective-permute-start = (bf16[128,768]{1,0:T(8,128)(2,1)S(1)}, bf16[128,768]{1,0:T(8,128)(2,1)S(1)}, u32[]{:S(2)}, u32[]{:S(2)}) collective-permute-start(bf16[128,768]{1,0:T(8,128)(2,1)S(1)} %fusion.19), channel_id=1, source_target_pairs={{0,0},{1,8},{2,16},{3,24},{4,4},{5,12},{6,20},{7,28},{8,1},{9,9},{... | collective-permute-start | bytes 589832 | tf_op jit(solution)/shard_map/ppermute | solution.py:1738
  110.1 41.4 %copy-start.15 = (bf16[128,768]{1,0:T(8,128)(2,1)}, bf16[128,768]{1,0:T(8,128)(2,1)S(1)}, u32[]{:S(2)}) copy-start(bf16[128,768]{1,0:T(8,128)(2,1)S(1)} %get-tuple-element.101.refs_19_) | copy-start | bytes 589828
  110.1 1.4 copy-start.4
  151.5 1.4 copy-start.3
  151.5 8.4 %copy-start = (bf16[128,2304]{1,0:T(8,128)(2,1)}, bf16[128,2304]{1,0:T(8,128)(2,1)S(1)}, u32[]{:S(2)}) copy-start(bf16[128,2304]{1,0:T(8,128)(2,1)S(1)} %get-tuple-element.56.refs_23_) | copy-start | bytes 1769476
  153.1 2.0 copy-start.22
  155.1 1.8 copy-start.10
  157.0 1.5 copy-start.14
  157.9 3.5 %copy-start.17 = (bf16[128,768]{1,0:T(8,128)(2,1)}, bf16[128,768]{1,0:T(8,128)(2,1)S(1)}, u32[]{:S(2)}) copy-start(bf16[128,768]{1,0:T(8,128)(2,1)S(1)} %get-tuple-element.95.refs_21_) | copy-start | bytes 589828
  157.9 3.6 %copy-start.25 = (f32[16,128]{1,0:T(8,128)S(1)}, f32[16,128]{1,0:T(8,128)}, u32[]{:S(2)}) copy-start(f32[16,128]{1,0:T(8,128)} %get-tuple-element.57) | copy-start | bytes 24580
  158.5 3.6 %copy-start.16 = (bf16[128,768]{1,0:T(8,128)(2,1)}, bf16[128,768]{1,0:T(8,128)(2,1)S(1)}, u32[]{:S(2)}) copy-start(bf16[128,768]{1,0:T(8,128)(2,1)S(1)} %convolution_convert_fusion.refs_0_) | copy-start | bytes 589828
  284.2 5.0 %copy-start.23 = (bf16[192,768]{1,0:T(8,128)(2,1)S(1)}, bf16[192,768]{1,0:T(8,128)(2,1)}, u32[]{:S(2)}) copy-start(bf16[192,768]{1,0:T(8,128)(2,1)} %get-tuple-element.67) | copy-start | bytes 884740
  286.5 3.5 %copy-start.19 = (bf16[192,3072]{1,0:T(8,128)(2,1)S(1)}, bf16[192,3072]{1,0:T(8,128)(2,1)}, u32[]{:S(2)}) copy-start(bf16[192,3072]{1,0:T(8,128)(2,1)} %get-tuple-element.68) | copy-start | bytes 3538948
  290.0 1.7 copy-start.18
  291.7 4.1 %copy-start.24 = (bf16[128,768]{1,0:T(8,128)(2,1)S(1)}, bf16[128,768]{1,0:T(8,128)(2,1)}, u32[]{:S(2)}) copy-start(bf16[128,768]{1,0:T(8,128)(2,1)} %get-tuple-element.64) | copy-start | bytes 589828
